TPU v7x, 32 devices: a whole 2x2x4 slice. The times are simulated.
32 devices in a mesh: groups: 2 (over x), head: 4 (over y, core), req: 4 (over z).
Axes of the slice: x: 2, y: 2, z: 4, core: 2. Of those that a mesh axis runs over, the one named last changes fastest.
Arguments:
- ssm_input: bfloat16 [16, 64, 4096], P(None, ('groups', 'req'), 'head'), parts along dimension 1, may hold values from -6 to 6
- write_vec: bfloat16 [16, 64, 128], P('head', ('groups', 'req')), parts along dimension 1, may hold values from -6 to 6
- read_vec: bfloat16 [16, 64, 128], P('head', ('groups', 'req')), parts along dimension 1, may hold values from -0.5 to 0.5
- step_raw: float32 [16, 64, 64], P(None, ('groups', 'req'), 'head'), parts along dimension 1, may hold values from -4 to 4
- step_bias: float32 [64], P('head'), may hold values from -3 to -0.5
- decay_rate: float32 [64], P('head'), may hold values from 1 to 16
- skip_gain: float32 [64], P('head'), may hold values from 0.5 to 1.5
- cache_state: bfloat16 [64, 64, 64, 128], P(('groups', 'req'), 'head'), parts along dimension 0, may hold values from -6 to 6
- parents: int32 [64, 16], P(('groups', 'req')), parts along dimension 0, may hold values from -1 to 14, as said below
- out_proj: bfloat16 [4096, 4096], P('head'), may hold values from -0.09375 to 0.09375
- residual: bfloat16 [16, 64, 4096], P('head', ('groups', 'req')), parts along dimension 1, may hold values from -6 to 6
- norm_gain: float32 [4096], replicated, may hold values from 0.1 to 1.9
- router: bfloat16 [4096, 64], replicated, may hold values from -0.09375 to 0.09375
- expert_ids: int32 [16, 64, 10], P('head', ('groups', 'req')), parts along dimension 1, may hold values from 0 to 63, as said below
- gate_proj: bfloat16 [128, 4096, 384], P(('head', 'req')), may hold values from -0.09375 to 0.09375
- up_proj: bfloat16 [128, 4096, 384], P(('head', 'req')), may hold values from -0.09375 to 0.09375
- down_proj: bfloat16 [128, 384, 4096], P(('head', 'req')), may hold values from -0.21875 to 0.21875
Outputs:
- layer_out: bfloat16 [16, 64, 4096], P('head', ('groups', 'req')), parts along dimension 1
There are 2 independent parts, one for each index of `groups`. A program takes and returns all parts, laid end to end along the dimension named above; an argument that names none is the same for every part. Nothing has to cross between parts.
Inputs may be any that keep to these rules, and one draw needn't show every extreme that they name: parents[r, 0] = -1 (the root); for j >= 1, parents[r, j] lies in 0 to j - 1; the last node's parent is node 14. `expert_ids`: each row names 10 different experts. Within the rows of one device (an aligned block of the 4 node index or indices and 8 requests held there) every expert is named by 4 or by 8 rows, 16 experts by 8; one expert is named by 8 rows in every such block.
All inputs are finite; a program needn't handle non-finite values.
Results may differ from a plain program's by a relative error of at most 0.0058.
Values may be sent and summed in bfloat16 or wider, within the bound.
No kernel may reach another device: no remote copies, remote signals or barrier semaphores. Data moves between devices by JAX's collectives and lax.ppermute only.
A program may use at most 192 MiB of HBM per device.

v0:
```python
import functools
import jax
import jax.numpy as jnp
from jax import lax
from jax.experimental import pallas as pl
from jax.experimental.pallas import tpu as pltpu
from jax.sharding import PartitionSpec as P


BF = jnp.bfloat16
F32 = jnp.float32
AXES = ("head", "req")
LANES = 128
MIX_CHUNKS = 2
AG_CHUNKS = 4
RS_CHUNKS = 4
DOWN_BLOCK = 512
BATCH = 16


def in_hbm(*arrays):
    return [pltpu.with_memory_space_constraint(a, pltpu.HBM) for a in arrays]


class Ring:
    def __init__(self, heads, reqs):
        self.heads, self.reqs = heads, reqs
        self.cores = 2 if heads % 2 == 0 else 1
        self.ys = heads // self.cores

    def pairs(self, dy, dc, dz):
        found = []
        for y in range(self.ys):
            for c in range(self.cores):
                for z in range(self.reqs):
                    there = ((y + dy) % self.ys) * self.cores + (c + dc) % self.cores
                    found.append(
                        (
                            (y * self.cores + c) * self.reqs + z,
                            there * self.reqs + (z + dz) % self.reqs,
                        )
                    )
        return found

    def shift(self, x, dy=0, dc=0, dz=0):
        return lax.ppermute(x, AXES, self.pairs(dy, dc, dz))

    def gather(self, x, axis):
        count = {"dc": self.cores, "dy": self.ys, "dz": self.reqs}[axis]
        moved = [self.shift(x, **{axis: s}) for s in range(1, count)]
        return jnp.stack([x] + moved)

    def scatter(self, parts, keep, axis):
        total = keep
        for s, part in enumerate(parts, 1):
            total = total + self.shift(part, **{axis: -s}).astype(F32)
        return total


def prep_body(heads, parents, step_raw, bias, decay, factor, grown):
    rows = parents.shape[0]
    reqs = step_raw.shape[1]
    lane = lax.broadcasted_iota(jnp.int32, (rows, rows), 1)
    row = lax.broadcasted_iota(jnp.int32, (rows, rows), 0)
    hop = parents[...]
    at = jnp.where(hop >= 0, hop * reqs + lax.broadcasted_iota(jnp.int32, hop.shape, 0) % reqs, -1)
    power = jnp.where(at == lane, 1.0, 0.0)
    reach = jnp.where(row == lane, 1.0, 0.0) + power
    power = power.astype(BF)
    span = 2
    while span * reqs < rows:
        power = jnp.dot(power, power, preferred_element_type=F32).astype(BF)
        reach = reach + jnp.dot(reach.astype(BF), power, preferred_element_type=F32)
        span *= 2
    raw = step_raw[...].reshape(rows, heads) + bias[...]
    step = jnp.maximum(raw, 0.0) + jnp.log1p(jnp.exp(-jnp.abs(raw)))
    rate = -step * decay[...]
    blank = jnp.zeros((rows, rows - heads), F32)
    wide_step = jnp.concatenate([step, blank], axis=1)
    wide_rate = jnp.concatenate([rate, blank], axis=1)
    depth = jnp.dot(
        reach, wide_rate, preferred_element_type=F32, precision=lax.Precision.HIGHEST
    )
    grown[...] = jnp.exp(depth[:, :heads])
    depth_t = depth.T
    step_t = wide_step.T
    linked = reach > 0
    for h in range(heads):
        spread = jnp.where(linked, depth[:, h : h + 1] - depth_t[h : h + 1, :], 0.0)
        factor[h] = jnp.where(linked, jnp.exp(spread) * step_t[h : h + 1, :], 0.0)


def prepare(parents, step_raw, step_bias, decay_rate):
    nodes, reqs, heads = step_raw.shape
    rows = nodes * reqs
    return pl.pallas_call(
        functools.partial(prep_body, heads),
        out_shape=(
            jax.ShapeDtypeStruct((heads, rows, rows), F32),
            jax.ShapeDtypeStruct((rows, heads), F32),
        ),
        compiler_params=pltpu.CompilerParams(vmem_limit_bytes=16 << 20),
        name="prepare",
    )(
        parents.T.reshape(rows, 1),
        *in_hbm(step_raw, step_bias.reshape(1, heads), decay_rate.reshape(1, heads)),
    )


def front_body(
    heads, near_rows, slot_of, goes_to, early, x, state, factor, grown, skip, weight,
    near, far, mixed_rows, read_rows, write_rows, cache, result,
):
    blocks, tokens = early.shape[0], early.shape[1]
    nodes, reqs, columns = x.shape
    rows = nodes * reqs
    size = columns // heads
    states = state.shape[2]

    @pl.when(pl.program_id(0) == 0)
    def _():
        for a in range(blocks):
            block = early[slot_of[a]].astype(F32)
            write_rows[a * tokens : (a + 1) * tokens] = block[:, :states]
            read_rows[a * tokens : (a + 1) * tokens] = block[:, states : 2 * states]
        writes = write_rows[...].astype(BF)
        reads = read_rows[...].astype(BF)
        affinity = lax.dot_general(
            reads, writes, (((1,), (1,)), ((), ())), preferred_element_type=F32
        )
        for r in range(reqs):
            mine = read_rows[pl.ds(r, nodes, stride=reqs), :].astype(BF)
            got = lax.dot_general(
                mine, state[r], (((1,), (1,)), ((), ())), preferred_element_type=F32
            )
            for i in range(columns // LANES):
                cache.at[i][pl.ds(r, nodes, stride=reqs), :] = got[:, i * LANES : (i + 1) * LANES]
        values = x[...].reshape(rows, columns)
        pair = 2 * size
        left = lax.broadcasted_iota(jnp.int32, (rows, pair), 1) < size
        for h in range(0, heads, 2):
            cut = slice(h * size, h * size + pair)
            own = values[:, cut]
            first = (factor[h] * affinity).astype(BF)
            second = (factor[h + 1] * affinity).astype(BF)
            zero = jnp.zeros_like(own)
            both = jnp.dot(
                jnp.concatenate([first, second], axis=1),
                jnp.concatenate([jnp.where(left, own, zero), jnp.where(left, zero, own)], axis=0),
                preferred_element_type=F32,
            )
            grow = jnp.where(left, grown[:, h : h + 1], grown[:, h + 1 : h + 2])
            gain = jnp.where(left, skip[:, h : h + 1], skip[:, h + 1 : h + 2])
            both = both + cache[h * size // LANES] * grow + gain * own.astype(F32)
            result[:, cut] = both.astype(BF).astype(F32)
        for s in range(blocks):
            start = pl.multiple_of(goes_to[s] * tokens, tokens)
            mixed_rows[s * tokens : (s + 1) * tokens] = result[pl.ds(start, tokens)].astype(BF)

    total = jnp.dot(mixed_rows[...], weight[...], preferred_element_type=F32)
    near[...] = total[:near_rows]
    far[...] = total[near_rows:].astype(BF)


def front(early, x, state, factor, grown, skip_gain, out_proj, slot_of, goes_to, near_rows, part, parts):
    nodes, reqs, columns = x.shape
    heads = skip_gain.shape[0]
    rows = nodes * reqs
    states = state.shape[3]
    span = out_proj.shape[1] // parts
    block = min(span, 512)
    steps = span // block
    whole = lambda a: pl.BlockSpec(a.shape, lambda j, *_: (0,) * len(a.shape))
    state = state.reshape(state.shape[0], columns, states)
    skip = skip_gain.reshape(1, heads)
    x, state, skip, out_proj = in_hbm(x, state, skip, out_proj)
    return pl.pallas_call(
        functools.partial(front_body, heads, near_rows),
        grid_spec=pltpu.PrefetchScalarGridSpec(
            num_scalar_prefetch=2,
            grid=(steps,),
            in_specs=[
                whole(early), whole(x), whole(state), whole(factor), whole(grown), whole(skip),
                pl.BlockSpec((columns, block), lambda j, *_: (0, part * steps + j)),
            ],
            out_specs=(
                pl.BlockSpec((near_rows, block), lambda j, *_: (0, j)),
                pl.BlockSpec((rows - near_rows, block), lambda j, *_: (0, j)),
                pl.BlockSpec((rows, columns), lambda j, *_: (0, 0)),
            ),
            scratch_shapes=[
                pltpu.VMEM((rows, states), F32),
                pltpu.VMEM((rows, states), F32),
                pltpu.VMEM((columns // LANES, rows, LANES), F32),
                pltpu.VMEM((rows, columns), F32),
            ],
        ),
        out_shape=(
            jax.ShapeDtypeStruct((near_rows, span), F32),
            jax.ShapeDtypeStruct((rows - near_rows, span), BF),
            jax.ShapeDtypeStruct((rows, columns), BF),
        ),
        compiler_params=pltpu.CompilerParams(vmem_limit_bytes=32 << 20),
        cost_estimate=pl.CostEstimate(
            flops=2 * rows * columns * span, transcendentals=0, bytes_accessed=2 * columns * span
        ),
        name="front",
    )(slot_of, goes_to, early, x, state, factor, grown, skip, out_proj)


def project_body(near_rows, rows, weight, near, far):
    total = jnp.dot(rows[...], weight[...], preferred_element_type=F32)
    near[...] = total[:near_rows]
    far[...] = total[near_rows:].astype(BF)


def project(rows, out_proj, near_rows, part, parts):
    count, columns = rows.shape
    span = out_proj.shape[1] // parts
    block = min(span, 512)
    steps = span // block
    return pl.pallas_call(
        functools.partial(project_body, near_rows),
        grid=(steps,),
        in_specs=[
            pl.BlockSpec((count, columns), lambda j: (0, 0)),
            pl.BlockSpec((columns, block), lambda j: (0, part * steps + j)),
        ],
        out_specs=(
            pl.BlockSpec((near_rows, block), lambda j: (0, j)),
            pl.BlockSpec((count - near_rows, block), lambda j: (0, j)),
        ),
        out_shape=(
            jax.ShapeDtypeStruct((near_rows, span), F32),
            jax.ShapeDtypeStruct((count - near_rows, span), BF),
        ),
        compiler_params=pltpu.CompilerParams(vmem_limit_bytes=16 << 20),
        cost_estimate=pl.CostEstimate(
            flops=2 * count * columns * span, transcendentals=0, bytes_accessed=2 * columns * span
        ),
        name="project",
    )(rows, *in_hbm(out_proj))


def up_body(first, last, token_at, x, wg, wu, *rest):
    rest = list(rest)
    if not first:
        gin, uin = rest.pop(0), rest.pop(0)
    if last:
        extra, spot, share = rest.pop(0), rest.pop(0), rest.pop(0)
    if last:
        act_out, comb_out, spread, picked, scales = rest
    else:
        gout, uout, spread, picked = rest
    q = pl.program_id(0)
    tokens, width = x.shape
    tall = width // LANES
    slots = picked.shape[0] // tall

    @pl.when(q == 0)
    def _():
        for i in range(tall):
            spread[pl.ds(i, tokens, stride=tall), :] = x[:, i * LANES : (i + 1) * LANES].astype(F32)

    for c in range(0, slots, BATCH):
        at = [token_at[q * slots + c + i] for i in range(BATCH)]
        got = [spread[pl.ds(pl.multiple_of(t * tall, tall), tall)] for t in at]
        picked[c * tall : (c + BATCH) * tall] = jnp.concatenate(got, axis=0)
        if last:
            got = [extra[pl.ds(t, 1)] for t in at]
            for i in range(BATCH):
                scales[c + i : c + i + 1] = got[i]
    rows = jnp.concatenate(
        [picked[pl.ds(i, slots, stride=tall), :].astype(BF) for i in range(tall)], axis=1
    )
    gated = jnp.dot(rows, wg[0], preferred_element_type=F32)
    lifted = jnp.dot(rows, wu[0], preferred_element_type=F32)
    if not first:
        gated = gated + gin[0]
        lifted = lifted + uin[0]
    if not last:
        gout[0] = gated
        uout[0] = lifted
        return
    scale = scales[:, 0:1] + scales[:, 1:2] + scales[:, 2:3]
    gated = gated * scale
    lifted = lifted * scale
    act_out[0] = (gated / (1.0 + jnp.exp(-gated)) * lifted).astype(BF)
    lane = lax.broadcasted_iota(jnp.int32, (tokens, slots), 1)
    column = lax.broadcasted_iota(jnp.int32, spot.shape, 1)
    own_spot = jnp.sum(jnp.where(column == q, spot[...], 0), axis=1, keepdims=True)
    own_share = jnp.sum(jnp.where(column == q, share[...], 0.0), axis=1, keepdims=True)
    comb_out[...] = jnp.where(lane == own_spot, own_share, 0.0).astype(BF)


def expert_up(k, chunks, token_at, x, gate_proj, up_proj, sums, extras):
    held = gate_proj.shape[0]
    tokens, width = x.shape
    slots = token_at.shape[0] // held
    units = gate_proj.shape[2]
    first, last = k == 0, k == chunks - 1
    per_expert = lambda *tail: pl.BlockSpec((1,) + tail, lambda q, *_: (q, 0, 0))
    whole = lambda a: pl.BlockSpec(a.shape, lambda q, *_: (0, 0))
    weight = pl.BlockSpec((1, width, units), lambda q, *_: (q, k, 0))
    in_specs = [whole(x), weight, weight]
    args = [x, *in_hbm(gate_proj, up_proj)]
    scratch = [
        pltpu.VMEM((tokens * width // LANES, LANES), F32),
        pltpu.VMEM((slots * width // LANES, LANES), F32),
    ]
    if not first:
        in_specs += [per_expert(slots, units)] * 2
        args += list(sums)
    if last:
        in_specs += [whole(a) for a in extras]
        args += list(extras)
        out_shape = (
            jax.ShapeDtypeStruct((held, slots, units), BF),
            jax.ShapeDtypeStruct((tokens, held * slots), BF),
        )
        out_specs = (per_expert(slots, units), pl.BlockSpec((tokens, slots), lambda q, *_: (0, q)))
        scratch.append(pltpu.VMEM((slots, extras[0].shape[1]), F32))
    else:
        out_shape = (jax.ShapeDtypeStruct((held, slots, units), F32),) * 2
        out_specs = (per_expert(slots, units),) * 2
    return pl.pallas_call(
        functools.partial(up_body, first, last),
        grid_spec=pltpu.PrefetchScalarGridSpec(
            num_scalar_prefetch=1,
            grid=(held,),
            in_specs=in_specs,
            out_specs=out_specs,
            scratch_shapes=scratch,
        ),
        out_shape=out_shape,
        compiler_params=pltpu.CompilerParams(vmem_limit_bytes=40 << 20),
        cost_estimate=pl.CostEstimate(
            flops=4 * held * slots * width * units,
            transcendentals=0,
            bytes_accessed=4 * held * width * units,
        ),
    )(token_at, *args)


def down_body(act, comb, wd, keep, send, halves):
    held, slots, _ = act.shape
    for q in range(held):
        halves[q * slots : (q + 1) * slots] = jnp.dot(
            act[q], wd[q], preferred_element_type=F32
        ).astype(BF)
    kept = keep.shape[0]
    total = jnp.dot(comb[...], halves[...], preferred_element_type=F32)
    keep[...] = total[:kept]
    send[...] = total[kept:].astype(BF)


def expert_down(k, chunks, act, comb, down_proj, kept):
    held, slots, units = act.shape
    tokens = comb.shape[0]
    width = down_proj.shape[2] // chunks
    block = min(width, DOWN_BLOCK)
    steps = width // block
    return pl.pallas_call(
        down_body,
        grid=(steps,),
        in_specs=[
            pl.BlockSpec(act.shape, lambda j: (0, 0, 0)),
            pl.BlockSpec(comb.shape, lambda j: (0, 0)),
            pl.BlockSpec((held, units, block), lambda j: (0, 0, k * steps + j)),
        ],
        out_specs=(
            pl.BlockSpec((kept, block), lambda j: (0, j)),
            pl.BlockSpec((tokens - kept, block), lambda j: (0, j)),
        ),
        out_shape=(
            jax.ShapeDtypeStruct((kept, width), F32),
            jax.ShapeDtypeStruct((tokens - kept, width), BF),
        ),
        scratch_shapes=[pltpu.VMEM((held * slots, block), BF)],
        compiler_params=pltpu.CompilerParams(vmem_limit_bytes=40 << 20),
        cost_estimate=pl.CostEstimate(
            flops=2 * held * slots * width * (tokens + units),
            transcendentals=0,
            bytes_accessed=2 * held * width * units,
        ),
    )(act, comb, *in_hbm(down_proj))


def layer(
    ssm_input,
    write_vec,
    read_vec,
    step_raw,
    step_bias,
    decay_rate,
    skip_gain,
    cache_state,
    parents,
    out_proj,
    residual,
    norm_gain,
    router,
    expert_ids,
    gate_proj,
    up_proj,
    down_proj,
):
    _, requests, _ = ssm_input.shape
    local_nodes, _, width = residual.shape
    tokens = local_nodes * requests
    topk = expert_ids.shape[2]
    experts = router.shape[1]
    held = gate_proj.shape[0]
    ring = Ring(lax.axis_size("head"), lax.axis_size("req"))
    cores, ys, reqs = ring.cores, ring.ys, ring.reqs
    head_at = lax.axis_index("head")
    y_at, c_at = head_at // cores, head_at % cores
    device = head_at * reqs + lax.axis_index("req")
    e0 = (device * held) % experts

    choices = expert_ids.reshape(tokens, topk)
    labels = jnp.arange(experts, dtype=jnp.int32)
    match = choices[:, :, None] == labels[None, None, :]
    named = jnp.any(match, axis=1).astype(BF)

    states = write_vec.shape[2]
    early = jnp.concatenate(
        [write_vec.reshape(tokens, states), read_vec.reshape(tokens, states)], axis=1
    )
    early = ring.gather(ring.gather(early, "dc"), "dy")
    early = early.reshape(ys * cores, tokens, -1)
    absolute = jnp.arange(ys * cores, dtype=jnp.int32)
    slot_of = ((y_at - absolute // cores) % ys) * cores + (c_at - absolute % cores) % cores
    slots = jnp.arange(cores * ys, dtype=jnp.int32)
    goes_to = ((y_at - slots % ys) % ys) * cores + (c_at - slots // ys) % cores
    factor, grown = prepare(parents, step_raw, step_bias, decay_rate)
    near_rows = ys * tokens

    all_tokens = cores * ys * reqs * tokens
    capacity = 2 * tokens * topk // (experts + experts // 4)
    room = capacity * cores * ys * reqs

    rows_left = residual.reshape(tokens, width)
    mixes = []
    part_span = width // MIX_CHUNKS
    for m in range(MIX_CHUNKS):
        cut = slice(m * part_span, (m + 1) * part_span)
        if m == 0:
            mixed, away, mixed_rows = front(
                early, ssm_input, cache_state, factor, grown, skip_gain, out_proj,
                slot_of, goes_to, near_rows, m, MIX_CHUNKS,
            )
        else:
            mixed, away = project(mixed_rows, out_proj, near_rows, m, MIX_CHUNKS)
        if cores > 1:
            mixed = ring.scatter([away], mixed, "dc")
        mixed = mixed.reshape(ys, tokens, part_span)
        mixed = ring.scatter([mixed[s].astype(BF) for s in range(1, ys)], mixed[0], "dy")
        mixes.append((rows_left[:, cut].astype(F32) + mixed).astype(BF))
    span = width // AG_CHUNKS
    after_mixer = jnp.concatenate(mixes, axis=1)
    sums = None
    for k in range(AG_CHUNKS):
        cut = slice(k * span, (k + 1) * span)
        m = k * MIX_CHUNKS // AG_CHUNKS
        local = slice(k * span - m * part_span, (k + 1) * span - m * part_span)
        payload = (mixes[m][:, local].astype(F32) * norm_gain[cut]).astype(BF)
        extras = None
        if k == AG_CHUNKS - 1:
            widened = after_mixer.astype(F32)
            scale = lax.rsqrt(jnp.mean(widened * widened, axis=-1, keepdims=True) + 1e-05)
            normed = (widened * scale * norm_gain).astype(BF)
            logits = jnp.dot(normed, router, preferred_element_type=F32)
            picked_logits = jnp.sum(jnp.where(match, logits[:, None, :], 0.0), axis=2)
            powered = jnp.exp(picked_logits)
            gate = (powered / jnp.sum(powered, axis=1, keepdims=True)).astype(BF)
            dense = jnp.sum(jnp.where(match, gate.astype(F32)[:, :, None], 0.0), axis=1)
            top = scale.astype(BF)
            middle = (scale - top.astype(F32)).astype(BF)
            low = (scale - top.astype(F32) - middle.astype(F32)).astype(BF)
            extra = jnp.concatenate([top, middle, low, dense.astype(BF)], axis=1)
            tail = -(-extra.shape[1] // LANES) * LANES
            extra = jnp.pad(extra, ((0, 0), (0, tail - extra.shape[1])))
            payload = jnp.concatenate([payload, extra], axis=1)
        if k == 0:
            tail = -(-experts // LANES) * LANES
            extra = jnp.pad(named, ((0, 0), (0, tail - experts)))
            payload = jnp.concatenate([payload, extra], axis=1)
        rows = ring.gather(payload, "dz")
        rows = ring.gather(rows, "dy")
        rows = ring.gather(rows, "dc")
        rows = rows.reshape(all_tokens, -1)
        if k == 0:
            named_all = rows[:, span : span + experts]
            mine = lax.dynamic_slice_in_dim(named_all, e0, held, axis=1)
            order = jnp.arange(all_tokens, dtype=jnp.int32)
            before = (order[:, None] > order[None, :]).astype(BF)
            rank = jnp.dot(before, mine, preferred_element_type=F32)
            place = jnp.where(mine > 0, rank, -1.0).astype(jnp.int32)
            spots = jnp.arange(room, dtype=jnp.int32)
            chosen = place.T[:, None, :] == spots[None, :, None]
            token_at = jnp.sum(jnp.where(chosen, order, 0), axis=2).reshape(-1)
        if k == AG_CHUNKS - 1:
            extra = rows[:, -tail:].astype(F32)
            share = lax.dynamic_slice_in_dim(extra, e0 + 3, held, axis=1)
            extras = (extra, place, share)
        rows = rows[:, :span]
        sums = expert_up(k, AG_CHUNKS, token_at, rows, gate_proj, up_proj, sums, extras)
    act, comb = sums

    pieces = []
    span = width // RS_CHUNKS
    for k in range(RS_CHUNKS):
        keep, send = expert_down(k, RS_CHUNKS, act, comb, down_proj, ys * reqs * tokens)
        total = ring.scatter([send], keep, "dc") if cores > 1 else keep
        total = total.reshape(ys, reqs * tokens, span)
        total = ring.scatter([total[s].astype(BF) for s in range(1, ys)], total[0], "dy")
        total = total.reshape(reqs, tokens, span)
        total = ring.scatter([total[s].astype(BF) for s in range(1, reqs)], total[0], "dz")
        cut = slice(k * span, (k + 1) * span)
        pieces.append((after_mixer[:, cut].astype(F32) + total).astype(BF))
    return jnp.concatenate(pieces, axis=1).reshape(local_nodes, requests, width)


def solution(mesh):
    in_specs = (
        P(None, ("groups", "req"), "head"),
        P("head", ("groups", "req"), None),
        P("head", ("groups", "req"), None),
        P(None, ("groups", "req"), "head"),
        P("head"),
        P("head"),
        P("head"),
        P(("groups", "req"), "head", None, None),
        P(("groups", "req"), None),
        P("head", None),
        P("head", ("groups", "req"), None),
        P(),
        P(),
        P("head", ("groups", "req"), None),
        P(("head", "req"), None, None),
        P(("head", "req"), None, None),
        P(("head", "req"), None, None),
    )
    out_specs = P("head", ("groups", "req"), None)
    return jax.shard_map(layer, mesh=mesh, in_specs=in_specs, out_specs=out_specs, check_vma=False)
```

profile of v0, /device:TPU:0, one launch (start us, length us, event | category | flops | bytes accessed | tf_op | source)
XLA Modules:
  0.0 191.1 jit_solution(13442760474982629480)
XLA Ops:
  2.1 2.8 %collective-permute-start.1 = (bf16[2,32,256]{2,1,0:T(8,128)(2,1)S(1)}, bf16[2,32,256]{2,1,0:T(8,128)(2,1)S(1)}, u32[]{:S(2)}, u32[]{:S(2)}) collective-permute-start(bf16[2,32,256]{2,1,0:T(8,128)(2,1)S(1)} %get-tuple-element.106), channel_id=1, source_target_pairs={{0,8},{1,9},{2,10},{3,11},{4,12},{5,13},{6,14},{7,15},{8,0},{9,1},... | collective-permute-start | bytes 98312 | tf_op jit(solution)/shard_map/ppermute | solution.py:46
  6.6 2.3 %prepare.1 = (f32[16,128,128]{2,1,0:T(8,128)S(1)}, f32[128,16]{1,0:T(8,128)S(1)}) custom-call(s32[128,1]{1,0:T(8,128)S(1)} %reshape.214.parents, f32[16,8,16]{2,1,0:T(8,128)} %step_raw.1, f32[1,16]{1,0:T(1,128)} %bitcast.109, f32[1,16]{1,0:T(1,128)} %bitcast.110), custom_call_target="tpu_custom_call" | custom-call | tf_op jit(solution)/shard_map/prepare/pallas_call | solution.py:96
  9.0 5.8 %front.1 = (f32[64,2048]{1,0:T(8,128)S(1)}, bf16[64,2048]{1,0:T(8,128)(2,1)S(1)}, bf16[128,1024]{1,0:T(8,128)(2,1)S(1)}) custom-call(s32[4]{0:T(128)S(1)} %get-tuple-element.113.slot_of, s32[4]{0:T(128)S(1)} %get-tuple-element.114.goes_to, bf16[4,32,256]{2,1,0:T(8,128)(2,1)S(1)} %bitcast.74, bf16[16,8,1024]{2,1,0:T(8,128)(2,1)} %x.5, ...), custom_call_target="tpu_custom_call" | custom-call | flops 536870912 | bytes 4194304 | tf_op jit(solution)/shard_map/front/pallas_call | solution.py:177
  14.9 3.6 %project.1 = (f32[64,2048]{1,0:T(8,128)S(1)}, bf16[64,2048]{1,0:T(8,128)(2,1)S(1)}) custom-call(bf16[128,1024]{1,0:T(8,128)(2,1)S(1)} %get-tuple-element.32.rows, bf16[1024,4096]{1,0:T(8,128)(2,1)} %weight.3), custom_call_target="tpu_custom_call" | custom-call | flops 536870912 | bytes 4194304 | tf_op jit(solution)/shard_map/project/pallas_call | solution.py:222
  21.5 4.1 %collective-permute-done.3 = bf16[32,2048]{1,0:T(8,128)(2,1)S(1)} collective-permute-done((bf16[32,2048]{1,0:T(8,128)(2,1)S(1)}, bf16[32,2048]{1,0:T(8,128)(2,1)S(1)}, u32[]{:S(2)}, u32[]{:S(2)}) %collective-permute-start.3) | collective-permute-done | bytes 131104 | tf_op jit(solution)/shard_map/ppermute | solution.py:46
  25.6 1.9 collective-permute-done.10
  27.6 1.6 collective-permute-start.4
  29.2 2.6 %collective-permute-start.5 = (bf16[32,1152]{1,0:T(8,128)(2,1)S(1)}, bf16[32,1152]{1,0:T(8,128)(2,1)S(1)}, u32[]{:S(2)}, u32[]{:S(2)}) collective-permute-start(bf16[32,1152]{1,0:T(8,128)(2,1)S(1)} %get-tuple-element.102), channel_id=1, source_target_pairs={{0,2},{1,3},{2,0},{3,1},{4,6},{5,7},{6,4},{7,5},{8,10},{9,11},{10,... | collective-permute-start | bytes 221192 | tf_op jit(solution)/shard_map/ppermute | solution.py:46
  32.0 1.7 collective-permute-start.22
  33.7 1.9 collective-permute-start.23
  37.0 1.4 collective-permute-done.21
  38.4 2.4 %collective-permute-start.16 = (bf16[32,1024]{1,0:T(8,128)(2,1)S(1)}, bf16[32,1024]{1,0:T(8,128)(2,1)S(1)}, u32[]{:S(2)}, u32[]{:S(2)}) collective-permute-start(bf16[32,1024]{1,0:T(8,128)(2,1)S(1)} %get-tuple-element.97), channel_id=1, source_target_pairs={{0,1},{1,2},{2,3},{3,0},{4,5},{5,6},{6,7},{7,4},{8,9},{9,10},{10,1... | collective-permute-start | bytes 196616 | tf_op jit(solution)/shard_map/ppermute | solution.py:46
  42.7 2.9 %collective-permute-start.18 = (bf16[32,1024]{1,0:T(8,128)(2,1)S(1)}, bf16[32,1024]{1,0:T(8,128)(2,1)S(1)}, u32[]{:S(2)}, u32[]{:S(2)}) collective-permute-start(bf16[32,1024]{1,0:T(8,128)(2,1)S(1)} %get-tuple-element.97), channel_id=1, source_target_pairs={{0,3},{1,0},{2,1},{3,2},{4,7},{5,4},{6,5},{7,6},{8,11},{9,8},{10,9... | collective-permute-start | bytes 196616 | tf_op jit(solution)/shard_map/ppermute | solution.py:46
  45.7 1.6 collective-permute-start.6
  47.3 2.5 %collective-permute-start.11 = (bf16[32,1152]{1,0:T(8,128)(2,1)S(1)}, bf16[32,1152]{1,0:T(8,128)(2,1)S(1)}, u32[]{:S(2)}, u32[]{:S(2)}) collective-permute-start(bf16[32,1152]{1,0:T(8,128)(2,1)S(1)} %get-tuple-element.100), channel_id=1, source_target_pairs={{0,1},{1,2},{2,3},{3,0},{4,5},{5,6},{6,7},{7,4},{8,9},{9,10},{10,1... | collective-permute-start | bytes 221192 | tf_op jit(solution)/shard_map/ppermute | solution.py:46
  49.9 3.4 %collective-permute-start.12 = (bf16[32,1152]{1,0:T(8,128)(2,1)S(1)}, bf16[32,1152]{1,0:T(8,128)(2,1)S(1)}, u32[]{:S(2)}, u32[]{:S(2)}) collective-permute-start(bf16[32,1152]{1,0:T(8,128)(2,1)S(1)} %get-tuple-element.100), channel_id=1, source_target_pairs={{0,2},{1,3},{2,0},{3,1},{4,6},{5,7},{6,4},{7,5},{8,10},{9,11},{10,... | collective-permute-start | bytes 221192 | tf_op jit(solution)/shard_map/ppermute | solution.py:46
  54.2 1.5 collective-permute-start.19
  56.6 1.3 collective-permute-done.13
  58.6 4.3 %collective-permute-done.24 = bf16[4,32,1024]{2,1,0:T(8,128)(2,1)S(1)} collective-permute-done((bf16[4,32,1024]{2,1,0:T(8,128)(2,1)S(1)}, bf16[4,32,1024]{2,1,0:T(8,128)(2,1)S(1)}, u32[]{:S(2)}, u32[]{:S(2)}) %collective-permute-start.24) | collective-permute-done | bytes 262176 | tf_op jit(solution)/shard_map/ppermute | solution.py:46
  63.0 5.5 %collective-permute-done.19 = bf16[4,32,1024]{2,1,0:T(8,128)(2,1)S(1)} collective-permute-done((bf16[4,32,1024]{2,1,0:T(8,128)(2,1)S(1)}, bf16[4,32,1024]{2,1,0:T(8,128)(2,1)S(1)}, u32[]{:S(2)}, u32[]{:S(2)}) %collective-permute-start.19) | collective-permute-done | bytes 262176 | tf_op jit(solution)/shard_map/ppermute | solution.py:46
  69.5 2.2 %collective-permute-done.7 = bf16[4,32,1152]{2,1,0:T(8,128)(2,1)S(1)} collective-permute-done((bf16[4,32,1152]{2,1,0:T(8,128)(2,1)S(1)}, bf16[4,32,1152]{2,1,0:T(8,128)(2,1)S(1)}, u32[]{:S(2)}, u32[]{:S(2)}) %collective-permute-start.7) | collective-permute-done | bytes 294944 | tf_op jit(solution)/shard_map/ppermute | solution.py:46
  72.6 2.2 %collective-permute-done.14 = bf16[4,32,1152]{2,1,0:T(8,128)(2,1)S(1)} collective-permute-done((bf16[4,32,1152]{2,1,0:T(8,128)(2,1)S(1)}, bf16[4,32,1152]{2,1,0:T(8,128)(2,1)S(1)}, u32[]{:S(2)}, u32[]{:S(2)}) %collective-permute-start.14) | collective-permute-done | bytes 294944 | tf_op jit(solution)/shard_map/ppermute | solution.py:46
  75.8 1.1 pad_maximum_fusion.3
  76.9 1.3 pad_maximum_fusion.2
  78.2 1.2 pad_maximum_fusion
  80.6 1.2 pad_maximum_fusion.1
  84.5 1.2 copy-done.2
  85.7 9.9 %shard_map.163 = (f32[8,128,384]{2,1,0:T(8,128)S(1)}, f32[8,128,384]{2,1,0:T(8,128)S(1)}) custom-call(s32[1024]{0:T(1024)S(1)} %bitcast.75, bf16[512,1024]{1,0:T(8,128)(2,1)S(1)} %copy-done.2, bf16[8,4096,384]{2,1,0:T(8,128)(2,1)} %wg.7, bf16[8,4096,384]{2,1,0:T(8,128)(2,1)} %wu.7), custom_call_target="tpu_custom_call" | custom-call | flops 1610612736 | bytes 12582912 | tf_op jit(solution)/shard_map/pallas_call | solution.py:326
  95.6 9.9 %shard_map.164 = (f32[8,128,384]{2,1,0:T(8,128)S(1)}, f32[8,128,384]{2,1,0:T(8,128)S(1)}) custom-call(s32[1024]{0:T(1024)S(1)} %bitcast.76, bf16[512,1024]{1,0:T(8,128)(2,1)S(1)} %bitcast.71, bf16[8,4096,384]{2,1,0:T(8,128)(2,1)} %wg.7, bf16[8,4096,384]{2,1,0:T(8,128)(2,1)} %wu.7, f32[8,128,384]{2,1,0:T(8,128)S(1)} %get-tuple-element.35.rest_0_, ...), custom_call_target="tpu_custom_call" | custom-call | flops 1610612736 | bytes 12582912 | tf_op jit(solution)/shard_map/pallas_call | solution.py:326
  105.6 9.9 %shard_map.165 = (f32[8,128,384]{2,1,0:T(8,128)S(1)}, f32[8,128,384]{2,1,0:T(8,128)S(1)}) custom-call(s32[1024]{0:T(1024)S(1)} %bitcast.77, bf16[512,1024]{1,0:T(8,128)(2,1)S(1)} %bitcast.72, bf16[8,4096,384]{2,1,0:T(8,128)(2,1)} %wg.7, bf16[8,4096,384]{2,1,0:T(8,128)(2,1)} %wu.7, f32[8,128,384]{2,1,0:T(8,128)S(1)} %get-tuple-element.37.rest_0_, ...), custom_call_target="tpu_custom_call" | custom-call | flops 1610612736 | bytes 12582912 | tf_op jit(solution)/shard_map/pallas_call | solution.py:326
  115.6 10.8 %shard_map.166 = (bf16[8,128,384]{2,1,0:T(8,128)(2,1)S(1)}, bf16[512,1024]{1,0:T(8,128)(2,1)S(1)}) custom-call(s32[1024]{0:T(1024)S(1)} %bitcast.78, bf16[512,1024]{1,0:T(8,128)(2,1)S(1)} %slice.227.x, bf16[8,4096,384]{2,1,0:T(8,128)(2,1)} %wg.7, bf16[8,4096,384]{2,1,0:T(8,128)(2,1)} %wu.7, f32[8,128,384]{2,1,0:T(8,128)S(1)} %get-tuple-element.39.rest_0_, ...), custom_call_target="tpu_custom_call" | custom-call | flops 1610612736 | bytes 12582912 | tf_op jit(solution)/shard_map/pallas_call | solution.py:326
  126.4 4.6 %shard_map.168 = (f32[256,1024]{1,0:T(8,128)S(1)}, bf16[256,1024]{1,0:T(8,128)(2,1)S(1)}) custom-call(bf16[8,128,384]{2,1,0:T(8,128)(2,1)S(1)} %get-tuple-element.41.act, bf16[512,1024]{1,0:T(8,128)(2,1)S(1)} %get-tuple-element.42.comb, bf16[8,384,4096]{2,1,0:T(8,128)(2,1)} %wd.7), custom_call_target="tpu_custom_call" | custom-call | flops 1879048192 | bytes 6291456 | tf_op jit(solution)/shard_map/pallas_call | solution.py:363
  131.5 4.5 %shard_map.167 = (f32[256,1024]{1,0:T(8,128)S(1)}, bf16[256,1024]{1,0:T(8,128)(2,1)S(1)}) custom-call(bf16[8,128,384]{2,1,0:T(8,128)(2,1)S(1)} %get-tuple-element.41.act, bf16[512,1024]{1,0:T(8,128)(2,1)S(1)} %get-tuple-element.42.comb, bf16[8,384,4096]{2,1,0:T(8,128)(2,1)} %wd.7), custom_call_target="tpu_custom_call" | custom-call | flops 1879048192 | bytes 6291456 | tf_op jit(solution)/shard_map/pallas_call | solution.py:363
  136.2 4.6 %shard_map.170 = (f32[256,1024]{1,0:T(8,128)S(1)}, bf16[256,1024]{1,0:T(8,128)(2,1)S(1)}) custom-call(bf16[8,128,384]{2,1,0:T(8,128)(2,1)S(1)} %get-tuple-element.41.act, bf16[512,1024]{1,0:T(8,128)(2,1)S(1)} %get-tuple-element.42.comb, bf16[8,384,4096]{2,1,0:T(8,128)(2,1)} %wd.7), custom_call_target="tpu_custom_call" | custom-call | flops 1879048192 | bytes 6291456 | tf_op jit(solution)/shard_map/pallas_call | solution.py:363
  141.3 4.5 %shard_map.169 = (f32[256,1024]{1,0:T(8,128)S(1)}, bf16[256,1024]{1,0:T(8,128)(2,1)S(1)}) custom-call(bf16[8,128,384]{2,1,0:T(8,128)(2,1)S(1)} %get-tuple-element.41.act, bf16[512,1024]{1,0:T(8,128)(2,1)S(1)} %get-tuple-element.42.comb, bf16[8,384,4096]{2,1,0:T(8,128)(2,1)} %wd.7), custom_call_target="tpu_custom_call" | custom-call | flops 1879048192 | bytes 6291456 | tf_op jit(solution)/shard_map/pallas_call | solution.py:363
  146.9 1.6 collective-permute-start.27
  149.6 1.6 collective-permute-start.37
  151.1 4.3 %collective-permute-done.32 = bf16[128,1024]{1,0:T(8,128)(2,1)S(1)} collective-permute-done((bf16[128,1024]{1,0:T(8,128)(2,1)S(1)}, bf16[128,1024]{1,0:T(8,128)(2,1)S(1)}, u32[]{:S(2)}, u32[]{:S(2)}) %collective-permute-start.32) | collective-permute-done | bytes 262176 | tf_op jit(solution)/shard_map/ppermute | solution.py:46
  156.4 1.2 collective-permute-start.34
  157.6 3.4 %collective-permute-done.27 = bf16[128,1024]{1,0:T(8,128)(2,1)S(1)} collective-permute-done((bf16[128,1024]{1,0:T(8,128)(2,1)S(1)}, bf16[128,1024]{1,0:T(8,128)(2,1)S(1)}, u32[]{:S(2)}, u32[]{:S(2)}) %collective-permute-start.27) | collective-permute-done | bytes 262176 | tf_op jit(solution)/shard_map/ppermute | solution.py:46
  161.7 4.9 %collective-permute-done.42 = bf16[128,1024]{1,0:T(8,128)(2,1)S(1)} collective-permute-done((bf16[128,1024]{1,0:T(8,128)(2,1)S(1)}, bf16[128,1024]{1,0:T(8,128)(2,1)S(1)}, u32[]{:S(2)}, u32[]{:S(2)}) %collective-permute-start.42) | collective-permute-done | bytes 262176 | tf_op jit(solution)/shard_map/ppermute | solution.py:46
  167.6 4.2 %collective-permute-done.37 = bf16[128,1024]{1,0:T(8,128)(2,1)S(1)} collective-permute-done((bf16[128,1024]{1,0:T(8,128)(2,1)S(1)}, bf16[128,1024]{1,0:T(8,128)(2,1)S(1)}, u32[]{:S(2)}, u32[]{:S(2)}) %collective-permute-start.37) | collective-permute-done | bytes 262176 | tf_op jit(solution)/shard_map/ppermute | solution.py:46
  171.8 1.7 collective-permute-start.29
  173.7 3.8 %collective-permute-start.43 = (bf16[32,1024]{1,0:T(8,128)(2,1)S(1)}, bf16[32,1024]{1,0:T(8,128)(2,1)S(1)}, u32[]{:S(2)}, u32[]{:S(2)}) collective-permute-start(bf16[32,1024]{1,0:T(8,128)(2,1)S(1)} %get-tuple-element.82), channel_id=1, source_target_pairs={{0,3},{1,0},{2,1},{3,2},{4,7},{5,4},{6,5},{7,6},{8,11},{9,8},{10,9... | collective-permute-start | bytes 196616 | tf_op jit(solution)/shard_map/ppermute | solution.py:46
  178.1 2.2 %collective-permute-done.29 = bf16[32,1024]{1,0:T(8,128)(2,1)S(1)} collective-permute-done((bf16[32,1024]{1,0:T(8,128)(2,1)S(1)}, bf16[32,1024]{1,0:T(8,128)(2,1)S(1)}, u32[]{:S(2)}, u32[]{:S(2)}) %collective-permute-start.29) | collective-permute-done | bytes 65568 | tf_op jit(solution)/shard_map/ppermute | solution.py:46
  182.5 1.3 collective-permute-start.40
  183.9 3.5 %collective-permute-done.44 = bf16[32,1024]{1,0:T(8,128)(2,1)S(1)} collective-permute-done((bf16[32,1024]{1,0:T(8,128)(2,1)S(1)}, bf16[32,1024]{1,0:T(8,128)(2,1)S(1)}, u32[]{:S(2)}, u32[]{:S(2)}) %collective-permute-start.44) | collective-permute-done | bytes 65568 | tf_op jit(solution)/shard_map/ppermute | solution.py:46
  187.4 2.9 %collective-permute-done.39 = bf16[32,1024]{1,0:T(8,128)(2,1)S(1)} collective-permute-done((bf16[32,1024]{1,0:T(8,128)(2,1)S(1)}, bf16[32,1024]{1,0:T(8,128)(2,1)S(1)}, u32[]{:S(2)}, u32[]{:S(2)}) %collective-permute-start.39) | collective-permute-done | bytes 65568 | tf_op jit(solution)/shard_map/ppermute | solution.py:46
  (142 shorter events, 29.6 us)
Async XLA Ops:
  0.0 36.0 %copy-start = (bf16[4096,64]{0,1:T(8,128)(2,1)S(1)}, bf16[4096,64]{0,1:T(8,128)(2,1)}, u32[]{:S(2)}) copy-start(bf16[4096,64]{0,1:T(8,128)(2,1)} %param.29) | copy-start | bytes 1572868
  0.8 1.3 collective-permute-start
  2.1 6.8 %collective-permute-start.1 = (bf16[2,32,256]{2,1,0:T(8,128)(2,1)S(1)}, bf16[2,32,256]{2,1,0:T(8,128)(2,1)S(1)}, u32[]{:S(2)}, u32[]{:S(2)}) collective-permute-start(bf16[2,32,256]{2,1,0:T(8,128)(2,1)S(1)} %get-tuple-element.106), channel_id=1, source_target_pairs={{0,8},{1,9},{2,10},{3,11},{4,12},{5,13},{6,14},{7,15},{8,0},{9,1},... | collective-permute-start | bytes 98312 | tf_op jit(solution)/shard_map/ppermute | solution.py:46
  14.8 4.2 %collective-permute-start.2 = (bf16[64,2048]{1,0:T(8,128)(2,1)S(1)}, bf16[64,2048]{1,0:T(8,128)(2,1)S(1)}, u32[]{:S(2)}, u32[]{:S(2)}) collective-permute-start(bf16[64,2048]{1,0:T(8,128)(2,1)S(1)} %get-tuple-element.31), channel_id=1, source_target_pairs={{0,4},{1,5},{2,6},{3,7},{4,0},{5,1},{6,2},{7,3},{8,12},{9,13},{10,... | collective-permute-start | bytes 786440 | tf_op jit(solution)/shard_map/ppermute | solution.py:46
  18.5 1.7 collective-permute-start.9
  19.1 6.4 %collective-permute-start.3 = (bf16[32,2048]{1,0:T(8,128)(2,1)S(1)}, bf16[32,2048]{1,0:T(8,128)(2,1)S(1)}, u32[]{:S(2)}, u32[]{:S(2)}) collective-permute-start(bf16[32,2048]{1,0:T(8,128)(2,1)S(1)} %slice.320), channel_id=1, source_target_pairs={{0,8},{1,9},{2,10},{3,11},{4,12},{5,13},{6,14},{7,15},{8,0},{9,1},... | collective-permute-start | bytes 393224 | tf_op jit(solution)/shard_map/ppermute | solution.py:46
  20.3 7.2 %collective-permute-start.10 = (bf16[32,2048]{1,0:T(8,128)(2,1)S(1)}, bf16[32,2048]{1,0:T(8,128)(2,1)S(1)}, u32[]{:S(2)}, u32[]{:S(2)}) collective-permute-start(bf16[32,2048]{1,0:T(8,128)(2,1)S(1)} %slice.319), channel_id=1, source_target_pairs={{0,8},{1,9},{2,10},{3,11},{4,12},{5,13},{6,14},{7,15},{8,0},{9,1},... | collective-permute-start | bytes 393224 | tf_op jit(solution)/shard_map/ppermute | solution.py:46
  27.5 18.2 %copy-start.4 = (bf16[32,2048]{1,0:T(8,128)(2,1)}, bf16[32,2048]{1,0:T(8,128)(2,1)S(1)}, u32[]{:S(2)}) copy-start(bf16[32,2048]{1,0:T(8,128)(2,1)S(1)} %get-tuple-element.90) | copy-start | bytes 393220
  27.6 25.7 %collective-permute-start.4 = (bf16[32,1152]{1,0:T(8,128)(2,1)S(1)}, bf16[32,1152]{1,0:T(8,128)(2,1)S(1)}, u32[]{:S(2)}, u32[]{:S(2)}) collective-permute-start(bf16[32,1152]{1,0:T(8,128)(2,1)S(1)} %get-tuple-element.102), channel_id=1, source_target_pairs={{0,1},{1,2},{2,3},{3,0},{4,5},{5,6},{6,7},{7,4},{8,9},{9,10},{10,1... | collective-permute-start | bytes 221192 | tf_op jit(solution)/shard_map/ppermute | solution.py:46
  29.2 24.3 %collective-permute-start.5 = (bf16[32,1152]{1,0:T(8,128)(2,1)S(1)}, bf16[32,1152]{1,0:T(8,128)(2,1)S(1)}, u32[]{:S(2)}, u32[]{:S(2)}) collective-permute-start(bf16[32,1152]{1,0:T(8,128)(2,1)S(1)} %get-tuple-element.102), channel_id=1, source_target_pairs={{0,2},{1,3},{2,0},{3,1},{4,6},{5,7},{6,4},{7,5},{8,10},{9,11},{10,... | collective-permute-start | bytes 221192 | tf_op jit(solution)/shard_map/ppermute | solution.py:46
  31.8 6.6 %collective-permute-start.21 = (bf16[32,1024]{1,0:T(8,128)(2,1)S(1)}, bf16[32,1024]{1,0:T(8,128)(2,1)S(1)}, u32[]{:S(2)}, u32[]{:S(2)}) collective-permute-start(bf16[32,1024]{1,0:T(8,128)(2,1)S(1)} %get-tuple-element.95), channel_id=1, source_target_pairs={{0,1},{1,2},{2,3},{3,0},{4,5},{5,6},{6,7},{7,4},{8,9},{9,10},{10,1... | collective-permute-start | bytes 196616 | tf_op jit(solution)/shard_map/ppermute | solution.py:46
  32.0 9.6 %collective-permute-start.22 = (bf16[32,1024]{1,0:T(8,128)(2,1)S(1)}, bf16[32,1024]{1,0:T(8,128)(2,1)S(1)}, u32[]{:S(2)}, u32[]{:S(2)}) collective-permute-start(bf16[32,1024]{1,0:T(8,128)(2,1)S(1)} %get-tuple-element.95), channel_id=1, source_target_pairs={{0,2},{1,3},{2,0},{3,1},{4,6},{5,7},{6,4},{7,5},{8,10},{9,11},{10,... | collective-permute-start | bytes 196616 | tf_op jit(solution)/shard_map/ppermute | solution.py:46
  33.7 9.0 %collective-permute-start.23 = (bf16[32,1024]{1,0:T(8,128)(2,1)S(1)}, bf16[32,1024]{1,0:T(8,128)(2,1)S(1)}, u32[]{:S(2)}, u32[]{:S(2)}) collective-permute-start(bf16[32,1024]{1,0:T(8,128)(2,1)S(1)} %get-tuple-element.95), channel_id=1, source_target_pairs={{0,3},{1,0},{2,1},{3,2},{4,7},{5,4},{6,5},{7,6},{8,11},{9,8},{10,9... | collective-permute-start | bytes 196616 | tf_op jit(solution)/shard_map/ppermute | solution.py:46
  38.4 7.3 %collective-permute-start.16 = (bf16[32,1024]{1,0:T(8,128)(2,1)S(1)}, bf16[32,1024]{1,0:T(8,128)(2,1)S(1)}, u32[]{:S(2)}, u32[]{:S(2)}) collective-permute-start(bf16[32,1024]{1,0:T(8,128)(2,1)S(1)} %get-tuple-element.97), channel_id=1, source_target_pairs={{0,1},{1,2},{2,3},{3,0},{4,5},{5,6},{6,7},{7,4},{8,9},{9,10},{10,1... | collective-permute-start | bytes 196616 | tf_op jit(solution)/shard_map/ppermute | solution.py:46
  41.6 5.7 %collective-permute-start.17 = (bf16[32,1024]{1,0:T(8,128)(2,1)S(1)}, bf16[32,1024]{1,0:T(8,128)(2,1)S(1)}, u32[]{:S(2)}, u32[]{:S(2)}) collective-permute-start(bf16[32,1024]{1,0:T(8,128)(2,1)S(1)} %get-tuple-element.97), channel_id=1, source_target_pairs={{0,2},{1,3},{2,0},{3,1},{4,6},{5,7},{6,4},{7,5},{8,10},{9,11},{10,... | collective-permute-start | bytes 196616 | tf_op jit(solution)/shard_map/ppermute | solution.py:46
  42.7 7.1 %collective-permute-start.18 = (bf16[32,1024]{1,0:T(8,128)(2,1)S(1)}, bf16[32,1024]{1,0:T(8,128)(2,1)S(1)}, u32[]{:S(2)}, u32[]{:S(2)}) collective-permute-start(bf16[32,1024]{1,0:T(8,128)(2,1)S(1)} %get-tuple-element.97), channel_id=1, source_target_pairs={{0,3},{1,0},{2,1},{3,2},{4,7},{5,4},{6,5},{7,6},{8,11},{9,8},{10,9... | collective-permute-start | bytes 196616 | tf_op jit(solution)/shard_map/ppermute | solution.py:46
  45.7 8.4 %collective-permute-start.6 = (bf16[32,1152]{1,0:T(8,128)(2,1)S(1)}, bf16[32,1152]{1,0:T(8,128)(2,1)S(1)}, u32[]{:S(2)}, u32[]{:S(2)}) collective-permute-start(bf16[32,1152]{1,0:T(8,128)(2,1)S(1)} %get-tuple-element.102), channel_id=1, source_target_pairs={{0,3},{1,0},{2,1},{3,2},{4,7},{5,4},{6,5},{7,6},{8,11},{9,8},{10,9... | collective-permute-start | bytes 221192 | tf_op jit(solution)/shard_map/ppermute | solution.py:46
  47.3 8.4 %collective-permute-start.11 = (bf16[32,1152]{1,0:T(8,128)(2,1)S(1)}, bf16[32,1152]{1,0:T(8,128)(2,1)S(1)}, u32[]{:S(2)}, u32[]{:S(2)}) collective-permute-start(bf16[32,1152]{1,0:T(8,128)(2,1)S(1)} %get-tuple-element.100), channel_id=1, source_target_pairs={{0,1},{1,2},{2,3},{3,0},{4,5},{5,6},{6,7},{7,4},{8,9},{9,10},{10,1... | collective-permute-start | bytes 221192 | tf_op jit(solution)/shard_map/ppermute | solution.py:46
  49.9 6.7 %collective-permute-start.12 = (bf16[32,1152]{1,0:T(8,128)(2,1)S(1)}, bf16[32,1152]{1,0:T(8,128)(2,1)S(1)}, u32[]{:S(2)}, u32[]{:S(2)}) collective-permute-start(bf16[32,1152]{1,0:T(8,128)(2,1)S(1)} %get-tuple-element.100), channel_id=1, source_target_pairs={{0,2},{1,3},{2,0},{3,1},{4,6},{5,7},{6,4},{7,5},{8,10},{9,11},{10,... | collective-permute-start | bytes 221192 | tf_op jit(solution)/shard_map/ppermute | solution.py:46
  53.3 4.6 %collective-permute-start.13 = (bf16[32,1152]{1,0:T(8,128)(2,1)S(1)}, bf16[32,1152]{1,0:T(8,128)(2,1)S(1)}, u32[]{:S(2)}, u32[]{:S(2)}) collective-permute-start(bf16[32,1152]{1,0:T(8,128)(2,1)S(1)} %get-tuple-element.100), channel_id=1, source_target_pairs={{0,3},{1,0},{2,1},{3,2},{4,7},{5,4},{6,5},{7,6},{8,11},{9,8},{10,9... | collective-permute-start | bytes 221192 | tf_op jit(solution)/shard_map/ppermute | solution.py:46
  53.6 9.2 %collective-permute-start.24 = (bf16[4,32,1024]{2,1,0:T(8,128)(2,1)S(1)}, bf16[4,32,1024]{2,1,0:T(8,128)(2,1)S(1)}, u32[]{:S(2)}, u32[]{:S(2)}) collective-permute-start(bf16[4,32,1024]{2,1,0:T(8,128)(2,1)S(1)} %get-tuple-element.86), channel_id=1, source_target_pairs={{0,8},{1,9},{2,10},{3,11},{4,12},{5,13},{6,14},{7,15},{8,0},{9,1},... | collective-permute-start | bytes 786440 | tf_op jit(solution)/shard_map/ppermute | solution.py:46
  54.2 14.3 %collective-permute-start.19 = (bf16[4,32,1024]{2,1,0:T(8,128)(2,1)S(1)}, bf16[4,32,1024]{2,1,0:T(8,128)(2,1)S(1)}, u32[]{:S(2)}, u32[]{:S(2)}) collective-permute-start(bf16[4,32,1024]{2,1,0:T(8,128)(2,1)S(1)} %get-tuple-element.88), channel_id=1, source_target_pairs={{0,8},{1,9},{2,10},{3,11},{4,12},{5,13},{6,14},{7,15},{8,0},{9,1},... | collective-permute-start | bytes 786440 | tf_op jit(solution)/shard_map/ppermute | solution.py:46
  55.7 16.0 %collective-permute-start.7 = (bf16[4,32,1152]{2,1,0:T(8,128)(2,1)S(1)}, bf16[4,32,1152]{2,1,0:T(8,128)(2,1)S(1)}, u32[]{:S(2)}, u32[]{:S(2)}) collective-permute-start(bf16[4,32,1152]{2,1,0:T(8,128)(2,1)S(1)} %get-tuple-element.72), channel_id=1, source_target_pairs={{0,8},{1,9},{2,10},{3,11},{4,12},{5,13},{6,14},{7,15},{8,0},{9,1},... | collective-permute-start | bytes 884744 | tf_op jit(solution)/shard_map/ppermute | solution.py:46
  58.0 16.9 %collective-permute-start.14 = (bf16[4,32,1152]{2,1,0:T(8,128)(2,1)S(1)}, bf16[4,32,1152]{2,1,0:T(8,128)(2,1)S(1)}, u32[]{:S(2)}, u32[]{:S(2)}) collective-permute-start(bf16[4,32,1152]{2,1,0:T(8,128)(2,1)S(1)} %get-tuple-element.70), channel_id=1, source_target_pairs={{0,8},{1,9},{2,10},{3,11},{4,12},{5,13},{6,14},{7,15},{8,0},{9,1},... | collective-permute-start | bytes 884744 | tf_op jit(solution)/shard_map/ppermute | solution.py:46
  62.9 12.9 %collective-permute-start.25 = (bf16[2,4,32,1024]{3,2,1,0:T(8,128)(2,1)S(1)}, bf16[2,4,32,1024]{3,2,1,0:T(8,128)(2,1)}, u32[]{:S(2)}, u32[]{:S(2)}) collective-permute-start(bf16[2,4,32,1024]{3,2,1,0:T(8,128)(2,1)S(1)} %get-tuple-element.66), channel_id=1, source_target_pairs={{0,4},{1,5},{2,6},{3,7},{4,0},{5,1},{6,2},{7,3},{8,12},{9,13},{10,... | collective-permute-start | bytes 1572872 | tf_op jit(solution)/shard_map/ppermute | solution.py:46
  69.5 7.4 %collective-permute-start.20 = (bf16[2,4,32,1024]{3,2,1,0:T(8,128)(2,1)}, bf16[2,4,32,1024]{3,2,1,0:T(8,128)(2,1)}, u32[]{:S(2)}, u32[]{:S(2)}) collective-permute-start(bf16[2,4,32,1024]{3,2,1,0:T(8,128)(2,1)} %get-tuple-element.68), channel_id=1, source_target_pairs={{0,4},{1,5},{2,6},{3,7},{4,0},{5,1},{6,2},{7,3},{8,12},{9,13},{10,... | collective-permute-start | bytes 1572872 | tf_op jit(solution)/shard_map/ppermute | solution.py:46
  72.6 5.6 %collective-permute-start.8 = (bf16[2,4,32,1152]{3,2,1,0:T(8,128)(2,1)}, bf16[2,4,32,1152]{3,2,1,0:T(8,128)(2,1)}, u32[]{:S(2)}, u32[]{:S(2)}) collective-permute-start(bf16[2,4,32,1152]{3,2,1,0:T(8,128)(2,1)} %get-tuple-element.64), channel_id=1, source_target_pairs={{0,4},{1,5},{2,6},{3,7},{4,0},{5,1},{6,2},{7,3},{8,12},{9,13},{10,... | collective-permute-start | bytes 1769480 | tf_op jit(solution)/shard_map/ppermute | solution.py:46
  75.8 4.8 %collective-permute-start.15 = (bf16[2,4,32,1152]{3,2,1,0:T(8,128)(2,1)}, bf16[2,4,32,1152]{3,2,1,0:T(8,128)(2,1)}, u32[]{:S(2)}, u32[]{:S(2)}) collective-permute-start(bf16[2,4,32,1152]{3,2,1,0:T(8,128)(2,1)} %get-tuple-element.62), channel_id=1, source_target_pairs={{0,4},{1,5},{2,6},{3,7},{4,0},{5,1},{6,2},{7,3},{8,12},{9,13},{10,... | collective-permute-start | bytes 1769480 | tf_op jit(solution)/shard_map/ppermute | solution.py:46
  131.0 15.0 %collective-permute-start.31 = (bf16[256,1024]{1,0:T(8,128)(2,1)S(1)}, bf16[256,1024]{1,0:T(8,128)(2,1)S(1)}, u32[]{:S(2)}, u32[]{:S(2)}) collective-permute-start(bf16[256,1024]{1,0:T(8,128)(2,1)S(1)} %get-tuple-element.46), channel_id=1, source_target_pairs={{0,4},{1,5},{2,6},{3,7},{4,0},{5,1},{6,2},{7,3},{8,12},{9,13},{10,... | collective-permute-start | bytes 1572872 | tf_op jit(solution)/shard_map/ppermute | solution.py:46
  136.1 10.6 %collective-permute-start.26 = (bf16[256,1024]{1,0:T(8,128)(2,1)S(1)}, bf16[256,1024]{1,0:T(8,128)(2,1)S(1)}, u32[]{:S(2)}, u32[]{:S(2)}) collective-permute-start(bf16[256,1024]{1,0:T(8,128)(2,1)S(1)} %get-tuple-element.44), channel_id=1, source_target_pairs={{0,4},{1,5},{2,6},{3,7},{4,0},{5,1},{6,2},{7,3},{8,12},{9,13},{10,... | collective-permute-start | bytes 1572872 | tf_op jit(solution)/shard_map/ppermute | solution.py:46
  140.8 7.7 %collective-permute-start.41 = (bf16[256,1024]{1,0:T(8,128)(2,1)S(1)}, bf16[256,1024]{1,0:T(8,128)(2,1)S(1)}, u32[]{:S(2)}, u32[]{:S(2)}) collective-permute-start(bf16[256,1024]{1,0:T(8,128)(2,1)S(1)} %get-tuple-element.50), channel_id=1, source_target_pairs={{0,4},{1,5},{2,6},{3,7},{4,0},{5,1},{6,2},{7,3},{8,12},{9,13},{10,... | collective-permute-start | bytes 1572872 | tf_op jit(solution)/shard_map/ppermute | solution.py:46
  145.9 3.5 %collective-permute-start.36 = (bf16[256,1024]{1,0:T(8,128)(2,1)S(1)}, bf16[256,1024]{1,0:T(8,128)(2,1)S(1)}, u32[]{:S(2)}, u32[]{:S(2)}) collective-permute-start(bf16[256,1024]{1,0:T(8,128)(2,1)S(1)} %get-tuple-element.48), channel_id=1, source_target_pairs={{0,4},{1,5},{2,6},{3,7},{4,0},{5,1},{6,2},{7,3},{8,12},{9,13},{10,... | collective-permute-start | bytes 1572872 | tf_op jit(solution)/shard_map/ppermute | solution.py:46
  146.2 9.2 %collective-permute-start.32 = (bf16[128,1024]{1,0:T(8,128)(2,1)S(1)}, bf16[128,1024]{1,0:T(8,128)(2,1)S(1)}, u32[]{:S(2)}, u32[]{:S(2)}) collective-permute-start(bf16[128,1024]{1,0:T(8,128)(2,1)S(1)} %slice.317), channel_id=1, source_target_pairs={{0,8},{1,9},{2,10},{3,11},{4,12},{5,13},{6,14},{7,15},{8,0},{9,1},... | collective-permute-start | bytes 786440 | tf_op jit(solution)/shard_map/ppermute | solution.py:46
  146.9 14.1 %collective-permute-start.27 = (bf16[128,1024]{1,0:T(8,128)(2,1)S(1)}, bf16[128,1024]{1,0:T(8,128)(2,1)S(1)}, u32[]{:S(2)}, u32[]{:S(2)}) collective-permute-start(bf16[128,1024]{1,0:T(8,128)(2,1)S(1)} %slice.318), channel_id=1, source_target_pairs={{0,8},{1,9},{2,10},{3,11},{4,12},{5,13},{6,14},{7,15},{8,0},{9,1},... | collective-permute-start | bytes 786440 | tf_op jit(solution)/shard_map/ppermute | solution.py:46
  148.8 17.9 %collective-permute-start.42 = (bf16[128,1024]{1,0:T(8,128)(2,1)S(1)}, bf16[128,1024]{1,0:T(8,128)(2,1)S(1)}, u32[]{:S(2)}, u32[]{:S(2)}) collective-permute-start(bf16[128,1024]{1,0:T(8,128)(2,1)S(1)} %slice.315), channel_id=1, source_target_pairs={{0,8},{1,9},{2,10},{3,11},{4,12},{5,13},{6,14},{7,15},{8,0},{9,1},... | collective-permute-start | bytes 786440 | tf_op jit(solution)/shard_map/ppermute | solution.py:46
  149.6 22.2 %collective-permute-start.37 = (bf16[128,1024]{1,0:T(8,128)(2,1)S(1)}, bf16[128,1024]{1,0:T(8,128)(2,1)S(1)}, u32[]{:S(2)}, u32[]{:S(2)}) collective-permute-start(bf16[128,1024]{1,0:T(8,128)(2,1)S(1)} %slice.316), channel_id=1, source_target_pairs={{0,8},{1,9},{2,10},{3,11},{4,12},{5,13},{6,14},{7,15},{8,0},{9,1},... | collective-permute-start | bytes 786440 | tf_op jit(solution)/shard_map/ppermute | solution.py:46
  155.5 18.1 %collective-permute-start.33 = (bf16[32,1024]{1,0:T(8,128)(2,1)S(1)}, bf16[32,1024]{1,0:T(8,128)(2,1)S(1)}, u32[]{:S(2)}, u32[]{:S(2)}) collective-permute-start(bf16[32,1024]{1,0:T(8,128)(2,1)S(1)} %get-tuple-element.76), channel_id=1, source_target_pairs={{0,3},{1,0},{2,1},{3,2},{4,7},{5,4},{6,5},{7,6},{8,11},{9,8},{10,9... | collective-permute-start | bytes 196616 | tf_op jit(solution)/shard_map/ppermute | solution.py:46
  156.4 17.3 %collective-permute-start.34 = (bf16[32,1024]{1,0:T(8,128)(2,1)S(1)}, bf16[32,1024]{1,0:T(8,128)(2,1)S(1)}, u32[]{:S(2)}, u32[]{:S(2)}) collective-permute-start(bf16[32,1024]{1,0:T(8,128)(2,1)S(1)} %get-tuple-element.78), channel_id=1, source_target_pairs={{0,2},{1,3},{2,0},{3,1},{4,6},{5,7},{6,4},{7,5},{8,10},{9,11},{10,... | collective-permute-start | bytes 196616 | tf_op jit(solution)/shard_map/ppermute | solution.py:46
  161.0 16.5 %collective-permute-start.35 = (bf16[32,1024]{1,0:T(8,128)(2,1)S(1)}, bf16[32,1024]{1,0:T(8,128)(2,1)S(1)}, u32[]{:S(2)}, u32[]{:S(2)}) collective-permute-start(bf16[32,1024]{1,0:T(8,128)(2,1)S(1)} %get-tuple-element.77), channel_id=1, source_target_pairs={{0,1},{1,2},{2,3},{3,0},{4,5},{5,6},{6,7},{7,4},{8,9},{9,10},{10,1... | collective-permute-start | bytes 196616 | tf_op jit(solution)/shard_map/ppermute | solution.py:46
  166.6 11.0 %collective-permute-start.28 = (bf16[32,1024]{1,0:T(8,128)(2,1)S(1)}, bf16[32,1024]{1,0:T(8,128)(2,1)S(1)}, u32[]{:S(2)}, u32[]{:S(2)}) collective-permute-start(bf16[32,1024]{1,0:T(8,128)(2,1)S(1)} %get-tuple-element.73), channel_id=1, source_target_pairs={{0,3},{1,0},{2,1},{3,2},{4,7},{5,4},{6,5},{7,6},{8,11},{9,8},{10,9... | collective-permute-start | bytes 196616 | tf_op jit(solution)/shard_map/ppermute | solution.py:46
  171.8 8.6 %collective-permute-start.29 = (bf16[32,1024]{1,0:T(8,128)(2,1)S(1)}, bf16[32,1024]{1,0:T(8,128)(2,1)S(1)}, u32[]{:S(2)}, u32[]{:S(2)}) collective-permute-start(bf16[32,1024]{1,0:T(8,128)(2,1)S(1)} %get-tuple-element.75), channel_id=1, source_target_pairs={{0,2},{1,3},{2,0},{3,1},{4,6},{5,7},{6,4},{7,5},{8,10},{9,11},{10,... | collective-permute-start | bytes 196616 | tf_op jit(solution)/shard_map/ppermute | solution.py:46
  173.6 7.9 %collective-permute-start.30 = (bf16[32,1024]{1,0:T(8,128)(2,1)S(1)}, bf16[32,1024]{1,0:T(8,128)(2,1)S(1)}, u32[]{:S(2)}, u32[]{:S(2)}) collective-permute-start(bf16[32,1024]{1,0:T(8,128)(2,1)S(1)} %get-tuple-element.74), channel_id=1, source_target_pairs={{0,1},{1,2},{2,3},{3,0},{4,5},{5,6},{6,7},{7,4},{8,9},{9,10},{10,1... | collective-permute-start | bytes 196616 | tf_op jit(solution)/shard_map/ppermute | solution.py:46
  173.7 8.9 %collective-permute-start.43 = (bf16[32,1024]{1,0:T(8,128)(2,1)S(1)}, bf16[32,1024]{1,0:T(8,128)(2,1)S(1)}, u32[]{:S(2)}, u32[]{:S(2)}) collective-permute-start(bf16[32,1024]{1,0:T(8,128)(2,1)S(1)} %get-tuple-element.82), channel_id=1, source_target_pairs={{0,3},{1,0},{2,1},{3,2},{4,7},{5,4},{6,5},{7,6},{8,11},{9,8},{10,9... | collective-permute-start | bytes 196616 | tf_op jit(solution)/shard_map/ppermute | solution.py:46
  177.5 9.9 %collective-permute-start.44 = (bf16[32,1024]{1,0:T(8,128)(2,1)S(1)}, bf16[32,1024]{1,0:T(8,128)(2,1)S(1)}, u32[]{:S(2)}, u32[]{:S(2)}) collective-permute-start(bf16[32,1024]{1,0:T(8,128)(2,1)S(1)} %get-tuple-element.84), channel_id=1, source_target_pairs={{0,2},{1,3},{2,0},{3,1},{4,6},{5,7},{6,4},{7,5},{8,10},{9,11},{10,... | collective-permute-start | bytes 196616 | tf_op jit(solution)/shard_map/ppermute | solution.py:46
  177.6 9.8 %collective-permute-start.45 = (bf16[32,1024]{1,0:T(8,128)(2,1)S(1)}, bf16[32,1024]{1,0:T(8,128)(2,1)S(1)}, u32[]{:S(2)}, u32[]{:S(2)}) collective-permute-start(bf16[32,1024]{1,0:T(8,128)(2,1)S(1)} %get-tuple-element.83), channel_id=1, source_target_pairs={{0,1},{1,2},{2,3},{3,0},{4,5},{5,6},{6,7},{7,4},{8,9},{9,10},{10,1... | collective-permute-start | bytes 196616 | tf_op jit(solution)/shard_map/ppermute | solution.py:46
  180.4 7.0 %collective-permute-start.38 = (bf16[32,1024]{1,0:T(8,128)(2,1)S(1)}, bf16[32,1024]{1,0:T(8,128)(2,1)S(1)}, u32[]{:S(2)}, u32[]{:S(2)}) collective-permute-start(bf16[32,1024]{1,0:T(8,128)(2,1)S(1)} %get-tuple-element.79), channel_id=1, source_target_pairs={{0,3},{1,0},{2,1},{3,2},{4,7},{5,4},{6,5},{7,6},{8,11},{9,8},{10,9... | collective-permute-start | bytes 196616 | tf_op jit(solution)/shard_map/ppermute | solution.py:46
  181.5 8.8 %collective-permute-start.39 = (bf16[32,1024]{1,0:T(8,128)(2,1)S(1)}, bf16[32,1024]{1,0:T(8,128)(2,1)S(1)}, u32[]{:S(2)}, u32[]{:S(2)}) collective-permute-start(bf16[32,1024]{1,0:T(8,128)(2,1)S(1)} %get-tuple-element.81), channel_id=1, source_target_pairs={{0,2},{1,3},{2,0},{3,1},{4,6},{5,7},{6,4},{7,5},{8,10},{9,11},{10,... | collective-permute-start | bytes 196616 | tf_op jit(solution)/shard_map/ppermute | solution.py:46
  182.5 7.8 %collective-permute-start.40 = (bf16[32,1024]{1,0:T(8,128)(2,1)S(1)}, bf16[32,1024]{1,0:T(8,128)(2,1)S(1)}, u32[]{:S(2)}, u32[]{:S(2)}) collective-permute-start(bf16[32,1024]{1,0:T(8,128)(2,1)S(1)} %get-tuple-element.80), channel_id=1, source_target_pairs={{0,1},{1,2},{2,3},{3,0},{4,5},{5,6},{6,7},{7,4},{8,9},{9,10},{10,1... | collective-permute-start | bytes 196616 | tf_op jit(solution)/shard_map/ppermute | solution.py:46
  (6 other events, 59.4 us)
where the time goes:
time: 192 us; the launch traced here: 191 us
  Pallas kernels  70.5 us (37%)
  waiting for transfers between devices  51.1 us (27%)
  starting transfers between devices  49.7 us (26%)
  other arithmetic  12 us (6%)
  local copies, waits for them, and re-layouts  5.83 us (3%)
    ppermute x46, waiting for transfers between devices, shift(): return lax.ppermute(x, AXES, self.pairs(dy, dc, dz))  51.1 us
    ppermute x46, starting transfers between devices, shift(): return lax.ppermute(x, AXES, self.pairs(dy, dc, dz))  49.7 us
    pallas_call x4, Pallas kernels, expert_up(): pl.pallas_call(functools.partial(up_body, first, last), grid_spec=pltpu.P...  40.6 us
    pallas_call x4, Pallas kernels, expert_down(): pl.pallas_call(down_body, grid=(steps,), in_specs=[pl.BlockSpec(act.shape...  18.2 us
    another operation x17, other arithmetic, gather(): return jnp.stack([x] + moved)  8.77 us
    pallas_call x1, Pallas kernels, front(): pl.pallas_call(functools.partial(front_body, heads, near_rows), grid_spec...  5.84 us
  transfers between devices with their start and end apart: 46, of which 19 were waited for; matrix products, arithmetic and copies ran while one was open for 6% of the time, Pallas kernels for 10%

commit v1 on v0

v1 whole, which is shorter than its diff:
```python
import functools
import jax
import jax.numpy as jnp
from jax import lax
from jax.experimental import pallas as pl
from jax.experimental.pallas import tpu as pltpu
from jax.sharding import PartitionSpec as P


BF = jnp.bfloat16
F32 = jnp.float32
AXES = ("head", "req")
LANES = 128
MIX_CHUNKS = 2
AG_CHUNKS = 4
RS_CHUNKS = 4
BATCH = 16


def in_hbm(*arrays):
    return [pltpu.with_memory_space_constraint(a, pltpu.HBM) for a in arrays]


class Ring:
    def __init__(self, heads, reqs):
        self.heads, self.reqs = heads, reqs
        self.cores = 2 if heads % 2 == 0 else 1
        self.ys = heads // self.cores

    def pairs(self, dy=0, dc=0, dz=0, flip=0):
        found = []
        for y in range(self.ys):
            for c in range(self.cores):
                for z in range(self.reqs):
                    there = ((y + dy) % self.ys) * self.cores + (c + dc) % self.cores
                    to = (z ^ flip) if flip else (z + dz) % self.reqs
                    found.append(((y * self.cores + c) * self.reqs + z, there * self.reqs + to))
        return found

    def shift(self, x, **how):
        return lax.ppermute(x, AXES, self.pairs(**how))

    def flips(self):
        if self.reqs & (self.reqs - 1):
            return None
        return [1 << b for b in range(self.reqs.bit_length() - 1)]

    def gather_z(self, x):
        flips = self.flips()
        if flips is None:
            return self.gather(x, "dz")
        for flip in reversed(flips):
            x = jnp.stack([x, self.shift(x, flip=flip)])
        return x

    def scatter_z(self, total):
        flips = self.flips()
        if flips is None:
            parts = [total[s].astype(BF) for s in range(1, self.reqs)]
            return self.scatter(parts, total[0], "dz")
        for flip in flips:
            half = total.shape[0] // 2
            sent = self.shift(total[half:].astype(BF), flip=flip)
            total = total[:half] + sent.astype(F32)
        return total[0]

    def gather(self, x, axis):
        count = {"dc": self.cores, "dy": self.ys, "dz": self.reqs}[axis]
        moved = [self.shift(x, **{axis: s}) for s in range(1, count)]
        return jnp.stack([x] + moved)

    def scatter(self, parts, keep, axis):
        total = keep
        for s, part in enumerate(parts, 1):
            total = total + self.shift(part, **{axis: -s}).astype(F32)
        return total


def prep_body(heads, parents, ids, step_raw, bias, decay, factor, grown, named):
    reqs, nodes = parents.shape
    rows = nodes * reqs
    lane = lax.broadcasted_iota(jnp.int32, (rows, rows), 1)
    row = lax.broadcasted_iota(jnp.int32, (rows, rows), 0)
    hop = jnp.concatenate([parents[:, j : j + 1] for j in range(nodes)], axis=0)
    at = jnp.where(hop >= 0, hop * reqs + lax.broadcasted_iota(jnp.int32, hop.shape, 0) % reqs, -1)
    power = jnp.where(at == lane, 1.0, 0.0)
    reach = jnp.where(row == lane, 1.0, 0.0) + power
    power = power.astype(BF)
    span = 2
    while span * reqs < rows:
        power = jnp.dot(power, power, preferred_element_type=F32).astype(BF)
        reach = reach + jnp.dot(reach.astype(BF), power, preferred_element_type=F32)
        span *= 2
    raw = step_raw[...].reshape(rows, heads) + bias[...]
    step = jnp.maximum(raw, 0.0) + jnp.log1p(jnp.exp(-jnp.abs(raw)))
    rate = -step * decay[...]
    blank = jnp.zeros((rows, rows - heads), F32)
    wide_step = jnp.concatenate([step, blank], axis=1)
    wide_rate = jnp.concatenate([rate, blank], axis=1)
    depth = jnp.dot(
        reach, wide_rate, preferred_element_type=F32, precision=lax.Precision.HIGHEST
    )
    grown[...] = jnp.exp(depth[:, :heads])
    depth_t = depth.T
    step_t = wide_step.T
    linked = reach > 0
    for h in range(heads):
        spread = jnp.where(linked, depth[:, h : h + 1] - depth_t[h : h + 1, :], 0.0)
        factor[h] = jnp.where(linked, jnp.exp(spread) * step_t[h : h + 1, :], 0.0)
    chosen = ids[...].reshape(named.shape[0], ids.shape[2])
    label = lax.broadcasted_iota(jnp.int32, named.shape, 1)
    mask = jnp.zeros(named.shape, F32)
    for k in range(ids.shape[2]):
        mask = jnp.where(chosen[:, k : k + 1] == label, 1.0, mask)
    named[...] = mask.astype(BF)


def prepare(parents, expert_ids, step_raw, step_bias, decay_rate, experts):
    nodes, reqs, heads = step_raw.shape
    rows = nodes * reqs
    tokens = expert_ids.shape[0] * expert_ids.shape[1]
    lanes = -(-experts // LANES) * LANES
    return pl.pallas_call(
        functools.partial(prep_body, heads),
        out_shape=(
            jax.ShapeDtypeStruct((heads, rows, rows), F32),
            jax.ShapeDtypeStruct((rows, heads), F32),
            jax.ShapeDtypeStruct((tokens, lanes), BF),
        ),
        compiler_params=pltpu.CompilerParams(vmem_limit_bytes=16 << 20),
        name="prepare",
    )(
        *in_hbm(
            parents, expert_ids, step_raw, step_bias.reshape(1, heads), decay_rate.reshape(1, heads)
        ),
    )


def gate_body(experts, after, gain, router_t, named, out):
    tokens, width = after.shape
    lanes = out.shape[1]
    wide = after[...].astype(F32)
    scale = lax.rsqrt(jnp.sum(wide * wide, axis=1, keepdims=True) / width + 1e-05)
    normed = (wide * scale * gain[...]).astype(BF)
    logits = lax.dot_general(
        normed, router_t[...], (((1,), (1,)), ((), ())), preferred_element_type=F32
    )
    powered = jnp.where(named[:, :experts] > 0, jnp.exp(logits), 0.0)
    gate = powered / jnp.sum(powered, axis=1, keepdims=True)
    top = scale.astype(BF).astype(F32)
    middle = (scale - top).astype(BF).astype(F32)
    low = scale - top - middle
    lane = lax.broadcasted_iota(jnp.int32, (tokens, lanes - experts), 1)
    head = jnp.where(lane == 0, top, jnp.where(lane == 1, middle, jnp.where(lane == 2, low, 0.0)))
    out[...] = jnp.concatenate([head, gate], axis=1).astype(BF)


def gate_lanes(experts):
    return -(-(experts + 3) // LANES) * LANES


def gates(after_mixer, norm_gain, router, named):
    tokens, width = after_mixer.shape
    experts = router.shape[1]
    return pl.pallas_call(
        functools.partial(gate_body, experts),
        out_shape=jax.ShapeDtypeStruct((tokens, gate_lanes(experts)), BF),
        compiler_params=pltpu.CompilerParams(vmem_limit_bytes=16 << 20),
        name="gates",
    )(after_mixer, norm_gain.reshape(1, width), router.T, named.astype(F32))


def project_blocks(rows, weight, held, arrived, first, near, far):
    near_rows = near.shape[0]
    block = held.shape[2]
    for b in range(held.shape[0]):
        weight_copy(weight, held, arrived, first, b).wait()
        total = jnp.dot(rows, held[b], preferred_element_type=F32)
        near[:, b * block : (b + 1) * block] = total[:near_rows]
        far[:, b * block : (b + 1) * block] = total[near_rows:].astype(BF)


def weight_copy(weight, held, arrived, first, b):
    block = held.shape[2]
    return pltpu.make_async_copy(
        weight.at[:, pl.ds(first + b * block, block)], held.at[b], arrived.at[b]
    )


def front_body(
    heads, first, slot_of, goes_to, early, x, state, factor, grown, skip, weight,
    near, far, mixed_rows, read_rows, write_rows, cache, result, states_held, states_in, held, arrived,
):
    blocks, tokens = early.shape[0], early.shape[1]
    nodes, reqs, columns = x.shape
    rows = nodes * reqs
    size = columns // heads
    states = state.shape[2]
    for r in range(reqs):
        pltpu.make_async_copy(state.at[r], states_held.at[r], states_in.at[r]).start()
    for b in range(held.shape[0]):
        weight_copy(weight, held, arrived, first, b).start()
    for a in range(blocks):
        block = early[slot_of[a]].astype(F32)
        write_rows[a * tokens : (a + 1) * tokens] = block[:, :states]
        read_rows[a * tokens : (a + 1) * tokens] = block[:, states : 2 * states]
    writes = write_rows[...].astype(BF)
    reads = read_rows[...].astype(BF)
    affinity = lax.dot_general(
        reads, writes, (((1,), (1,)), ((), ())), preferred_element_type=F32
    )
    for r in range(reqs):
        pltpu.make_async_copy(state.at[r], states_held.at[r], states_in.at[r]).wait()
        mine = read_rows[pl.ds(r, nodes, stride=reqs), :].astype(BF)
        got = lax.dot_general(
            mine, states_held[r], (((1,), (1,)), ((), ())), preferred_element_type=F32
        )
        for i in range(columns // LANES):
            cache.at[i][pl.ds(r, nodes, stride=reqs), :] = got[:, i * LANES : (i + 1) * LANES]
    values = x[...].reshape(rows, columns)
    pair = 2 * size
    left = lax.broadcasted_iota(jnp.int32, (rows, pair), 1) < size
    for h in range(0, heads, 2):
        cut = slice(h * size, h * size + pair)
        own = values[:, cut]
        one = (factor[h] * affinity).astype(BF)
        two = (factor[h + 1] * affinity).astype(BF)
        zero = jnp.zeros_like(own)
        both = jnp.dot(
            jnp.concatenate([one, two], axis=1),
            jnp.concatenate([jnp.where(left, own, zero), jnp.where(left, zero, own)], axis=0),
            preferred_element_type=F32,
        )
        grow = jnp.where(left, grown[:, h : h + 1], grown[:, h + 1 : h + 2])
        gain = jnp.where(left, skip[:, h : h + 1], skip[:, h + 1 : h + 2])
        both = both + cache[h * size // LANES] * grow + gain * own.astype(F32)
        result[:, cut] = both.astype(BF).astype(F32)
    for s in range(blocks):
        start = pl.multiple_of(goes_to[s] * tokens, tokens)
        mixed_rows[s * tokens : (s + 1) * tokens] = result[pl.ds(start, tokens)].astype(BF)
    project_blocks(mixed_rows[...], weight, held, arrived, first, near, far)


def weight_scratch(columns, span):
    block = min(span, 512)
    return [
        pltpu.VMEM((span // block, columns, block), BF),
        pltpu.SemaphoreType.DMA((span // block,)),
    ]


def front(early, x, state, factor, grown, skip_gain, out_proj, slot_of, goes_to, near_rows, part, parts):
    nodes, reqs, columns = x.shape
    heads = skip_gain.shape[0]
    rows = nodes * reqs
    states = state.shape[3]
    span = out_proj.shape[1] // parts
    state = state.reshape(state.shape[0], columns, states)
    skip = skip_gain.reshape(1, heads)
    x, state, skip, out_proj = in_hbm(x, state, skip, out_proj)
    vmem = pl.BlockSpec(memory_space=pltpu.VMEM)
    hbm = pl.BlockSpec(memory_space=pltpu.HBM)
    return pl.pallas_call(
        functools.partial(front_body, heads, part * span),
        grid_spec=pltpu.PrefetchScalarGridSpec(
            num_scalar_prefetch=2,
            in_specs=[vmem, vmem, hbm, vmem, vmem, vmem, hbm],
            out_specs=(vmem, vmem, vmem),
            scratch_shapes=[
                pltpu.VMEM((rows, states), F32),
                pltpu.VMEM((rows, states), F32),
                pltpu.VMEM((columns // LANES, rows, LANES), F32),
                pltpu.VMEM((rows, columns), F32),
                pltpu.VMEM(state.shape, BF),
                pltpu.SemaphoreType.DMA((reqs,)),
                *weight_scratch(columns, span),
            ],
        ),
        out_shape=(
            jax.ShapeDtypeStruct((near_rows, span), F32),
            jax.ShapeDtypeStruct((rows - near_rows, span), BF),
            jax.ShapeDtypeStruct((rows, columns), BF),
        ),
        compiler_params=pltpu.CompilerParams(vmem_limit_bytes=32 << 20),
        cost_estimate=pl.CostEstimate(
            flops=2 * rows * columns * span, transcendentals=0, bytes_accessed=2 * columns * span
        ),
        name="front",
    )(slot_of, goes_to, early, x, state, factor, grown, skip, out_proj)


def project_body(first, rows, weight, near, far, held, arrived):
    for b in range(held.shape[0]):
        weight_copy(weight, held, arrived, first, b).start()
    project_blocks(rows[...], weight, held, arrived, first, near, far)


def project(rows, out_proj, near_rows, part, parts):
    count, columns = rows.shape
    span = out_proj.shape[1] // parts
    vmem = pl.BlockSpec(memory_space=pltpu.VMEM)
    return pl.pallas_call(
        functools.partial(project_body, part * span),
        in_specs=[vmem, pl.BlockSpec(memory_space=pltpu.HBM)],
        out_specs=(vmem, vmem),
        out_shape=(
            jax.ShapeDtypeStruct((near_rows, span), F32),
            jax.ShapeDtypeStruct((count - near_rows, span), BF),
        ),
        scratch_shapes=weight_scratch(columns, span),
        compiler_params=pltpu.CompilerParams(vmem_limit_bytes=16 << 20),
        cost_estimate=pl.CostEstimate(
            flops=2 * count * columns * span, transcendentals=0, bytes_accessed=2 * columns * span
        ),
        name="project",
    )(rows, *in_hbm(out_proj))


def up_body(first, last, begin, token_at, x, wg, wu, *rest):
    rest = list(rest)
    if not first:
        gin, uin = rest.pop(0), rest.pop(0)
    if last:
        extra, spot, share = rest.pop(0), rest.pop(0), rest.pop(0)
    if last:
        act_out, comb_out, spread, picked, gates_held, ups_held, arrived, scales = rest
    else:
        gout, uout, spread, picked, gates_held, ups_held, arrived = rest
    q = pl.program_id(0)
    tokens, width = x.shape
    tall = width // LANES
    slots = picked.shape[0] // tall

    def copies(e):
        cut = pl.ds(begin, width)
        return (
            pltpu.make_async_copy(wg.at[e, cut], gates_held.at[e], arrived.at[0, e]),
            pltpu.make_async_copy(wu.at[e, cut], ups_held.at[e], arrived.at[1, e]),
        )

    @pl.when(q == 0)
    def _():
        for e in range(gates_held.shape[0]):
            for copy in copies(e):
                copy.start()
        for i in range(tall):
            spread[pl.ds(i, tokens, stride=tall), :] = x[:, i * LANES : (i + 1) * LANES].astype(F32)

    for c in range(0, slots, BATCH):
        at = [token_at[q * slots + c + i] for i in range(BATCH)]
        got = [spread[pl.ds(pl.multiple_of(t * tall, tall), tall)] for t in at]
        picked[c * tall : (c + BATCH) * tall] = jnp.concatenate(got, axis=0)
        if last:
            got = [extra[pl.ds(t, 1)] for t in at]
            for i in range(BATCH):
                scales[c + i : c + i + 1] = got[i]
    rows = jnp.concatenate(
        [picked[pl.ds(i, slots, stride=tall), :].astype(BF) for i in range(tall)], axis=1
    )
    for copy in copies(q):
        copy.wait()
    gated = jnp.dot(rows, gates_held[q], preferred_element_type=F32)
    lifted = jnp.dot(rows, ups_held[q], preferred_element_type=F32)
    if not first:
        gated = gated + gin[0]
        lifted = lifted + uin[0]
    if not last:
        gout[0] = gated
        uout[0] = lifted
        return
    scale = scales[:, 0:1] + scales[:, 1:2] + scales[:, 2:3]
    gated = gated * scale
    lifted = lifted * scale
    act_out[0] = (gated / (1.0 + jnp.exp(-gated)) * lifted).astype(BF)
    lane = lax.broadcasted_iota(jnp.int32, (tokens, slots), 1)
    column = lax.broadcasted_iota(jnp.int32, spot.shape, 1)
    own_spot = jnp.sum(jnp.where(column == q, spot[...], 0), axis=1, keepdims=True)
    own_share = jnp.sum(jnp.where(column == q, share[...], 0.0), axis=1, keepdims=True)
    comb_out[...] = jnp.where(lane == own_spot, own_share, 0.0).astype(BF)


def expert_up(k, chunks, token_at, x, gate_proj, up_proj, sums, extras):
    held = gate_proj.shape[0]
    tokens, width = x.shape
    slots = token_at.shape[0] // held
    units = gate_proj.shape[2]
    first, last = k == 0, k == chunks - 1
    per_expert = lambda *tail: pl.BlockSpec((1,) + tail, lambda q, *_: (q, 0, 0))
    whole = lambda a: pl.BlockSpec(a.shape, lambda q, *_: (0, 0))
    weight = pl.BlockSpec(memory_space=pltpu.HBM)
    in_specs = [whole(x), weight, weight]
    args = [x, *in_hbm(gate_proj, up_proj)]
    scratch = [
        pltpu.VMEM((tokens * width // LANES, LANES), F32),
        pltpu.VMEM((slots * width // LANES, LANES), F32),
        pltpu.VMEM((held, width, units), BF),
        pltpu.VMEM((held, width, units), BF),
        pltpu.SemaphoreType.DMA((2, held)),
    ]
    if not first:
        in_specs += [per_expert(slots, units)] * 2
        args += list(sums)
    if last:
        in_specs += [whole(a) for a in extras]
        args += list(extras)
        out_shape = (
            jax.ShapeDtypeStruct((held, slots, units), BF),
            jax.ShapeDtypeStruct((tokens, held * slots), BF),
        )
        out_specs = (per_expert(slots, units), pl.BlockSpec((tokens, slots), lambda q, *_: (0, q)))
        scratch.append(pltpu.VMEM((slots, extras[0].shape[1]), F32))
    else:
        out_shape = (jax.ShapeDtypeStruct((held, slots, units), F32),) * 2
        out_specs = (per_expert(slots, units),) * 2
    return pl.pallas_call(
        functools.partial(up_body, first, last, k * width),
        grid_spec=pltpu.PrefetchScalarGridSpec(
            num_scalar_prefetch=1,
            grid=(held,),
            in_specs=in_specs,
            out_specs=out_specs,
            scratch_shapes=scratch,
        ),
        out_shape=out_shape,
        compiler_params=pltpu.CompilerParams(vmem_limit_bytes=48 << 20),
        cost_estimate=pl.CostEstimate(
            flops=4 * held * slots * width * units,
            transcendentals=0,
            bytes_accessed=4 * held * width * units,
        ),
    )(token_at, *args)


def down_body(begin, act, comb, wd, keep, send, halves, held_rows, arrived):
    held, slots, _ = act.shape
    width = keep.shape[1]

    def copy(q):
        return pltpu.make_async_copy(
            wd.at[q, :, pl.ds(begin, width)], held_rows.at[q], arrived.at[q]
        )

    for q in range(held):
        copy(q).start()
    for q in range(held):
        copy(q).wait()
        halves[q * slots : (q + 1) * slots] = jnp.dot(
            act[q], held_rows[q], preferred_element_type=F32
        ).astype(BF)
    kept = keep.shape[0]
    block = min(width, 256)
    for j in range(0, width, block):
        cut = slice(j, j + block)
        total = jnp.dot(comb[...], halves[:, cut], preferred_element_type=F32)
        keep[:, cut] = total[:kept]
        send[:, cut] = total[kept:].astype(BF)


def expert_down(k, chunks, act, comb, down_proj, kept):
    held, slots, units = act.shape
    tokens = comb.shape[0]
    width = down_proj.shape[2] // chunks
    vmem = pl.BlockSpec(memory_space=pltpu.VMEM)
    return pl.pallas_call(
        functools.partial(down_body, k * width),
        in_specs=[vmem, vmem, pl.BlockSpec(memory_space=pltpu.HBM)],
        out_specs=(vmem, vmem),
        out_shape=(
            jax.ShapeDtypeStruct((kept, width), F32),
            jax.ShapeDtypeStruct((tokens - kept, width), BF),
        ),
        scratch_shapes=[
            pltpu.VMEM((held * slots, width), BF),
            pltpu.VMEM((held, units, width), BF),
            pltpu.SemaphoreType.DMA((held,)),
        ],
        compiler_params=pltpu.CompilerParams(vmem_limit_bytes=48 << 20),
        cost_estimate=pl.CostEstimate(
            flops=2 * held * slots * width * (tokens + units),
            transcendentals=0,
            bytes_accessed=2 * held * width * units,
        ),
    )(act, comb, *in_hbm(down_proj))


def layer(
    ssm_input,
    write_vec,
    read_vec,
    step_raw,
    step_bias,
    decay_rate,
    skip_gain,
    cache_state,
    parents,
    out_proj,
    residual,
    norm_gain,
    router,
    expert_ids,
    gate_proj,
    up_proj,
    down_proj,
):
    _, requests, _ = ssm_input.shape
    local_nodes, _, width = residual.shape
    tokens = local_nodes * requests
    topk = expert_ids.shape[2]
    experts = router.shape[1]
    held = gate_proj.shape[0]
    ring = Ring(lax.axis_size("head"), lax.axis_size("req"))
    cores, ys, reqs = ring.cores, ring.ys, ring.reqs
    head_at = lax.axis_index("head")
    y_at, c_at = head_at // cores, head_at % cores
    device = head_at * reqs + lax.axis_index("req")
    e0 = (device * held) % experts

    states = write_vec.shape[2]
    early = jnp.concatenate(
        [write_vec.reshape(tokens, states), read_vec.reshape(tokens, states)], axis=1
    )
    early = ring.gather(ring.gather(early, "dc"), "dy")
    early = early.reshape(ys * cores, tokens, -1)
    absolute = jnp.arange(ys * cores, dtype=jnp.int32)
    slot_of = ((y_at - absolute // cores) % ys) * cores + (c_at - absolute % cores) % cores
    slots = jnp.arange(cores * ys, dtype=jnp.int32)
    goes_to = ((y_at - slots % ys) % ys) * cores + (c_at - slots // ys) % cores
    factor, grown, named = prepare(parents, expert_ids, step_raw, step_bias, decay_rate, experts)
    near_rows = ys * tokens

    all_tokens = cores * ys * reqs * tokens
    capacity = 2 * tokens * topk // (experts + experts // 4)
    room = capacity * cores * ys * reqs

    rows_left = residual.reshape(tokens, width)
    mixes = []
    part_span = width // MIX_CHUNKS
    for m in range(MIX_CHUNKS):
        cut = slice(m * part_span, (m + 1) * part_span)
        if m == 0:
            mixed, away, mixed_rows = front(
                early, ssm_input, cache_state, factor, grown, skip_gain, out_proj,
                slot_of, goes_to, near_rows, m, MIX_CHUNKS,
            )
        else:
            mixed, away = project(mixed_rows, out_proj, near_rows, m, MIX_CHUNKS)
        if cores > 1:
            mixed = ring.scatter([away], mixed, "dc")
        mixed = mixed.reshape(ys, tokens, part_span)
        mixed = ring.scatter([mixed[s].astype(BF) for s in range(1, ys)], mixed[0], "dy")
        mixes.append((rows_left[:, cut].astype(F32) + mixed).astype(BF))
    span = width // AG_CHUNKS
    after_mixer = jnp.concatenate(mixes, axis=1)
    sums = None
    for k in range(AG_CHUNKS):
        cut = slice(k * span, (k + 1) * span)
        m = k * MIX_CHUNKS // AG_CHUNKS
        local = slice(k * span - m * part_span, (k + 1) * span - m * part_span)
        payload = (mixes[m][:, local].astype(F32) * norm_gain[cut]).astype(BF)
        extras = None
        if k == AG_CHUNKS - 1:
            extra = gates(after_mixer, norm_gain, router, named)
            payload = jnp.concatenate([payload, extra], axis=1)
        if k == 0:
            payload = jnp.concatenate([payload, named], axis=1)
        rows = ring.gather_z(payload)
        rows = ring.gather(rows, "dy")
        rows = ring.gather(rows, "dc")
        rows = rows.reshape(all_tokens, -1)
        if k == 0:
            named_all = rows[:, span : span + experts]
            mine = lax.dynamic_slice_in_dim(named_all, e0, held, axis=1)
            order = jnp.arange(all_tokens, dtype=jnp.int32)
            before = (order[:, None] > order[None, :]).astype(BF)
            rank = jnp.dot(before, mine, preferred_element_type=F32)
            place = jnp.where(mine > 0, rank, -1.0).astype(jnp.int32)
            spots = jnp.arange(room, dtype=jnp.int32)
            chosen = place.T[:, None, :] == spots[None, :, None]
            token_at = jnp.sum(jnp.where(chosen, order, 0), axis=2).reshape(-1)
        if k == AG_CHUNKS - 1:
            extra = rows[:, rows.shape[1] - gate_lanes(experts) :].astype(F32)
            share = lax.dynamic_slice_in_dim(
                extra, e0 + extra.shape[1] - experts, held, axis=1
            )
            extras = (extra, place, share)
        rows = rows[:, :span]
        sums = expert_up(k, AG_CHUNKS, token_at, rows, gate_proj, up_proj, sums, extras)
    act, comb = sums

    pieces = []
    span = width // RS_CHUNKS
    for k in range(RS_CHUNKS):
        keep, send = expert_down(k, RS_CHUNKS, act, comb, down_proj, ys * reqs * tokens)
        total = ring.scatter([send], keep, "dc") if cores > 1 else keep
        total = total.reshape(ys, reqs * tokens, span)
        total = ring.scatter([total[s].astype(BF) for s in range(1, ys)], total[0], "dy")
        total = ring.scatter_z(total.reshape(reqs, tokens, span))
        cut = slice(k * span, (k + 1) * span)
        pieces.append((after_mixer[:, cut].astype(F32) + total).astype(BF))
    return jnp.concatenate(pieces, axis=1).reshape(local_nodes, requests, width)


def solution(mesh):
    in_specs = (
        P(None, ("groups", "req"), "head"),
        P("head", ("groups", "req"), None),
        P("head", ("groups", "req"), None),
        P(None, ("groups", "req"), "head"),
        P("head"),
        P("head"),
        P("head"),
        P(("groups", "req"), "head", None, None),
        P(("groups", "req"), None),
        P("head", None),
        P("head", ("groups", "req"), None),
        P(),
        P(),
        P("head", ("groups", "req"), None),
        P(("head", "req"), None, None),
        P(("head", "req"), None, None),
        P(("head", "req"), None, None),
    )
    out_specs = P("head", ("groups", "req"), None)
    return jax.shard_map(layer, mesh=mesh, in_specs=in_specs, out_specs=out_specs, check_vma=False)
```

time: 192 us -> 193 us (level)
  starting transfers between devices: 49.7 us -> 35.7 us
  waiting for transfers between devices: 51.1 us -> 64.6 us
  local copies, waits for them, and re-layouts: 5.83 us -> 8.26 us
    ppermute x46 -> x38, starting transfers between devices: 49.7 us -> 35.7 us  [shift(): return lax.ppermute(x, AXES, self.pairs(**how))]
    ppermute x46 -> x38, waiting for transfers between devices: 51.1 us -> 64.6 us  [shift(): return lax.ppermute(x, AXES, self.pairs(**how))]
    unnamed x16 -> x26, local copies, waits for them, and re-layouts: 1.26 us -> 5.52 us
    pallas_call x10 -> x11, Pallas kernels: 68.2 us -> 68.6 us  [the longest x4 40.6 us: expert_up(): pl.pallas_call(functools.partial(up_body, first, last, k * width), grid_s...]
    another operation x17 -> x15, other arithmetic: 8.77 us -> 8.65 us  [gather(): return jnp.stack([x] + moved)]
  transfers between devices with their start and end apart: 46 -> 38, of which waited for: 19 -> 22; matrix products, arithmetic and copies ran while one was open for 6% -> 5% of each run, Pallas kernels for 10% -> 10%
where the time goes in v1:
time: 193 us
  Pallas kernels  71.1 us (37%)
  waiting for transfers between devices  64.6 us (33%)
  starting transfers between devices  35.7 us (18%)
  other arithmetic  11.2 us (6%)
  local copies, waits for them, and re-layouts  8.26 us (4%)
    ppermute x38, waiting for transfers between devices, shift(): return lax.ppermute(x, AXES, self.pairs(**how))  64.6 us
    pallas_call x4, Pallas kernels, expert_up(): pl.pallas_call(functools.partial(up_body, first, last, k * width), grid_s...  40.6 us
    ppermute x38, starting transfers between devices, shift(): return lax.ppermute(x, AXES, self.pairs(**how))  35.7 us
    pallas_call x4, Pallas kernels, expert_down(): pl.pallas_call(functools.partial(down_body, k * width), in_specs=[vmem, v...  19.2 us
    another operation x15, other arithmetic, gather(): return jnp.stack([x] + moved)  8.65 us
    pallas_call x1, Pallas kernels, front(): pl.pallas_call(functools.partial(front_body, heads, part * span), grid_sp...  5.82 us
    unnamed x26, local copies, waits for them, and re-layouts  5.52 us
  transfers between devices with their start and end apart: 38, of which 22 were waited for; matrix products, arithmetic and copies ran while one was open for 5% of the time, Pallas kernels for 10%

profile of v1, /device:TPU:0, one launch (start us, length us, event | category | flops | bytes accessed | tf_op | source)
XLA Modules:
  0.0 192.6 jit_solution(15117204909628792010)
XLA Ops:
  2.1 2.8 %collective-permute-start.1 = (bf16[2,32,256]{2,1,0:T(8,128)(2,1)S(1)}, bf16[2,32,256]{2,1,0:T(8,128)(2,1)S(1)}, u32[]{:S(2)}, u32[]{:S(2)}) collective-permute-start(bf16[2,32,256]{2,1,0:T(8,128)(2,1)S(1)} %get-tuple-element.92), channel_id=1, source_target_pairs={{0,8},{1,9},{2,10},{3,11},{4,12},{5,13},{6,14},{7,15},{8,0},{9,1},... | collective-permute-start | bytes 98312 | tf_op jit(solution)/shard_map/ppermute | solution.py:41
  4.9 2.4 %prepare.1 = (f32[16,128,128]{2,1,0:T(8,128)S(1)}, f32[128,16]{1,0:T(8,128)S(1)}, bf16[32,128]{1,0:T(8,128)(2,1)S(1)}) custom-call(s32[8,16]{1,0:T(8,128)} %parents.1, s32[4,8,10]{2,1,0:T(8,128)} %ids.1, f32[16,8,16]{2,1,0:T(8,128)} %step_raw.1, f32[1,16]{1,0:T(1,128)} %bitcast.137, f32[1,16]{1,0:T(1,128)} %bitcast.138), custom_call_target="tpu_custom_call" | custom-call | tf_op jit(solution)/shard_map/prepare/pallas_call | solution.py:123
  7.4 5.8 %front.1 = (f32[64,2048]{1,0:T(8,128)S(1)}, bf16[64,2048]{1,0:T(8,128)(2,1)S(1)}, bf16[128,1024]{1,0:T(8,128)(2,1)S(1)}) custom-call(s32[4]{0:T(128)S(1)} %get-tuple-element.99.slot_of, s32[4]{0:T(128)S(1)} %get-tuple-element.100.goes_to, bf16[4,32,256]{2,1,0:T(8,128)(2,1)S(1)} %bitcast.98, bf16[16,8,1024]{2,1,0:T(8,128)(2,1)} %x.1, ...), custom_call_target="tpu_custom_call" | custom-call | flops 536870912 | bytes 4194304 | tf_op jit(solution)/shard_map/front/pallas_call | solution.py:263
  13.3 2.5 %project.1 = (f32[64,2048]{1,0:T(8,128)S(1)}, bf16[64,2048]{1,0:T(8,128)(2,1)S(1)}) custom-call(bf16[128,1024]{1,0:T(8,128)(2,1)S(1)} %get-tuple-element.34.rows, bf16[1024,4096]{1,0:T(8,128)(2,1)} %weight.3), custom_call_target="tpu_custom_call" | custom-call | flops 536870912 | bytes 4194304 | tf_op jit(solution)/shard_map/project/pallas_call | solution.py:302
  16.5 1.5 collective-permute-start.3
  19.2 3.7 %collective-permute-done.3 = bf16[32,2048]{1,0:T(8,128)(2,1)S(1)} collective-permute-done((bf16[32,2048]{1,0:T(8,128)(2,1)S(1)}, bf16[32,2048]{1,0:T(8,128)(2,1)S(1)}, u32[]{:S(2)}, u32[]{:S(2)}) %collective-permute-start.3) | collective-permute-done | bytes 131104 | tf_op jit(solution)/shard_map/ppermute | solution.py:41
  22.9 1.9 collective-permute-done.9
  25.0 2.7 %collective-permute-start.4 = (bf16[32,1152]{1,0:T(8,128)(2,1)S(1)}, bf16[32,1152]{1,0:T(8,128)(2,1)S(1)}, u32[]{:S(2)}, u32[]{:S(2)}) collective-permute-start(bf16[32,1152]{1,0:T(8,128)(2,1)S(1)} %get-tuple-element.90), channel_id=1, source_target_pairs={{0,2},{1,3},{2,0},{3,1},{4,6},{5,7},{6,4},{7,5},{8,10},{9,11},{10,... | collective-permute-start | bytes 221192 | tf_op jit(solution)/shard_map/ppermute | solution.py:41
  28.0 2.7 %collective-permute-start.14 = (bf16[32,1024]{1,0:T(8,128)(2,1)S(1)}, bf16[32,1024]{1,0:T(8,128)(2,1)S(1)}, u32[]{:S(2)}, u32[]{:S(2)}) collective-permute-start(bf16[32,1024]{1,0:T(8,128)(2,1)S(1)} %get-tuple-element.85), channel_id=1, source_target_pairs={{0,2},{1,3},{2,0},{3,1},{4,6},{5,7},{6,4},{7,5},{8,10},{9,11},{10,... | collective-permute-start | bytes 196616 | tf_op jit(solution)/shard_map/ppermute | solution.py:41
  31.7 4.7 %collective-permute-done.18 = bf16[32,1024]{1,0:T(8,128)(2,1)S(1)} collective-permute-done((bf16[32,1024]{1,0:T(8,128)(2,1)S(1)}, bf16[32,1024]{1,0:T(8,128)(2,1)S(1)}, u32[]{:S(2)}, u32[]{:S(2)}) %collective-permute-start.18) | collective-permute-done | bytes 65568 | tf_op jit(solution)/shard_map/ppermute | solution.py:41
  36.4 1.3 collective-permute-start.19
  39.2 1.7 collective-permute-start.5
  41.4 1.5 collective-permute-done.19
  42.9 1.5 collective-permute-start.20
  44.4 1.2 collective-permute-done.15
  45.7 1.5 collective-permute-start.16
  47.2 1.6 collective-permute-done.5
  48.9 1.5 collective-permute-start.6
  50.4 1.4 collective-permute-done.11
  51.9 1.5 collective-permute-start.12
  53.6 4.2 %collective-permute-done.16 = bf16[2,2,32,1024]{3,2,1,0:T(8,128)(2,1)S(1)} collective-permute-done((bf16[2,2,32,1024]{3,2,1,0:T(8,128)(2,1)S(1)}, bf16[2,2,32,1024]{3,2,1,0:T(8,128)(2,1)S(1)}, u32[]{:S(2)}, u32[]{:S(2)}) %collective-permute-start.16) | collective-permute-done | bytes 262176 | tf_op jit(solution)/shard_map/ppermute | solution.py:41
  58.8 5.2 %collective-permute-done.6 = bf16[2,2,32,1152]{3,2,1,0:T(8,128)(2,1)S(1)} collective-permute-done((bf16[2,2,32,1152]{3,2,1,0:T(8,128)(2,1)S(1)}, bf16[2,2,32,1152]{3,2,1,0:T(8,128)(2,1)S(1)}, u32[]{:S(2)}, u32[]{:S(2)}) %collective-permute-start.6) | collective-permute-done | bytes 294944 | tf_op jit(solution)/shard_map/ppermute | solution.py:41
  65.0 4.2 %collective-permute-done.12 = bf16[2,2,32,1152]{3,2,1,0:T(8,128)(2,1)S(1)} collective-permute-done((bf16[2,2,32,1152]{3,2,1,0:T(8,128)(2,1)S(1)}, bf16[2,2,32,1152]{3,2,1,0:T(8,128)(2,1)S(1)}, u32[]{:S(2)}, u32[]{:S(2)}) %collective-permute-start.12) | collective-permute-done | bytes 294944 | tf_op jit(solution)/shard_map/ppermute | solution.py:41
  72.1 1.3 pad_maximum_fusion.2
  73.4 1.2 pad_maximum_fusion
  75.8 1.2 pad_maximum_fusion.1
  79.7 1.2 copy-done
  80.9 7.1 %shard_map.163 = (f32[8,128,384]{2,1,0:T(8,128)S(1)}, f32[8,128,384]{2,1,0:T(8,128)S(1)}) custom-call(s32[1024]{0:T(1024)S(1)} %bitcast.99, bf16[512,1024]{1,0:T(8,128)(2,1)S(1)} %copy-done, bf16[8,4096,384]{2,1,0:T(8,128)(2,1)} %wg.7, bf16[8,4096,384]{2,1,0:T(8,128)(2,1)} %wu.7), custom_call_target="tpu_custom_call" | custom-call | flops 1610612736 | bytes 12582912 | tf_op jit(solution)/shard_map/pallas_call | solution.py:415
  89.2 11.0 %shard_map.164 = (f32[8,128,384]{2,1,0:T(8,128)S(1)}, f32[8,128,384]{2,1,0:T(8,128)S(1)}) custom-call(s32[1024]{0:T(1024)S(1)} %bitcast.100, bf16[512,1024]{1,0:T(8,128)(2,1)S(1)} %bitcast.94, bf16[8,4096,384]{2,1,0:T(8,128)(2,1)} %wg.7, bf16[8,4096,384]{2,1,0:T(8,128)(2,1)} %wu.7, f32[8,128,384]{2,1,0:T(8,128)S(1)} %get-tuple-element.37.rest_0_, ...), custom_call_target="tpu_custom_call" | custom-call | flops 1610612736 | bytes 12582912 | tf_op jit(solution)/shard_map/pallas_call | solution.py:415
  101.3 11.0 %shard_map.165 = (f32[8,128,384]{2,1,0:T(8,128)S(1)}, f32[8,128,384]{2,1,0:T(8,128)S(1)}) custom-call(s32[1024]{0:T(1024)S(1)} %bitcast.101, bf16[512,1024]{1,0:T(8,128)(2,1)S(1)} %bitcast.95, bf16[8,4096,384]{2,1,0:T(8,128)(2,1)} %wg.7, bf16[8,4096,384]{2,1,0:T(8,128)(2,1)} %wu.7, f32[8,128,384]{2,1,0:T(8,128)S(1)} %get-tuple-element.39.rest_0_, ...), custom_call_target="tpu_custom_call" | custom-call | flops 1610612736 | bytes 12582912 | tf_op jit(solution)/shard_map/pallas_call | solution.py:415
  113.5 11.5 %shard_map.166 = (bf16[8,128,384]{2,1,0:T(8,128)(2,1)S(1)}, bf16[512,1024]{1,0:T(8,128)(2,1)S(1)}) custom-call(s32[1024]{0:T(1024)S(1)} %bitcast.102, bf16[512,1024]{1,0:T(8,128)(2,1)S(1)} %slice.227.x, bf16[8,4096,384]{2,1,0:T(8,128)(2,1)} %wg.7, bf16[8,4096,384]{2,1,0:T(8,128)(2,1)} %wu.7, f32[8,128,384]{2,1,0:T(8,128)S(1)} %get-tuple-element.41.rest_0_, ...), custom_call_target="tpu_custom_call" | custom-call | flops 1610612736 | bytes 12582912 | tf_op jit(solution)/shard_map/pallas_call | solution.py:415
  125.0 4.8 %shard_map.168 = (f32[256,1024]{1,0:T(8,128)S(1)}, bf16[256,1024]{1,0:T(8,128)(2,1)S(1)}) custom-call(bf16[8,128,384]{2,1,0:T(8,128)(2,1)S(1)} %get-tuple-element.43.act, bf16[512,1024]{1,0:T(8,128)(2,1)S(1)} %get-tuple-element.44.comb, bf16[8,384,4096]{2,1,0:T(8,128)(2,1)} %wd.7), custom_call_target="tpu_custom_call" | custom-call | flops 1879048192 | bytes 6291456 | tf_op jit(solution)/shard_map/pallas_call | solution.py:464
  130.3 4.7 %shard_map.167 = (f32[256,1024]{1,0:T(8,128)S(1)}, bf16[256,1024]{1,0:T(8,128)(2,1)S(1)}) custom-call(bf16[8,128,384]{2,1,0:T(8,128)(2,1)S(1)} %get-tuple-element.43.act, bf16[512,1024]{1,0:T(8,128)(2,1)S(1)} %get-tuple-element.44.comb, bf16[8,384,4096]{2,1,0:T(8,128)(2,1)} %wd.7), custom_call_target="tpu_custom_call" | custom-call | flops 1879048192 | bytes 6291456 | tf_op jit(solution)/shard_map/pallas_call | solution.py:464
  135.2 4.8 %shard_map.170 = (f32[256,1024]{1,0:T(8,128)S(1)}, bf16[256,1024]{1,0:T(8,128)(2,1)S(1)}) custom-call(bf16[8,128,384]{2,1,0:T(8,128)(2,1)S(1)} %get-tuple-element.43.act, bf16[512,1024]{1,0:T(8,128)(2,1)S(1)} %get-tuple-element.44.comb, bf16[8,384,4096]{2,1,0:T(8,128)(2,1)} %wd.7), custom_call_target="tpu_custom_call" | custom-call | flops 1879048192 | bytes 6291456 | tf_op jit(solution)/shard_map/pallas_call | solution.py:464
  140.5 4.8 %shard_map.169 = (f32[256,1024]{1,0:T(8,128)S(1)}, bf16[256,1024]{1,0:T(8,128)(2,1)S(1)}) custom-call(bf16[8,128,384]{2,1,0:T(8,128)(2,1)S(1)} %get-tuple-element.43.act, bf16[512,1024]{1,0:T(8,128)(2,1)S(1)} %get-tuple-element.44.comb, bf16[8,384,4096]{2,1,0:T(8,128)(2,1)} %wd.7), custom_call_target="tpu_custom_call" | custom-call | flops 1879048192 | bytes 6291456 | tf_op jit(solution)/shard_map/pallas_call | solution.py:464
  145.6 1.5 collective-permute-start.27
  148.2 1.5 collective-permute-start.35
  150.5 4.3 %collective-permute-done.27 = bf16[128,1024]{1,0:T(8,128)(2,1)S(1)} collective-permute-done((bf16[128,1024]{1,0:T(8,128)(2,1)S(1)}, bf16[128,1024]{1,0:T(8,128)(2,1)S(1)}, u32[]{:S(2)}, u32[]{:S(2)}) %collective-permute-start.27) | collective-permute-done | bytes 262176 | tf_op jit(solution)/shard_map/ppermute | solution.py:41
  154.9 5.5 %collective-permute-done.23 = bf16[128,1024]{1,0:T(8,128)(2,1)S(1)} collective-permute-done((bf16[128,1024]{1,0:T(8,128)(2,1)S(1)}, bf16[128,1024]{1,0:T(8,128)(2,1)S(1)}, u32[]{:S(2)}, u32[]{:S(2)}) %collective-permute-start.23) | collective-permute-done | bytes 262176 | tf_op jit(solution)/shard_map/ppermute | solution.py:41
  160.6 5.5 %collective-permute-done.35 = bf16[128,1024]{1,0:T(8,128)(2,1)S(1)} collective-permute-done((bf16[128,1024]{1,0:T(8,128)(2,1)S(1)}, bf16[128,1024]{1,0:T(8,128)(2,1)S(1)}, u32[]{:S(2)}, u32[]{:S(2)}) %collective-permute-start.35) | collective-permute-done | bytes 262176 | tf_op jit(solution)/shard_map/ppermute | solution.py:41
  166.3 4.9 %collective-permute-done.31 = bf16[128,1024]{1,0:T(8,128)(2,1)S(1)} collective-permute-done((bf16[128,1024]{1,0:T(8,128)(2,1)S(1)}, bf16[128,1024]{1,0:T(8,128)(2,1)S(1)}, u32[]{:S(2)}, u32[]{:S(2)}) %collective-permute-start.31) | collective-permute-done | bytes 262176 | tf_op jit(solution)/shard_map/ppermute | solution.py:41
  171.4 2.0 %collective-permute-start.36 = (bf16[2,32,1024]{2,1,0:T(8,128)(2,1)S(1)}, bf16[2,32,1024]{2,1,0:T(8,128)(2,1)S(1)}, u32[]{:S(2)}, u32[]{:S(2)}) collective-permute-start(bf16[2,32,1024]{2,1,0:T(8,128)(2,1)S(1)} %bitcast.123), channel_id=1, source_target_pairs={{0,1},{1,0},{2,3},{3,2},{4,5},{5,4},{6,7},{7,6},{8,9},{9,8},{10,11... | collective-permute-start | bytes 393224 | tf_op jit(solution)/shard_map/ppermute | solution.py:41
  173.5 3.0 %collective-permute-start.29 = (bf16[1,32,1024]{2,1,0:T(8,128)(2,1)S(1)}, bf16[1,32,1024]{2,1,0:T(8,128)(2,1)S(1)}, u32[]{:S(2)}, u32[]{:S(2)}) collective-permute-start(bf16[1,32,1024]{2,1,0:T(8,128)(2,1)S(1)} %slice.327), channel_id=1, source_target_pairs={{0,2},{1,3},{2,0},{3,1},{4,6},{5,7},{6,4},{7,5},{8,10},{9,11},{10,... | collective-permute-start | bytes 196616 | tf_op jit(solution)/shard_map/ppermute | solution.py:41
  176.6 3.3 %collective-permute-done.24 = bf16[2,32,1024]{2,1,0:T(8,128)(2,1)S(1)} collective-permute-done((bf16[2,32,1024]{2,1,0:T(8,128)(2,1)S(1)}, bf16[2,32,1024]{2,1,0:T(8,128)(2,1)S(1)}, u32[]{:S(2)}, u32[]{:S(2)}) %collective-permute-start.24) | collective-permute-done | bytes 131104 | tf_op jit(solution)/shard_map/ppermute | solution.py:41
  180.0 2.7 %collective-permute-done.36 = bf16[2,32,1024]{2,1,0:T(8,128)(2,1)S(1)} collective-permute-done((bf16[2,32,1024]{2,1,0:T(8,128)(2,1)S(1)}, bf16[2,32,1024]{2,1,0:T(8,128)(2,1)S(1)}, u32[]{:S(2)}, u32[]{:S(2)}) %collective-permute-start.36) | collective-permute-done | bytes 131104 | tf_op jit(solution)/shard_map/ppermute | solution.py:41
  184.3 1.5 collective-permute-start.33
  185.8 3.3 %collective-permute-done.25 = bf16[1,32,1024]{2,1,0:T(8,128)(2,1)S(1)} collective-permute-done((bf16[1,32,1024]{2,1,0:T(8,128)(2,1)S(1)}, bf16[1,32,1024]{2,1,0:T(8,128)(2,1)S(1)}, u32[]{:S(2)}, u32[]{:S(2)}) %collective-permute-start.25) | collective-permute-done | bytes 65568 | tf_op jit(solution)/shard_map/ppermute | solution.py:41
  189.2 1.9 collective-permute-done.37
  (139 shorter events, 27.0 us)
Async XLA Ops:
  0.7 1.3 collective-permute-start
  2.1 5.3 %collective-permute-start.1 = (bf16[2,32,256]{2,1,0:T(8,128)(2,1)S(1)}, bf16[2,32,256]{2,1,0:T(8,128)(2,1)S(1)}, u32[]{:S(2)}, u32[]{:S(2)}) collective-permute-start(bf16[2,32,256]{2,1,0:T(8,128)(2,1)S(1)} %get-tuple-element.92), channel_id=1, source_target_pairs={{0,8},{1,9},{2,10},{3,11},{4,12},{5,13},{6,14},{7,15},{8,0},{9,1},... | collective-permute-start | bytes 98312 | tf_op jit(solution)/shard_map/ppermute | solution.py:41
  13.2 3.2 %collective-permute-start.2 = (bf16[64,2048]{1,0:T(8,128)(2,1)S(1)}, bf16[64,2048]{1,0:T(8,128)(2,1)S(1)}, u32[]{:S(2)}, u32[]{:S(2)}) collective-permute-start(bf16[64,2048]{1,0:T(8,128)(2,1)S(1)} %get-tuple-element.32), channel_id=1, source_target_pairs={{0,4},{1,5},{2,6},{3,7},{4,0},{5,1},{6,2},{7,3},{8,12},{9,13},{10,... | collective-permute-start | bytes 786440 | tf_op jit(solution)/shard_map/ppermute | solution.py:41
  15.8 2.2 %collective-permute-start.8 = (bf16[64,2048]{1,0:T(8,128)(2,1)S(1)}, bf16[64,2048]{1,0:T(8,128)(2,1)S(1)}, u32[]{:S(2)}, u32[]{:S(2)}) collective-permute-start(bf16[64,2048]{1,0:T(8,128)(2,1)S(1)} %get-tuple-element.36), channel_id=1, source_target_pairs={{0,4},{1,5},{2,6},{3,7},{4,0},{5,1},{6,2},{7,3},{8,12},{9,13},{10,... | collective-permute-start | bytes 786440 | tf_op jit(solution)/shard_map/ppermute | solution.py:41
  16.4 2.8 %copy-start.6 = (f32[4096]{0:T(1024)S(1)}, f32[4096]{0:T(1024)}, u32[]{:S(2)}) copy-start(f32[4096]{0:T(1024)} %param.28) | copy-start | bytes 49156
  16.4 8.4 %copy-start.12 = (bf16[4,8,4096]{2,1,0:T(8,128)(2,1)S(1)}, bf16[4,8,4096]{2,1,0:T(8,128)(2,1)}, u32[]{:S(2)}) copy-start(bf16[4,8,4096]{2,1,0:T(8,128)(2,1)} %param.27) | copy-start | bytes 786436
  16.5 6.4 %collective-permute-start.3 = (bf16[32,2048]{1,0:T(8,128)(2,1)S(1)}, bf16[32,2048]{1,0:T(8,128)(2,1)S(1)}, u32[]{:S(2)}, u32[]{:S(2)}) collective-permute-start(bf16[32,2048]{1,0:T(8,128)(2,1)S(1)} %slice.324), channel_id=1, source_target_pairs={{0,8},{1,9},{2,10},{3,11},{4,12},{5,13},{6,14},{7,15},{8,0},{9,1},... | collective-permute-start | bytes 393224 | tf_op jit(solution)/shard_map/ppermute | solution.py:41
  18.1 12.6 %copy-start.5 = (bf16[4096,64]{0,1:T(8,128)(2,1)S(1)}, bf16[4096,64]{0,1:T(8,128)(2,1)}, u32[]{:S(2)}) copy-start(bf16[4096,64]{0,1:T(8,128)(2,1)} %param.29) | copy-start | bytes 1572868
  18.1 6.7 %collective-permute-start.9 = (bf16[32,2048]{1,0:T(8,128)(2,1)S(1)}, bf16[32,2048]{1,0:T(8,128)(2,1)S(1)}, u32[]{:S(2)}, u32[]{:S(2)}) collective-permute-start(bf16[32,2048]{1,0:T(8,128)(2,1)S(1)} %slice.323), channel_id=1, source_target_pairs={{0,8},{1,9},{2,10},{3,11},{4,12},{5,13},{6,14},{7,15},{8,0},{9,1},... | collective-permute-start | bytes 393224 | tf_op jit(solution)/shard_map/ppermute | solution.py:41
  24.9 13.7 %copy-start.7 = (bf16[32,2048]{1,0:T(8,128)(2,1)}, bf16[32,2048]{1,0:T(8,128)(2,1)S(1)}, u32[]{:S(2)}) copy-start(bf16[32,2048]{1,0:T(8,128)(2,1)S(1)} %get-tuple-element.70) | copy-start | bytes 393220
  25.0 14.2 %collective-permute-start.4 = (bf16[32,1152]{1,0:T(8,128)(2,1)S(1)}, bf16[32,1152]{1,0:T(8,128)(2,1)S(1)}, u32[]{:S(2)}, u32[]{:S(2)}) collective-permute-start(bf16[32,1152]{1,0:T(8,128)(2,1)S(1)} %get-tuple-element.90), channel_id=1, source_target_pairs={{0,2},{1,3},{2,0},{3,1},{4,6},{5,7},{6,4},{7,5},{8,10},{9,11},{10,... | collective-permute-start | bytes 221192 | tf_op jit(solution)/shard_map/ppermute | solution.py:41
  27.6 8.8 %collective-permute-start.18 = (bf16[32,1024]{1,0:T(8,128)(2,1)S(1)}, bf16[32,1024]{1,0:T(8,128)(2,1)S(1)}, u32[]{:S(2)}, u32[]{:S(2)}) collective-permute-start(bf16[32,1024]{1,0:T(8,128)(2,1)S(1)} %get-tuple-element.81), channel_id=1, source_target_pairs={{0,2},{1,3},{2,0},{3,1},{4,6},{5,7},{6,4},{7,5},{8,10},{9,11},{10,... | collective-permute-start | bytes 196616 | tf_op jit(solution)/shard_map/ppermute | solution.py:41
  28.0 10.6 %collective-permute-start.14 = (bf16[32,1024]{1,0:T(8,128)(2,1)S(1)}, bf16[32,1024]{1,0:T(8,128)(2,1)S(1)}, u32[]{:S(2)}, u32[]{:S(2)}) collective-permute-start(bf16[32,1024]{1,0:T(8,128)(2,1)S(1)} %get-tuple-element.85), channel_id=1, source_target_pairs={{0,2},{1,3},{2,0},{3,1},{4,6},{5,7},{6,4},{7,5},{8,10},{9,11},{10,... | collective-permute-start | bytes 196616 | tf_op jit(solution)/shard_map/ppermute | solution.py:41
  31.3 9.6 %collective-permute-start.10 = (bf16[32,1152]{1,0:T(8,128)(2,1)S(1)}, bf16[32,1152]{1,0:T(8,128)(2,1)S(1)}, u32[]{:S(2)}, u32[]{:S(2)}) collective-permute-start(bf16[32,1152]{1,0:T(8,128)(2,1)S(1)} %get-tuple-element.88), channel_id=1, source_target_pairs={{0,2},{1,3},{2,0},{3,1},{4,6},{5,7},{6,4},{7,5},{8,10},{9,11},{10,... | collective-permute-start | bytes 221192 | tf_op jit(solution)/shard_map/ppermute | solution.py:41
  36.4 6.4 %collective-permute-start.19 = (bf16[2,32,1024]{2,1,0:T(8,128)(2,1)S(1)}, bf16[2,32,1024]{2,1,0:T(8,128)(2,1)S(1)}, u32[]{:S(2)}, u32[]{:S(2)}) collective-permute-start(bf16[2,32,1024]{2,1,0:T(8,128)(2,1)S(1)} %get-tuple-element.80), channel_id=1, source_target_pairs={{0,1},{1,0},{2,3},{3,2},{4,5},{5,4},{6,7},{7,6},{8,9},{9,8},{10,11... | collective-permute-start | bytes 393224 | tf_op jit(solution)/shard_map/ppermute | solution.py:41
  38.6 7.0 %collective-permute-start.15 = (bf16[2,32,1024]{2,1,0:T(8,128)(2,1)S(1)}, bf16[2,32,1024]{2,1,0:T(8,128)(2,1)S(1)}, u32[]{:S(2)}, u32[]{:S(2)}) collective-permute-start(bf16[2,32,1024]{2,1,0:T(8,128)(2,1)S(1)} %get-tuple-element.84), channel_id=1, source_target_pairs={{0,1},{1,0},{2,3},{3,2},{4,5},{5,4},{6,7},{7,6},{8,9},{9,8},{10,11... | collective-permute-start | bytes 393224 | tf_op jit(solution)/shard_map/ppermute | solution.py:41
  39.2 9.7 %collective-permute-start.5 = (bf16[2,32,1152]{2,1,0:T(8,128)(2,1)S(1)}, bf16[2,32,1152]{2,1,0:T(8,128)(2,1)S(1)}, u32[]{:S(2)}, u32[]{:S(2)}) collective-permute-start(bf16[2,32,1152]{2,1,0:T(8,128)(2,1)S(1)} %get-tuple-element.74), channel_id=1, source_target_pairs={{0,1},{1,0},{2,3},{3,2},{4,5},{5,4},{6,7},{7,6},{8,9},{9,8},{10,11... | collective-permute-start | bytes 442376 | tf_op jit(solution)/shard_map/ppermute | solution.py:41
  40.9 11.0 %collective-permute-start.11 = (bf16[2,32,1152]{2,1,0:T(8,128)(2,1)S(1)}, bf16[2,32,1152]{2,1,0:T(8,128)(2,1)S(1)}, u32[]{:S(2)}, u32[]{:S(2)}) collective-permute-start(bf16[2,32,1152]{2,1,0:T(8,128)(2,1)S(1)} %get-tuple-element.72), channel_id=1, source_target_pairs={{0,1},{1,0},{2,3},{3,2},{4,5},{5,4},{6,7},{7,6},{8,9},{9,8},{10,11... | collective-permute-start | bytes 442376 | tf_op jit(solution)/shard_map/ppermute | solution.py:41
  42.9 10.5 %collective-permute-start.20 = (bf16[2,2,32,1024]{3,2,1,0:T(8,128)(2,1)S(1)}, bf16[2,2,32,1024]{3,2,1,0:T(8,128)(2,1)S(1)}, u32[]{:S(2)}, u32[]{:S(2)}) collective-permute-start(bf16[2,2,32,1024]{3,2,1,0:T(8,128)(2,1)S(1)} %get-tuple-element.66), channel_id=1, source_target_pairs={{0,8},{1,9},{2,10},{3,11},{4,12},{5,13},{6,14},{7,15},{8,0},{9,1},... | collective-permute-start | bytes 786440 | tf_op jit(solution)/shard_map/ppermute | solution.py:41
  45.7 12.1 %collective-permute-start.16 = (bf16[2,2,32,1024]{3,2,1,0:T(8,128)(2,1)S(1)}, bf16[2,2,32,1024]{3,2,1,0:T(8,128)(2,1)S(1)}, u32[]{:S(2)}, u32[]{:S(2)}) collective-permute-start(bf16[2,2,32,1024]{3,2,1,0:T(8,128)(2,1)S(1)} %get-tuple-element.68), channel_id=1, source_target_pairs={{0,8},{1,9},{2,10},{3,11},{4,12},{5,13},{6,14},{7,15},{8,0},{9,1},... | collective-permute-start | bytes 786440 | tf_op jit(solution)/shard_map/ppermute | solution.py:41
  48.9 15.2 %collective-permute-start.6 = (bf16[2,2,32,1152]{3,2,1,0:T(8,128)(2,1)S(1)}, bf16[2,2,32,1152]{3,2,1,0:T(8,128)(2,1)S(1)}, u32[]{:S(2)}, u32[]{:S(2)}) collective-permute-start(bf16[2,2,32,1152]{3,2,1,0:T(8,128)(2,1)S(1)} %get-tuple-element.64), channel_id=1, source_target_pairs={{0,8},{1,9},{2,10},{3,11},{4,12},{5,13},{6,14},{7,15},{8,0},{9,1},... | collective-permute-start | bytes 884744 | tf_op jit(solution)/shard_map/ppermute | solution.py:41
  51.9 17.3 %collective-permute-start.12 = (bf16[2,2,32,1152]{3,2,1,0:T(8,128)(2,1)S(1)}, bf16[2,2,32,1152]{3,2,1,0:T(8,128)(2,1)S(1)}, u32[]{:S(2)}, u32[]{:S(2)}) collective-permute-start(bf16[2,2,32,1152]{3,2,1,0:T(8,128)(2,1)S(1)} %get-tuple-element.62), channel_id=1, source_target_pairs={{0,8},{1,9},{2,10},{3,11},{4,12},{5,13},{6,14},{7,15},{8,0},{9,1},... | collective-permute-start | bytes 884744 | tf_op jit(solution)/shard_map/ppermute | solution.py:41
  53.5 16.6 %collective-permute-start.21 = (bf16[2,2,2,32,1024]{4,3,2,1,0:T(8,128)(2,1)S(1)}, bf16[2,2,2,32,1024]{4,3,2,1,0:T(8,128)(2,1)S(1)}, u32[]{:S(2)}, u32[]{:S(2)}) collective-permute-start(bf16[2,2,2,32,1024]{4,3,2,1,0:T(8,128)(2,1)S(1)} %get-tuple-element.58), channel_id=1, source_target_pairs={{0,4},{1,5},{2,6},{3,7},{4,0},{5,1},{6,2},{7,3},{8,12},{9,13},{10,... | collective-permute-start | bytes 1572872 | tf_op jit(solution)/shard_map/ppermute | solution.py:41
  58.8 13.3 %collective-permute-start.17 = (bf16[2,2,2,32,1024]{4,3,2,1,0:T(8,128)(2,1)}, bf16[2,2,2,32,1024]{4,3,2,1,0:T(8,128)(2,1)}, u32[]{:S(2)}, u32[]{:S(2)}) collective-permute-start(bf16[2,2,2,32,1024]{4,3,2,1,0:T(8,128)(2,1)} %get-tuple-element.60), channel_id=1, source_target_pairs={{0,4},{1,5},{2,6},{3,7},{4,0},{5,1},{6,2},{7,3},{8,12},{9,13},{10,... | collective-permute-start | bytes 1572872 | tf_op jit(solution)/shard_map/ppermute | solution.py:41
  65.0 8.4 %collective-permute-start.7 = (bf16[2,2,2,32,1152]{4,3,2,1,0:T(8,128)(2,1)}, bf16[2,2,2,32,1152]{4,3,2,1,0:T(8,128)(2,1)}, u32[]{:S(2)}, u32[]{:S(2)}) collective-permute-start(bf16[2,2,2,32,1152]{4,3,2,1,0:T(8,128)(2,1)} %get-tuple-element.56), channel_id=1, source_target_pairs={{0,4},{1,5},{2,6},{3,7},{4,0},{5,1},{6,2},{7,3},{8,12},{9,13},{10,... | collective-permute-start | bytes 1769480 | tf_op jit(solution)/shard_map/ppermute | solution.py:41
  70.1 5.6 %collective-permute-start.13 = (bf16[2,2,2,32,1152]{4,3,2,1,0:T(8,128)(2,1)}, bf16[2,2,2,32,1152]{4,3,2,1,0:T(8,128)(2,1)}, u32[]{:S(2)}, u32[]{:S(2)}) collective-permute-start(bf16[2,2,2,32,1152]{4,3,2,1,0:T(8,128)(2,1)} %get-tuple-element.54), channel_id=1, source_target_pairs={{0,4},{1,5},{2,6},{3,7},{4,0},{5,1},{6,2},{7,3},{8,12},{9,13},{10,... | collective-permute-start | bytes 1769480 | tf_op jit(solution)/shard_map/ppermute | solution.py:41
  101.3 12.1 %copy-start.4 = (s32[512,8]{1,0:T(8,128)S(1)}, s32[512,8]{1,0:T(8,128)}, u32[]{:S(2)}) copy-start(s32[512,8]{1,0:T(8,128)} %fusion.rest_3_) | copy-start | bytes 49156
  129.7 15.7 %collective-permute-start.26 = (bf16[256,1024]{1,0:T(8,128)(2,1)S(1)}, bf16[256,1024]{1,0:T(8,128)(2,1)S(1)}, u32[]{:S(2)}, u32[]{:S(2)}) collective-permute-start(bf16[256,1024]{1,0:T(8,128)(2,1)S(1)} %get-tuple-element.48), channel_id=1, source_target_pairs={{0,4},{1,5},{2,6},{3,7},{4,0},{5,1},{6,2},{7,3},{8,12},{9,13},{10,... | collective-permute-start | bytes 1572872 | tf_op jit(solution)/shard_map/ppermute | solution.py:41
  135.1 12.0 %collective-permute-start.22 = (bf16[256,1024]{1,0:T(8,128)(2,1)S(1)}, bf16[256,1024]{1,0:T(8,128)(2,1)S(1)}, u32[]{:S(2)}, u32[]{:S(2)}) collective-permute-start(bf16[256,1024]{1,0:T(8,128)(2,1)S(1)} %get-tuple-element.46), channel_id=1, source_target_pairs={{0,4},{1,5},{2,6},{3,7},{4,0},{5,1},{6,2},{7,3},{8,12},{9,13},{10,... | collective-permute-start | bytes 1572872 | tf_op jit(solution)/shard_map/ppermute | solution.py:41
  140.0 8.0 %collective-permute-start.34 = (bf16[256,1024]{1,0:T(8,128)(2,1)S(1)}, bf16[256,1024]{1,0:T(8,128)(2,1)S(1)}, u32[]{:S(2)}, u32[]{:S(2)}) collective-permute-start(bf16[256,1024]{1,0:T(8,128)(2,1)S(1)} %get-tuple-element.52), channel_id=1, source_target_pairs={{0,4},{1,5},{2,6},{3,7},{4,0},{5,1},{6,2},{7,3},{8,12},{9,13},{10,... | collective-permute-start | bytes 1572872 | tf_op jit(solution)/shard_map/ppermute | solution.py:41
  145.3 4.4 %collective-permute-start.30 = (bf16[256,1024]{1,0:T(8,128)(2,1)S(1)}, bf16[256,1024]{1,0:T(8,128)(2,1)S(1)}, u32[]{:S(2)}, u32[]{:S(2)}) collective-permute-start(bf16[256,1024]{1,0:T(8,128)(2,1)S(1)} %get-tuple-element.50), channel_id=1, source_target_pairs={{0,4},{1,5},{2,6},{3,7},{4,0},{5,1},{6,2},{7,3},{8,12},{9,13},{10,... | collective-permute-start | bytes 1572872 | tf_op jit(solution)/shard_map/ppermute | solution.py:41
  145.6 9.2 %collective-permute-start.27 = (bf16[128,1024]{1,0:T(8,128)(2,1)S(1)}, bf16[128,1024]{1,0:T(8,128)(2,1)S(1)}, u32[]{:S(2)}, u32[]{:S(2)}) collective-permute-start(bf16[128,1024]{1,0:T(8,128)(2,1)S(1)} %slice.317), channel_id=1, source_target_pairs={{0,8},{1,9},{2,10},{3,11},{4,12},{5,13},{6,14},{7,15},{8,0},{9,1},... | collective-permute-start | bytes 786440 | tf_op jit(solution)/shard_map/ppermute | solution.py:41
  147.4 13.1 %collective-permute-start.23 = (bf16[128,1024]{1,0:T(8,128)(2,1)S(1)}, bf16[128,1024]{1,0:T(8,128)(2,1)S(1)}, u32[]{:S(2)}, u32[]{:S(2)}) collective-permute-start(bf16[128,1024]{1,0:T(8,128)(2,1)S(1)} %slice.318), channel_id=1, source_target_pairs={{0,8},{1,9},{2,10},{3,11},{4,12},{5,13},{6,14},{7,15},{8,0},{9,1},... | collective-permute-start | bytes 786440 | tf_op jit(solution)/shard_map/ppermute | solution.py:41
  148.2 17.9 %collective-permute-start.35 = (bf16[128,1024]{1,0:T(8,128)(2,1)S(1)}, bf16[128,1024]{1,0:T(8,128)(2,1)S(1)}, u32[]{:S(2)}, u32[]{:S(2)}) collective-permute-start(bf16[128,1024]{1,0:T(8,128)(2,1)S(1)} %slice.315), channel_id=1, source_target_pairs={{0,8},{1,9},{2,10},{3,11},{4,12},{5,13},{6,14},{7,15},{8,0},{9,1},... | collective-permute-start | bytes 786440 | tf_op jit(solution)/shard_map/ppermute | solution.py:41
  149.9 21.3 %collective-permute-start.31 = (bf16[128,1024]{1,0:T(8,128)(2,1)S(1)}, bf16[128,1024]{1,0:T(8,128)(2,1)S(1)}, u32[]{:S(2)}, u32[]{:S(2)}) collective-permute-start(bf16[128,1024]{1,0:T(8,128)(2,1)S(1)} %slice.316), channel_id=1, source_target_pairs={{0,8},{1,9},{2,10},{3,11},{4,12},{5,13},{6,14},{7,15},{8,0},{9,1},... | collective-permute-start | bytes 786440 | tf_op jit(solution)/shard_map/ppermute | solution.py:41
  154.9 11.2 %copy-start.9 = (f32[128,1024]{1,0:T(8,128)}, f32[128,1024]{1,0:T(8,128)S(1)}, u32[]{:S(2)}) copy-start(f32[128,1024]{1,0:T(8,128)S(1)} %slice_add_fusion.2) | copy-start | bytes 1572868
  160.5 5.7 %copy-start.10 = (f32[128,1024]{1,0:T(8,128)}, f32[128,1024]{1,0:T(8,128)S(1)}, u32[]{:S(2)}) copy-start(f32[128,1024]{1,0:T(8,128)S(1)} %slice_add_fusion.3) | copy-start | bytes 1572868
  166.2 7.3 %slice-start = ((f32[128,1024]{1,0:T(8,128)}), f32[64,1024]{1,0:T(8,128)S(1)}, s32[]{:S(2)}) async-start(f32[128,1024]{1,0:T(8,128)} %copy-done.9), calls=%async_computation | async-start | bytes 524288 | tf_op jit(solution)/shard_map/slice | solution.py:64
  166.2 13.6 %slice-start.1 = ((f32[128,1024]{1,0:T(8,128)}), f32[64,1024]{1,0:T(8,128)S(1)}, s32[]{:S(2)}) async-start(f32[128,1024]{1,0:T(8,128)} %copy-done.10), calls=%async_computation.1 | async-start | bytes 524288 | tf_op jit(solution)/shard_map/slice | solution.py:64
  166.2 7.3 %collective-permute-start.28 = (bf16[2,32,1024]{2,1,0:T(8,128)(2,1)S(1)}, bf16[2,32,1024]{2,1,0:T(8,128)(2,1)S(1)}, u32[]{:S(2)}, u32[]{:S(2)}) collective-permute-start(bf16[2,32,1024]{2,1,0:T(8,128)(2,1)S(1)} %bitcast.126), channel_id=1, source_target_pairs={{0,1},{1,0},{2,3},{3,2},{4,5},{5,4},{6,7},{7,6},{8,9},{9,8},{10,11... | collective-permute-start | bytes 393224 | tf_op jit(solution)/shard_map/ppermute | solution.py:41
  171.3 8.5 %collective-permute-start.24 = (bf16[2,32,1024]{2,1,0:T(8,128)(2,1)S(1)}, bf16[2,32,1024]{2,1,0:T(8,128)(2,1)S(1)}, u32[]{:S(2)}, u32[]{:S(2)}) collective-permute-start(bf16[2,32,1024]{2,1,0:T(8,128)(2,1)S(1)} %bitcast.124), channel_id=1, source_target_pairs={{0,1},{1,0},{2,3},{3,2},{4,5},{5,4},{6,7},{7,6},{8,9},{9,8},{10,11... | collective-permute-start | bytes 393224 | tf_op jit(solution)/shard_map/ppermute | solution.py:41
  171.4 11.3 %collective-permute-start.36 = (bf16[2,32,1024]{2,1,0:T(8,128)(2,1)S(1)}, bf16[2,32,1024]{2,1,0:T(8,128)(2,1)S(1)}, u32[]{:S(2)}, u32[]{:S(2)}) collective-permute-start(bf16[2,32,1024]{2,1,0:T(8,128)(2,1)S(1)} %bitcast.123), channel_id=1, source_target_pairs={{0,1},{1,0},{2,3},{3,2},{4,5},{5,4},{6,7},{7,6},{8,9},{9,8},{10,11... | collective-permute-start | bytes 393224 | tf_op jit(solution)/shard_map/ppermute | solution.py:41
  173.4 10.9 %collective-permute-start.32 = (bf16[2,32,1024]{2,1,0:T(8,128)(2,1)S(1)}, bf16[2,32,1024]{2,1,0:T(8,128)(2,1)S(1)}, u32[]{:S(2)}, u32[]{:S(2)}) collective-permute-start(bf16[2,32,1024]{2,1,0:T(8,128)(2,1)S(1)} %bitcast.125), channel_id=1, source_target_pairs={{0,1},{1,0},{2,3},{3,2},{4,5},{5,4},{6,7},{7,6},{8,9},{9,8},{10,11... | collective-permute-start | bytes 393224 | tf_op jit(solution)/shard_map/ppermute | solution.py:41
  173.5 15.7 %copy-start.8 = (bf16[32,2048]{1,0:T(8,128)(2,1)S(1)}, bf16[32,2048]{1,0:T(8,128)(2,1)}, u32[]{:S(2)}) copy-start(bf16[32,2048]{1,0:T(8,128)(2,1)} %copy-done.7) | copy-start | bytes 393220
  173.5 12.3 %collective-permute-start.29 = (bf16[1,32,1024]{2,1,0:T(8,128)(2,1)S(1)}, bf16[1,32,1024]{2,1,0:T(8,128)(2,1)S(1)}, u32[]{:S(2)}, u32[]{:S(2)}) collective-permute-start(bf16[1,32,1024]{2,1,0:T(8,128)(2,1)S(1)} %slice.327), channel_id=1, source_target_pairs={{0,2},{1,3},{2,0},{3,1},{4,6},{5,7},{6,4},{7,5},{8,10},{9,11},{10,... | collective-permute-start | bytes 196616 | tf_op jit(solution)/shard_map/ppermute | solution.py:41
  179.9 9.3 %collective-permute-start.25 = (bf16[1,32,1024]{2,1,0:T(8,128)(2,1)S(1)}, bf16[1,32,1024]{2,1,0:T(8,128)(2,1)S(1)}, u32[]{:S(2)}, u32[]{:S(2)}) collective-permute-start(bf16[1,32,1024]{2,1,0:T(8,128)(2,1)S(1)} %slice.328), channel_id=1, source_target_pairs={{0,2},{1,3},{2,0},{3,1},{4,6},{5,7},{6,4},{7,5},{8,10},{9,11},{10,... | collective-permute-start | bytes 196616 | tf_op jit(solution)/shard_map/ppermute | solution.py:41
  182.7 8.4 %collective-permute-start.37 = (bf16[1,32,1024]{2,1,0:T(8,128)(2,1)S(1)}, bf16[1,32,1024]{2,1,0:T(8,128)(2,1)S(1)}, u32[]{:S(2)}, u32[]{:S(2)}) collective-permute-start(bf16[1,32,1024]{2,1,0:T(8,128)(2,1)S(1)} %slice.325), channel_id=1, source_target_pairs={{0,2},{1,3},{2,0},{3,1},{4,6},{5,7},{6,4},{7,5},{8,10},{9,11},{10,... | collective-permute-start | bytes 196616 | tf_op jit(solution)/shard_map/ppermute | solution.py:41
  184.3 7.5 %collective-permute-start.33 = (bf16[1,32,1024]{2,1,0:T(8,128)(2,1)S(1)}, bf16[1,32,1024]{2,1,0:T(8,128)(2,1)S(1)}, u32[]{:S(2)}, u32[]{:S(2)}) collective-permute-start(bf16[1,32,1024]{2,1,0:T(8,128)(2,1)S(1)} %slice.326), channel_id=1, source_target_pairs={{0,2},{1,3},{2,0},{3,1},{4,6},{5,7},{6,4},{7,5},{8,10},{9,11},{10,... | collective-permute-start | bytes 196616 | tf_op jit(solution)/shard_map/ppermute | solution.py:41
  (5 other events, 5.5 us)

commit v2 on v1

--- a/solution.py
+++ b/solution.py
@@ -281,7 +281,7 @@
             jax.ShapeDtypeStruct((rows - near_rows, span), BF),
             jax.ShapeDtypeStruct((rows, columns), BF),
         ),
-        compiler_params=pltpu.CompilerParams(vmem_limit_bytes=32 << 20),
+        compiler_params=pltpu.CompilerParams(vmem_limit_bytes=16 << 20),
         cost_estimate=pl.CostEstimate(
             flops=2 * rows * columns * span, transcendentals=0, bytes_accessed=2 * columns * span
         ),
@@ -308,7 +308,7 @@
             jax.ShapeDtypeStruct((count - near_rows, span), BF),
         ),
         scratch_shapes=weight_scratch(columns, span),
-        compiler_params=pltpu.CompilerParams(vmem_limit_bytes=16 << 20),
+        compiler_params=pltpu.CompilerParams(vmem_limit_bytes=10 << 20),
         cost_estimate=pl.CostEstimate(
             flops=2 * count * columns * span, transcendentals=0, bytes_accessed=2 * columns * span
         ),
@@ -316,18 +316,18 @@
     )(rows, *in_hbm(out_proj))
 
 
-def up_body(first, last, begin, token_at, x, wg, wu, *rest):
+def up_body(first, last, begin, pieces, width, token_at, *rest):
     rest = list(rest)
+    xs = [rest.pop(0) for _ in range(pieces)]
+    wg, wu = rest.pop(0), rest.pop(0)
     if not first:
         gin, uin = rest.pop(0), rest.pop(0)
     if last:
         extra, spot, share = rest.pop(0), rest.pop(0), rest.pop(0)
-    if last:
         act_out, comb_out, spread, picked, gates_held, ups_held, arrived, scales = rest
     else:
         gout, uout, spread, picked, gates_held, ups_held, arrived = rest
-    q = pl.program_id(0)
-    tokens, width = x.shape
+    held = gates_held.shape[0]
     tall = width // LANES
     slots = picked.shape[0] // tall
 
@@ -338,58 +338,66 @@
             pltpu.make_async_copy(wu.at[e, cut], ups_held.at[e], arrived.at[1, e]),
         )
 
-    @pl.when(q == 0)
-    def _():
-        for e in range(gates_held.shape[0]):
-            for copy in copies(e):
-                copy.start()
+    for e in range(held):
+        for copy in copies(e):
+            copy.start()
+    done = 0
+    for x in xs:
+        tokens = x.shape[0]
         for i in range(tall):
-            spread[pl.ds(i, tokens, stride=tall), :] = x[:, i * LANES : (i + 1) * LANES].astype(F32)
-
-    for c in range(0, slots, BATCH):
-        at = [token_at[q * slots + c + i] for i in range(BATCH)]
-        got = [spread[pl.ds(pl.multiple_of(t * tall, tall), tall)] for t in at]
-        picked[c * tall : (c + BATCH) * tall] = jnp.concatenate(got, axis=0)
-        if last:
-            got = [extra[pl.ds(t, 1)] for t in at]
-            for i in range(BATCH):
-                scales[c + i : c + i + 1] = got[i]
-    rows = jnp.concatenate(
-        [picked[pl.ds(i, slots, stride=tall), :].astype(BF) for i in range(tall)], axis=1
-    )
-    for copy in copies(q):
-        copy.wait()
-    gated = jnp.dot(rows, gates_held[q], preferred_element_type=F32)
-    lifted = jnp.dot(rows, ups_held[q], preferred_element_type=F32)
-    if not first:
-        gated = gated + gin[0]
-        lifted = lifted + uin[0]
-    if not last:
-        gout[0] = gated
-        uout[0] = lifted
-        return
-    scale = scales[:, 0:1] + scales[:, 1:2] + scales[:, 2:3]
-    gated = gated * scale
-    lifted = lifted * scale
-    act_out[0] = (gated / (1.0 + jnp.exp(-gated)) * lifted).astype(BF)
-    lane = lax.broadcasted_iota(jnp.int32, (tokens, slots), 1)
-    column = lax.broadcasted_iota(jnp.int32, spot.shape, 1)
-    own_spot = jnp.sum(jnp.where(column == q, spot[...], 0), axis=1, keepdims=True)
-    own_share = jnp.sum(jnp.where(column == q, share[...], 0.0), axis=1, keepdims=True)
-    comb_out[...] = jnp.where(lane == own_spot, own_share, 0.0).astype(BF)
-
-
-def expert_up(k, chunks, token_at, x, gate_proj, up_proj, sums, extras):
+            spread[pl.ds(done * tall + i, tokens, stride=tall), :] = x[
+                :, i * LANES : (i + 1) * LANES
+            ].astype(F32)
+        done += tokens
+
+    def visit(q, carry):
+        for c in range(0, slots, BATCH):
+            at = [token_at[q * slots + c + i] for i in range(BATCH)]
+            got = [spread[pl.ds(pl.multiple_of(t * tall, tall), tall)] for t in at]
+            picked[c * tall : (c + BATCH) * tall] = jnp.concatenate(got, axis=0)
+            if last:
+                got = [extra[pl.ds(t, 1)] for t in at]
+                for i in range(BATCH):
+                    scales[c + i : c + i + 1] = got[i]
+        rows = jnp.concatenate(
+            [picked[pl.ds(i, slots, stride=tall), :].astype(BF) for i in range(tall)], axis=1
+        )
+        for copy in copies(q):
+            copy.wait()
+        gated = jnp.dot(rows, gates_held[q], preferred_element_type=F32)
+        lifted = jnp.dot(rows, ups_held[q], preferred_element_type=F32)
+        if not first:
+            gated = gated + gin[q]
+            lifted = lifted + uin[q]
+        if not last:
+            gout[q] = gated
+            uout[q] = lifted
+            return carry
+        scale = scales[:, 0:1] + scales[:, 1:2] + scales[:, 2:3]
+        gated = gated * scale
+        lifted = lifted * scale
+        act_out[q] = (gated / (1.0 + jnp.exp(-gated)) * lifted).astype(BF)
+        lane = lax.broadcasted_iota(jnp.int32, (done, slots), 1)
+        column = lax.broadcasted_iota(jnp.int32, spot.shape, 1)
+        own_spot = jnp.sum(jnp.where(column == q, spot[...], 0), axis=1, keepdims=True)
+        own_share = jnp.sum(jnp.where(column == q, share[...], 0.0), axis=1, keepdims=True)
+        comb_out[q] = jnp.where(lane == own_spot, own_share, 0.0).astype(BF)
+        return carry
+
+    lax.fori_loop(0, held, visit, 0)
+
+
+def expert_up(k, chunks, token_at, xs, gate_proj, up_proj, sums, extras):
     held = gate_proj.shape[0]
-    tokens, width = x.shape
+    width = gate_proj.shape[1] // chunks
+    tokens = sum(x.shape[0] for x in xs)
     slots = token_at.shape[0] // held
     units = gate_proj.shape[2]
     first, last = k == 0, k == chunks - 1
-    per_expert = lambda *tail: pl.BlockSpec((1,) + tail, lambda q, *_: (q, 0, 0))
-    whole = lambda a: pl.BlockSpec(a.shape, lambda q, *_: (0, 0))
-    weight = pl.BlockSpec(memory_space=pltpu.HBM)
-    in_specs = [whole(x), weight, weight]
-    args = [x, *in_hbm(gate_proj, up_proj)]
+    vmem = pl.BlockSpec(memory_space=pltpu.VMEM)
+    hbm = pl.BlockSpec(memory_space=pltpu.HBM)
+    in_specs = [pl.BlockSpec(memory_space=pltpu.SMEM)] + [vmem] * len(xs) + [hbm, hbm]
+    args = [token_at, *xs, *in_hbm(gate_proj, up_proj)]
     scratch = [
         pltpu.VMEM((tokens * width // LANES, LANES), F32),
         pltpu.VMEM((slots * width // LANES, LANES), F32),
@@ -397,38 +405,36 @@
         pltpu.VMEM((held, width, units), BF),
         pltpu.SemaphoreType.DMA((2, held)),
     ]
+    aliases = {}
     if not first:
-        in_specs += [per_expert(slots, units)] * 2
+        if not last:
+            aliases = {len(args): 0, len(args) + 1: 1}
+        in_specs += [vmem] * 2
         args += list(sums)
     if last:
-        in_specs += [whole(a) for a in extras]
+        in_specs += [vmem] * 3
         args += list(extras)
         out_shape = (
             jax.ShapeDtypeStruct((held, slots, units), BF),
-            jax.ShapeDtypeStruct((tokens, held * slots), BF),
+            jax.ShapeDtypeStruct((held, tokens, slots), BF),
         )
-        out_specs = (per_expert(slots, units), pl.BlockSpec((tokens, slots), lambda q, *_: (0, q)))
         scratch.append(pltpu.VMEM((slots, extras[0].shape[1]), F32))
     else:
         out_shape = (jax.ShapeDtypeStruct((held, slots, units), F32),) * 2
-        out_specs = (per_expert(slots, units),) * 2
     return pl.pallas_call(
-        functools.partial(up_body, first, last, k * width),
-        grid_spec=pltpu.PrefetchScalarGridSpec(
-            num_scalar_prefetch=1,
-            grid=(held,),
-            in_specs=in_specs,
-            out_specs=out_specs,
-            scratch_shapes=scratch,
-        ),
+        functools.partial(up_body, first, last, k * width, len(xs), width),
+        in_specs=in_specs,
+        out_specs=(vmem, vmem),
         out_shape=out_shape,
-        compiler_params=pltpu.CompilerParams(vmem_limit_bytes=48 << 20),
+        scratch_shapes=scratch,
+        input_output_aliases=aliases,
+        compiler_params=pltpu.CompilerParams(vmem_limit_bytes=4 * held * width * units + 4 * tokens * width + (6 << 20)),
         cost_estimate=pl.CostEstimate(
             flops=4 * held * slots * width * units,
             transcendentals=0,
             bytes_accessed=4 * held * width * units,
         ),
-    )(token_at, *args)
+    )(*args)
 
 
 def down_body(begin, act, comb, wd, keep, send, halves, held_rows, arrived):
@@ -448,17 +454,18 @@
             act[q], held_rows[q], preferred_element_type=F32
         ).astype(BF)
     kept = keep.shape[0]
+    comb_rows = jnp.concatenate([comb[q] for q in range(held)], axis=1)
     block = min(width, 256)
     for j in range(0, width, block):
         cut = slice(j, j + block)
-        total = jnp.dot(comb[...], halves[:, cut], preferred_element_type=F32)
+        total = jnp.dot(comb_rows, halves[:, cut], preferred_element_type=F32)
         keep[:, cut] = total[:kept]
         send[:, cut] = total[kept:].astype(BF)
 
 
 def expert_down(k, chunks, act, comb, down_proj, kept):
     held, slots, units = act.shape
-    tokens = comb.shape[0]
+    tokens = comb.shape[1]
     width = down_proj.shape[2] // chunks
     vmem = pl.BlockSpec(memory_space=pltpu.VMEM)
     return pl.pallas_call(
@@ -474,7 +481,7 @@
             pltpu.VMEM((held, units, width), BF),
             pltpu.SemaphoreType.DMA((held,)),
         ],
-        compiler_params=pltpu.CompilerParams(vmem_limit_bytes=48 << 20),
+        compiler_params=pltpu.CompilerParams(vmem_limit_bytes=2 * held * width * (units + slots) + (8 << 20)),
         cost_estimate=pl.CostEstimate(
             flops=2 * held * slots * width * (tokens + units),
             transcendentals=0,
@@ -565,10 +572,12 @@
             payload = jnp.concatenate([payload, named], axis=1)
         rows = ring.gather_z(payload)
         rows = ring.gather(rows, "dy")
-        rows = ring.gather(rows, "dc")
-        rows = rows.reshape(all_tokens, -1)
+        rows = rows.reshape(all_tokens // cores, -1)
+        xs = [rows]
+        if cores > 1:
+            xs.append(ring.shift(rows, dc=1))
         if k == 0:
-            named_all = rows[:, span : span + experts]
+            named_all = jnp.concatenate([x[:, span : span + experts] for x in xs], axis=0)
             mine = lax.dynamic_slice_in_dim(named_all, e0, held, axis=1)
             order = jnp.arange(all_tokens, dtype=jnp.int32)
             before = (order[:, None] > order[None, :]).astype(BF)
@@ -578,13 +587,13 @@
             chosen = place.T[:, None, :] == spots[None, :, None]
             token_at = jnp.sum(jnp.where(chosen, order, 0), axis=2).reshape(-1)
         if k == AG_CHUNKS - 1:
-            extra = rows[:, rows.shape[1] - gate_lanes(experts) :].astype(F32)
+            tail = rows.shape[1] - gate_lanes(experts)
+            extra = jnp.concatenate([x[:, tail:] for x in xs], axis=0).astype(F32)
             share = lax.dynamic_slice_in_dim(
                 extra, e0 + extra.shape[1] - experts, held, axis=1
             )
             extras = (extra, place, share)
-        rows = rows[:, :span]
-        sums = expert_up(k, AG_CHUNKS, token_at, rows, gate_proj, up_proj, sums, extras)
+        sums = expert_up(k, AG_CHUNKS, token_at, xs, gate_proj, up_proj, sums, extras)
     act, comb = sums
 
     pieces = []

time: 193 us -> 178 us (0.922)
  Pallas kernels: 71.1 us -> 60.9 us
  local copies, waits for them, and re-layouts: 8.26 us -> 2.97 us
  other arithmetic: 11.2 us -> 7.03 us
  starting transfers between devices: 35.7 us -> 39.6 us
    pallas_call x4, Pallas kernels: 40.6 us -> 30.2 us  [expert_up(): pl.pallas_call(functools.partial(up_body, first, last, k * width, len(xs)...]
    another operation x15 -> x11, other arithmetic: 8.65 us -> 4.44 us  [gather(): return jnp.stack([x] + moved)]
    unnamed x26 -> x14, local copies, waits for them, and re-layouts: 5.52 us -> 1.55 us
    ppermute x38, starting transfers between devices: 35.7 us -> 39.6 us  [shift(): return lax.ppermute(x, AXES, self.pairs(**how))]
  transfers between devices with their start and end apart: 38 -> 38, of which waited for: 22 -> 22; matrix products, arithmetic and copies ran while one was open for 5% -> 4% of each run, Pallas kernels for 10% -> 20%
where the time goes in v2:
time: 178 us; the launch traced here: 177 us
  waiting for transfers between devices  65.8 us (37%)
  Pallas kernels  60.9 us (34%)
  starting transfers between devices  39.6 us (22%)
  other arithmetic  7.03 us (4%)
  local copies, waits for them, and re-layouts  2.97 us (2%)
    ppermute x38, waiting for transfers between devices, shift(): return lax.ppermute(x, AXES, self.pairs(**how))  65.8 us
    ppermute x38, starting transfers between devices, shift(): return lax.ppermute(x, AXES, self.pairs(**how))  39.6 us
    pallas_call x4, Pallas kernels, expert_up(): pl.pallas_call(functools.partial(up_body, first, last, k * width, len(xs)...  30.2 us
    pallas_call x4, Pallas kernels, expert_down(): pl.pallas_call(functools.partial(down_body, k * width), in_specs=[vmem, v...  19.3 us
    pallas_call x1, Pallas kernels, front(): pl.pallas_call(functools.partial(front_body, heads, part * span), grid_sp...  5.82 us
    another operation x11, other arithmetic, gather(): return jnp.stack([x] + moved)  4.44 us
  transfers between devices with their start and end apart: 38, of which 22 were waited for; matrix products, arithmetic and copies ran while one was open for 4% of the time, Pallas kernels for 20%

profile of v2, /device:TPU:0, one launch (start us, length us, event | category | flops | bytes accessed | tf_op | source)
XLA Modules:
  0.0 177.2 jit_solution(7318485562832161781)
XLA Ops:
  2.1 2.8 %collective-permute-start.1 = (bf16[2,32,256]{2,1,0:T(8,128)(2,1)S(1)}, bf16[2,32,256]{2,1,0:T(8,128)(2,1)S(1)}, u32[]{:S(2)}, u32[]{:S(2)}) collective-permute-start(bf16[2,32,256]{2,1,0:T(8,128)(2,1)S(1)} %get-tuple-element.84), channel_id=1, source_target_pairs={{0,8},{1,9},{2,10},{3,11},{4,12},{5,13},{6,14},{7,15},{8,0},{9,1},... | collective-permute-start | bytes 98312 | tf_op jit(solution)/shard_map/ppermute | solution.py:41
  4.9 2.4 %prepare.1 = (f32[16,128,128]{2,1,0:T(8,128)S(1)}, f32[128,16]{1,0:T(8,128)S(1)}, bf16[32,128]{1,0:T(8,128)(2,1)S(1)}) custom-call(s32[8,16]{1,0:T(8,128)} %parents.1, s32[4,8,10]{2,1,0:T(8,128)} %ids.1, f32[16,8,16]{2,1,0:T(8,128)} %step_raw.1, f32[1,16]{1,0:T(1,128)} %bitcast.127, f32[1,16]{1,0:T(1,128)} %bitcast.128), custom_call_target="tpu_custom_call" | custom-call | tf_op jit(solution)/shard_map/prepare/pallas_call | solution.py:123
  7.4 5.8 %front.1 = (f32[64,2048]{1,0:T(8,128)S(1)}, bf16[64,2048]{1,0:T(8,128)(2,1)S(1)}, bf16[128,1024]{1,0:T(8,128)(2,1)S(1)}) custom-call(s32[4]{0:T(128)S(1)} %get-tuple-element.91.slot_of, s32[4]{0:T(128)S(1)} %get-tuple-element.92.goes_to, bf16[4,32,256]{2,1,0:T(8,128)(2,1)S(1)} %bitcast.94, bf16[16,8,1024]{2,1,0:T(8,128)(2,1)} %x.1, ...), custom_call_target="tpu_custom_call" | custom-call | flops 536870912 | bytes 4194304 | tf_op jit(solution)/shard_map/front/pallas_call | solution.py:263
  13.3 2.5 %project.1 = (f32[64,2048]{1,0:T(8,128)S(1)}, bf16[64,2048]{1,0:T(8,128)(2,1)S(1)}) custom-call(bf16[128,1024]{1,0:T(8,128)(2,1)S(1)} %get-tuple-element.34.rows, bf16[1024,4096]{1,0:T(8,128)(2,1)} %weight.3), custom_call_target="tpu_custom_call" | custom-call | flops 536870912 | bytes 4194304 | tf_op jit(solution)/shard_map/project/pallas_call | solution.py:302
  16.5 1.5 collective-permute-start.3
  18.1 1.1 collective-permute-start.9
  19.2 3.8 %collective-permute-done.3 = bf16[32,2048]{1,0:T(8,128)(2,1)S(1)} collective-permute-done((bf16[32,2048]{1,0:T(8,128)(2,1)S(1)}, bf16[32,2048]{1,0:T(8,128)(2,1)S(1)}, u32[]{:S(2)}, u32[]{:S(2)}) %collective-permute-start.3) | collective-permute-done | bytes 131104 | tf_op jit(solution)/shard_map/ppermute | solution.py:41
  22.9 1.9 %collective-permute-done.9 = bf16[32,2048]{1,0:T(8,128)(2,1)S(1)} collective-permute-done((bf16[32,2048]{1,0:T(8,128)(2,1)S(1)}, bf16[32,2048]{1,0:T(8,128)(2,1)S(1)}, u32[]{:S(2)}, u32[]{:S(2)}) %collective-permute-start.9) | collective-permute-done | bytes 131104 | tf_op jit(solution)/shard_map/ppermute | solution.py:41
  25.0 2.7 %collective-permute-start.4 = (bf16[32,1152]{1,0:T(8,128)(2,1)S(1)}, bf16[32,1152]{1,0:T(8,128)(2,1)S(1)}, u32[]{:S(2)}, u32[]{:S(2)}) collective-permute-start(bf16[32,1152]{1,0:T(8,128)(2,1)S(1)} %get-tuple-element.82), channel_id=1, source_target_pairs={{0,2},{1,3},{2,0},{3,1},{4,6},{5,7},{6,4},{7,5},{8,10},{9,11},{10,... | collective-permute-start | bytes 221192 | tf_op jit(solution)/shard_map/ppermute | solution.py:41
  28.0 2.7 %collective-permute-start.14 = (bf16[32,1024]{1,0:T(8,128)(2,1)S(1)}, bf16[32,1024]{1,0:T(8,128)(2,1)S(1)}, u32[]{:S(2)}, u32[]{:S(2)}) collective-permute-start(bf16[32,1024]{1,0:T(8,128)(2,1)S(1)} %get-tuple-element.77), channel_id=1, source_target_pairs={{0,2},{1,3},{2,0},{3,1},{4,6},{5,7},{6,4},{7,5},{8,10},{9,11},{10,... | collective-permute-start | bytes 196616 | tf_op jit(solution)/shard_map/ppermute | solution.py:41
  31.7 4.7 %collective-permute-done.18 = bf16[32,1024]{1,0:T(8,128)(2,1)S(1)} collective-permute-done((bf16[32,1024]{1,0:T(8,128)(2,1)S(1)}, bf16[32,1024]{1,0:T(8,128)(2,1)S(1)}, u32[]{:S(2)}, u32[]{:S(2)}) %collective-permute-start.18) | collective-permute-done | bytes 65568 | tf_op jit(solution)/shard_map/ppermute | solution.py:41
  36.4 1.3 collective-permute-start.19
  40.8 1.3 collective-permute-start.5
  42.2 6.7 %collective-permute-done.11 = bf16[2,32,1152]{2,1,0:T(8,128)(2,1)S(1)} collective-permute-done((bf16[2,32,1152]{2,1,0:T(8,128)(2,1)S(1)}, bf16[2,32,1152]{2,1,0:T(8,128)(2,1)S(1)}, u32[]{:S(2)}, u32[]{:S(2)}) %collective-permute-start.11) | collective-permute-done | bytes 147488 | tf_op jit(solution)/shard_map/ppermute | solution.py:41
  48.9 1.5 collective-permute-start.12
  50.4 1.4 collective-permute-done.5
  51.8 1.5 collective-permute-start.6
  54.7 4.1 %collective-permute-done.12 = bf16[2,2,32,1152]{3,2,1,0:T(8,128)(2,1)S(1)} collective-permute-done((bf16[2,2,32,1152]{3,2,1,0:T(8,128)(2,1)S(1)}, bf16[2,2,32,1152]{3,2,1,0:T(8,128)(2,1)S(1)}, u32[]{:S(2)}, u32[]{:S(2)}) %collective-permute-start.12) | collective-permute-done | bytes 294944 | tf_op jit(solution)/shard_map/ppermute | solution.py:41
  59.0 6.2 %collective-permute-done.6 = bf16[2,2,32,1152]{3,2,1,0:T(8,128)(2,1)S(1)} collective-permute-done((bf16[2,2,32,1152]{3,2,1,0:T(8,128)(2,1)S(1)}, bf16[2,2,32,1152]{3,2,1,0:T(8,128)(2,1)S(1)}, u32[]{:S(2)}, u32[]{:S(2)}) %collective-permute-start.6) | collective-permute-done | bytes 294944 | tf_op jit(solution)/shard_map/ppermute | solution.py:41
  66.0 1.5 collective-permute-start.16
  67.5 2.3 %collective-permute-done.20 = bf16[2,2,32,1024]{3,2,1,0:T(8,128)(2,1)} collective-permute-done((bf16[2,2,32,1024]{3,2,1,0:T(8,128)(2,1)}, bf16[2,2,32,1024]{3,2,1,0:T(8,128)(2,1)}, u32[]{:S(2)}, u32[]{:S(2)}) %collective-permute-start.20) | collective-permute-done | bytes 262176 | tf_op jit(solution)/shard_map/ppermute | solution.py:41
  69.8 1.0 pad_maximum_fusion.3
  70.9 4.2 %collective-permute-done.16 = bf16[2,2,32,1024]{3,2,1,0:T(8,128)(2,1)S(1)} collective-permute-done((bf16[2,2,32,1024]{3,2,1,0:T(8,128)(2,1)}, bf16[2,2,32,1024]{3,2,1,0:T(8,128)(2,1)S(1)}, u32[]{:S(2)}, u32[]{:S(2)}) %collective-permute-start.16) | collective-permute-done | bytes 262176 | tf_op jit(solution)/shard_map/ppermute | solution.py:41
  75.8 1.0 pad_maximum_fusion.2
  79.6 7.5 %shard_map.163 = (f32[8,128,384]{2,1,0:T(8,128)S(1)}, f32[8,128,384]{2,1,0:T(8,128)S(1)}) custom-call(s32[1024]{0:T(1024)S(1)} %bitcast.95, bf16[256,1152]{1,0:T(8,128)(2,1)S(1)} %bitcast.87, bf16[256,1152]{1,0:T(8,128)(2,1)} %collective-permute-done.7.rest_1_, bf16[8,4096,384]{2,1,0:T(8,128)(2,1)} %rest_2_.7, bf16[8,4096,384]{2,1,0:T(8,128)(2,1)} %rest_3_.7), custom_call_target="tpu_custom_call" | custom-call | flops 1610612736 | bytes 12582912 | tf_op jit(solution)/shard_map/pallas_call | solution.py:424
  87.1 7.5 %shard_map.164 = (f32[8,128,384]{2,1,0:T(8,128)S(1)}, f32[8,128,384]{2,1,0:T(8,128)S(1)}) custom-call(s32[1024]{0:T(1024)S(1)} %bitcast.96, bf16[256,1024]{1,0:T(8,128)(2,1)S(1)} %bitcast.89, bf16[256,1024]{1,0:T(8,128)(2,1)} %collective-permute-done.21.rest_1_, bf16[8,4096,384]{2,1,0:T(8,128)(2,1)} %rest_2_.7, ...), custom_call_target="tpu_custom_call", output_to_operand_aliasing={{0}: (5, {}), {1}: (6, {})} | custom-call | flops 1610612736 | bytes 12582912 | tf_op jit(solution)/shard_map/pallas_call | solution.py:424
  94.6 7.6 %shard_map.165 = (f32[8,128,384]{2,1,0:T(8,128)S(1)}, f32[8,128,384]{2,1,0:T(8,128)S(1)}) custom-call(s32[1024]{0:T(1024)S(1)} %bitcast.97, bf16[256,1024]{1,0:T(8,128)(2,1)S(1)} %bitcast.91, bf16[256,1024]{1,0:T(8,128)(2,1)} %collective-permute-done.17.rest_1_, bf16[8,4096,384]{2,1,0:T(8,128)(2,1)} %rest_2_.7, ...), custom_call_target="tpu_custom_call", output_to_operand_aliasing={{0}: (5, {}), {1}: (6, {})} | custom-call | flops 1610612736 | bytes 12582912 | tf_op jit(solution)/shard_map/pallas_call | solution.py:424
  102.2 7.7 %shard_map.166 = (bf16[8,128,384]{2,1,0:T(8,128)(2,1)S(1)}, bf16[8,512,128]{2,1,0:T(8,128)(2,1)S(1)}) custom-call(s32[1024]{0:T(1024)S(1)} %bitcast.98, bf16[256,1152]{1,0:T(8,128)(2,1)S(1)} %bitcast.84, bf16[256,1152]{1,0:T(8,128)(2,1)S(1)} %copy-done.1, bf16[8,4096,384]{2,1,0:T(8,128)(2,1)} %rest_2_.7, bf16[8,4096,384]{2,1,0:T(8,128)(2,1)} %rest_3_.7, ...), custom_call_target="tpu_custom_call" | custom-call | flops 1610612736 | bytes 12582912 | tf_op jit(solution)/shard_map/pallas_call | solution.py:424
  109.9 4.8 %shard_map.168 = (f32[256,1024]{1,0:T(8,128)S(1)}, bf16[256,1024]{1,0:T(8,128)(2,1)S(1)}) custom-call(bf16[8,128,384]{2,1,0:T(8,128)(2,1)S(1)} %get-tuple-element.43.act, bf16[8,512,128]{2,1,0:T(8,128)(2,1)S(1)} %get-tuple-element.44.comb, bf16[8,384,4096]{2,1,0:T(8,128)(2,1)} %wd.7), custom_call_target="tpu_custom_call" | custom-call | flops 1879048192 | bytes 6291456 | tf_op jit(solution)/shard_map/pallas_call | solution.py:471
  115.3 4.8 %shard_map.167 = (f32[256,1024]{1,0:T(8,128)S(1)}, bf16[256,1024]{1,0:T(8,128)(2,1)S(1)}) custom-call(bf16[8,128,384]{2,1,0:T(8,128)(2,1)S(1)} %get-tuple-element.43.act, bf16[8,512,128]{2,1,0:T(8,128)(2,1)S(1)} %get-tuple-element.44.comb, bf16[8,384,4096]{2,1,0:T(8,128)(2,1)} %wd.7), custom_call_target="tpu_custom_call" | custom-call | flops 1879048192 | bytes 6291456 | tf_op jit(solution)/shard_map/pallas_call | solution.py:471
  120.2 4.8 %shard_map.170 = (f32[256,1024]{1,0:T(8,128)S(1)}, bf16[256,1024]{1,0:T(8,128)(2,1)S(1)}) custom-call(bf16[8,128,384]{2,1,0:T(8,128)(2,1)S(1)} %get-tuple-element.43.act, bf16[8,512,128]{2,1,0:T(8,128)(2,1)S(1)} %get-tuple-element.44.comb, bf16[8,384,4096]{2,1,0:T(8,128)(2,1)} %wd.7), custom_call_target="tpu_custom_call" | custom-call | flops 1879048192 | bytes 6291456 | tf_op jit(solution)/shard_map/pallas_call | solution.py:471
  125.6 4.8 %shard_map.169 = (f32[256,1024]{1,0:T(8,128)S(1)}, bf16[256,1024]{1,0:T(8,128)(2,1)S(1)}) custom-call(bf16[8,128,384]{2,1,0:T(8,128)(2,1)S(1)} %get-tuple-element.43.act, bf16[8,512,128]{2,1,0:T(8,128)(2,1)S(1)} %get-tuple-element.44.comb, bf16[8,384,4096]{2,1,0:T(8,128)(2,1)} %wd.7), custom_call_target="tpu_custom_call" | custom-call | flops 1879048192 | bytes 6291456 | tf_op jit(solution)/shard_map/pallas_call | solution.py:471
  130.8 1.5 collective-permute-start.27
  133.4 1.5 collective-permute-start.35
  135.8 4.2 %collective-permute-done.27 = bf16[128,1024]{1,0:T(8,128)(2,1)S(1)} collective-permute-done((bf16[128,1024]{1,0:T(8,128)(2,1)S(1)}, bf16[128,1024]{1,0:T(8,128)(2,1)S(1)}, u32[]{:S(2)}, u32[]{:S(2)}) %collective-permute-start.27) | collective-permute-done | bytes 262176 | tf_op jit(solution)/shard_map/ppermute | solution.py:41
  140.1 5.5 %collective-permute-done.23 = bf16[128,1024]{1,0:T(8,128)(2,1)S(1)} collective-permute-done((bf16[128,1024]{1,0:T(8,128)(2,1)S(1)}, bf16[128,1024]{1,0:T(8,128)(2,1)S(1)}, u32[]{:S(2)}, u32[]{:S(2)}) %collective-permute-start.23) | collective-permute-done | bytes 262176 | tf_op jit(solution)/shard_map/ppermute | solution.py:41
  145.8 5.5 %collective-permute-done.35 = bf16[128,1024]{1,0:T(8,128)(2,1)S(1)} collective-permute-done((bf16[128,1024]{1,0:T(8,128)(2,1)S(1)}, bf16[128,1024]{1,0:T(8,128)(2,1)S(1)}, u32[]{:S(2)}, u32[]{:S(2)}) %collective-permute-start.35) | collective-permute-done | bytes 262176 | tf_op jit(solution)/shard_map/ppermute | solution.py:41
  151.4 1.0 collective-permute-start.28
  152.4 4.0 %collective-permute-done.31 = bf16[128,1024]{1,0:T(8,128)(2,1)S(1)} collective-permute-done((bf16[128,1024]{1,0:T(8,128)(2,1)S(1)}, bf16[128,1024]{1,0:T(8,128)(2,1)S(1)}, u32[]{:S(2)}, u32[]{:S(2)}) %collective-permute-start.31) | collective-permute-done | bytes 262176 | tf_op jit(solution)/shard_map/ppermute | solution.py:41
  156.5 1.0 collective-permute-start.24
  157.5 1.1 collective-permute-start.36
  158.6 0.9 collective-permute-start.32
  159.6 3.6 %collective-permute-start.29 = (bf16[1,32,1024]{2,1,0:T(8,128)(2,1)S(1)}, bf16[1,32,1024]{2,1,0:T(8,128)(2,1)S(1)}, u32[]{:S(2)}, u32[]{:S(2)}) collective-permute-start(bf16[1,32,1024]{2,1,0:T(8,128)(2,1)S(1)} %slice.326), channel_id=1, source_target_pairs={{0,2},{1,3},{2,0},{3,1},{4,6},{5,7},{6,4},{7,5},{8,10},{9,11},{10,... | collective-permute-start | bytes 196616 | tf_op jit(solution)/shard_map/ppermute | solution.py:41
  163.7 1.9 %collective-permute-start.25 = (bf16[1,32,1024]{2,1,0:T(8,128)(2,1)S(1)}, bf16[1,32,1024]{2,1,0:T(8,128)(2,1)S(1)}, u32[]{:S(2)}, u32[]{:S(2)}) collective-permute-start(bf16[1,32,1024]{2,1,0:T(8,128)(2,1)S(1)} %slice.327), channel_id=1, source_target_pairs={{0,2},{1,3},{2,0},{3,1},{4,6},{5,7},{6,4},{7,5},{8,10},{9,11},{10,... | collective-permute-start | bytes 196616 | tf_op jit(solution)/shard_map/ppermute | solution.py:41
  165.6 2.3 %collective-permute-done.36 = bf16[2,32,1024]{2,1,0:T(8,128)(2,1)S(1)} collective-permute-done((bf16[2,32,1024]{2,1,0:T(8,128)(2,1)S(1)}, bf16[2,32,1024]{2,1,0:T(8,128)(2,1)S(1)}, u32[]{:S(2)}, u32[]{:S(2)}) %collective-permute-start.36) | collective-permute-done | bytes 131104 | tf_op jit(solution)/shard_map/ppermute | solution.py:41
  167.9 2.0 %collective-permute-start.37 = (bf16[1,32,1024]{2,1,0:T(8,128)(2,1)S(1)}, bf16[1,32,1024]{2,1,0:T(8,128)(2,1)S(1)}, u32[]{:S(2)}, u32[]{:S(2)}) collective-permute-start(bf16[1,32,1024]{2,1,0:T(8,128)(2,1)S(1)} %slice.324), channel_id=1, source_target_pairs={{0,2},{1,3},{2,0},{3,1},{4,6},{5,7},{6,4},{7,5},{8,10},{9,11},{10,... | collective-permute-start | bytes 196616 | tf_op jit(solution)/shard_map/ppermute | solution.py:41
  171.4 2.9 %collective-permute-done.25 = bf16[1,32,1024]{2,1,0:T(8,128)(2,1)S(1)} collective-permute-done((bf16[1,32,1024]{2,1,0:T(8,128)(2,1)S(1)}, bf16[1,32,1024]{2,1,0:T(8,128)(2,1)S(1)}, u32[]{:S(2)}, u32[]{:S(2)}) %collective-permute-start.25) | collective-permute-done | bytes 65568 | tf_op jit(solution)/shard_map/ppermute | solution.py:41
  174.4 1.3 collective-permute-done.37
  (123 shorter events, 20.9 us)
Async XLA Ops:
  0.7 1.3 collective-permute-start
  2.1 5.3 %collective-permute-start.1 = (bf16[2,32,256]{2,1,0:T(8,128)(2,1)S(1)}, bf16[2,32,256]{2,1,0:T(8,128)(2,1)S(1)}, u32[]{:S(2)}, u32[]{:S(2)}) collective-permute-start(bf16[2,32,256]{2,1,0:T(8,128)(2,1)S(1)} %get-tuple-element.84), channel_id=1, source_target_pairs={{0,8},{1,9},{2,10},{3,11},{4,12},{5,13},{6,14},{7,15},{8,0},{9,1},... | collective-permute-start | bytes 98312 | tf_op jit(solution)/shard_map/ppermute | solution.py:41
  13.2 3.2 %collective-permute-start.2 = (bf16[64,2048]{1,0:T(8,128)(2,1)S(1)}, bf16[64,2048]{1,0:T(8,128)(2,1)S(1)}, u32[]{:S(2)}, u32[]{:S(2)}) collective-permute-start(bf16[64,2048]{1,0:T(8,128)(2,1)S(1)} %get-tuple-element.32), channel_id=1, source_target_pairs={{0,4},{1,5},{2,6},{3,7},{4,0},{5,1},{6,2},{7,3},{8,12},{9,13},{10,... | collective-permute-start | bytes 786440 | tf_op jit(solution)/shard_map/ppermute | solution.py:41
  15.8 3.3 %copy-start.3 = (f32[4096]{0:T(1024)S(1)}, f32[4096]{0:T(1024)}, u32[]{:S(2)}) copy-start(f32[4096]{0:T(1024)} %param.28) | copy-start | bytes 49156
  15.9 9.0 %copy-start.5 = (bf16[4,8,4096]{2,1,0:T(8,128)(2,1)S(1)}, bf16[4,8,4096]{2,1,0:T(8,128)(2,1)}, u32[]{:S(2)}) copy-start(bf16[4,8,4096]{2,1,0:T(8,128)(2,1)} %param.27) | copy-start | bytes 786436
  15.9 2.2 %collective-permute-start.8 = (bf16[64,2048]{1,0:T(8,128)(2,1)S(1)}, bf16[64,2048]{1,0:T(8,128)(2,1)S(1)}, u32[]{:S(2)}, u32[]{:S(2)}) collective-permute-start(bf16[64,2048]{1,0:T(8,128)(2,1)S(1)} %get-tuple-element.36), channel_id=1, source_target_pairs={{0,4},{1,5},{2,6},{3,7},{4,0},{5,1},{6,2},{7,3},{8,12},{9,13},{10,... | collective-permute-start | bytes 786440 | tf_op jit(solution)/shard_map/ppermute | solution.py:41
  16.5 6.4 %collective-permute-start.3 = (bf16[32,2048]{1,0:T(8,128)(2,1)S(1)}, bf16[32,2048]{1,0:T(8,128)(2,1)S(1)}, u32[]{:S(2)}, u32[]{:S(2)}) collective-permute-start(bf16[32,2048]{1,0:T(8,128)(2,1)S(1)} %slice.323), channel_id=1, source_target_pairs={{0,8},{1,9},{2,10},{3,11},{4,12},{5,13},{6,14},{7,15},{8,0},{9,1},... | collective-permute-start | bytes 393224 | tf_op jit(solution)/shard_map/ppermute | solution.py:41
  18.0 12.6 %copy-start.2 = (bf16[4096,64]{0,1:T(8,128)(2,1)S(1)}, bf16[4096,64]{0,1:T(8,128)(2,1)}, u32[]{:S(2)}) copy-start(bf16[4096,64]{0,1:T(8,128)(2,1)} %param.29) | copy-start | bytes 1572868
  18.1 6.7 %collective-permute-start.9 = (bf16[32,2048]{1,0:T(8,128)(2,1)S(1)}, bf16[32,2048]{1,0:T(8,128)(2,1)S(1)}, u32[]{:S(2)}, u32[]{:S(2)}) collective-permute-start(bf16[32,2048]{1,0:T(8,128)(2,1)S(1)} %slice.322), channel_id=1, source_target_pairs={{0,8},{1,9},{2,10},{3,11},{4,12},{5,13},{6,14},{7,15},{8,0},{9,1},... | collective-permute-start | bytes 393224 | tf_op jit(solution)/shard_map/ppermute | solution.py:41
  25.0 15.8 %collective-permute-start.4 = (bf16[32,1152]{1,0:T(8,128)(2,1)S(1)}, bf16[32,1152]{1,0:T(8,128)(2,1)S(1)}, u32[]{:S(2)}, u32[]{:S(2)}) collective-permute-start(bf16[32,1152]{1,0:T(8,128)(2,1)S(1)} %get-tuple-element.82), channel_id=1, source_target_pairs={{0,2},{1,3},{2,0},{3,1},{4,6},{5,7},{6,4},{7,5},{8,10},{9,11},{10,... | collective-permute-start | bytes 221192 | tf_op jit(solution)/shard_map/ppermute | solution.py:41
  27.6 8.8 %collective-permute-start.18 = (bf16[32,1024]{1,0:T(8,128)(2,1)S(1)}, bf16[32,1024]{1,0:T(8,128)(2,1)S(1)}, u32[]{:S(2)}, u32[]{:S(2)}) collective-permute-start(bf16[32,1024]{1,0:T(8,128)(2,1)S(1)} %get-tuple-element.73), channel_id=1, source_target_pairs={{0,2},{1,3},{2,0},{3,1},{4,6},{5,7},{6,4},{7,5},{8,10},{9,11},{10,... | collective-permute-start | bytes 196616 | tf_op jit(solution)/shard_map/ppermute | solution.py:41
  28.0 10.6 %collective-permute-start.14 = (bf16[32,1024]{1,0:T(8,128)(2,1)S(1)}, bf16[32,1024]{1,0:T(8,128)(2,1)S(1)}, u32[]{:S(2)}, u32[]{:S(2)}) collective-permute-start(bf16[32,1024]{1,0:T(8,128)(2,1)S(1)} %get-tuple-element.77), channel_id=1, source_target_pairs={{0,2},{1,3},{2,0},{3,1},{4,6},{5,7},{6,4},{7,5},{8,10},{9,11},{10,... | collective-permute-start | bytes 196616 | tf_op jit(solution)/shard_map/ppermute | solution.py:41
  31.3 8.7 %collective-permute-start.10 = (bf16[32,1152]{1,0:T(8,128)(2,1)S(1)}, bf16[32,1152]{1,0:T(8,128)(2,1)S(1)}, u32[]{:S(2)}, u32[]{:S(2)}) collective-permute-start(bf16[32,1152]{1,0:T(8,128)(2,1)S(1)} %get-tuple-element.80), channel_id=1, source_target_pairs={{0,2},{1,3},{2,0},{3,1},{4,6},{5,7},{6,4},{7,5},{8,10},{9,11},{10,... | collective-permute-start | bytes 221192 | tf_op jit(solution)/shard_map/ppermute | solution.py:41
  36.4 16.9 %collective-permute-start.19 = (bf16[2,32,1024]{2,1,0:T(8,128)(2,1)S(1)}, bf16[2,32,1024]{2,1,0:T(8,128)(2,1)S(1)}, u32[]{:S(2)}, u32[]{:S(2)}) collective-permute-start(bf16[2,32,1024]{2,1,0:T(8,128)(2,1)S(1)} %get-tuple-element.72), channel_id=1, source_target_pairs={{0,1},{1,0},{2,3},{3,2},{4,5},{5,4},{6,7},{7,6},{8,9},{9,8},{10,11... | collective-permute-start | bytes 393224 | tf_op jit(solution)/shard_map/ppermute | solution.py:41
  38.6 26.7 %collective-permute-start.15 = (bf16[2,32,1024]{2,1,0:T(8,128)(2,1)S(1)}, bf16[2,32,1024]{2,1,0:T(8,128)(2,1)S(1)}, u32[]{:S(2)}, u32[]{:S(2)}) collective-permute-start(bf16[2,32,1024]{2,1,0:T(8,128)(2,1)S(1)} %get-tuple-element.76), channel_id=1, source_target_pairs={{0,1},{1,0},{2,3},{3,2},{4,5},{5,4},{6,7},{7,6},{8,9},{9,8},{10,11... | collective-permute-start | bytes 393224 | tf_op jit(solution)/shard_map/ppermute | solution.py:41
  40.0 8.8 %collective-permute-start.11 = (bf16[2,32,1152]{2,1,0:T(8,128)(2,1)S(1)}, bf16[2,32,1152]{2,1,0:T(8,128)(2,1)S(1)}, u32[]{:S(2)}, u32[]{:S(2)}) collective-permute-start(bf16[2,32,1152]{2,1,0:T(8,128)(2,1)S(1)} %get-tuple-element.64), channel_id=1, source_target_pairs={{0,1},{1,0},{2,3},{3,2},{4,5},{5,4},{6,7},{7,6},{8,9},{9,8},{10,11... | collective-permute-start | bytes 442376 | tf_op jit(solution)/shard_map/ppermute | solution.py:41
  40.8 11.0 %collective-permute-start.5 = (bf16[2,32,1152]{2,1,0:T(8,128)(2,1)S(1)}, bf16[2,32,1152]{2,1,0:T(8,128)(2,1)S(1)}, u32[]{:S(2)}, u32[]{:S(2)}) collective-permute-start(bf16[2,32,1152]{2,1,0:T(8,128)(2,1)S(1)} %get-tuple-element.66), channel_id=1, source_target_pairs={{0,1},{1,0},{2,3},{3,2},{4,5},{5,4},{6,7},{7,6},{8,9},{9,8},{10,11... | collective-permute-start | bytes 442376 | tf_op jit(solution)/shard_map/ppermute | solution.py:41
  48.9 9.9 %collective-permute-start.12 = (bf16[2,2,32,1152]{3,2,1,0:T(8,128)(2,1)S(1)}, bf16[2,2,32,1152]{3,2,1,0:T(8,128)(2,1)S(1)}, u32[]{:S(2)}, u32[]{:S(2)}) collective-permute-start(bf16[2,2,32,1152]{3,2,1,0:T(8,128)(2,1)S(1)} %get-tuple-element.54), channel_id=1, source_target_pairs={{0,8},{1,9},{2,10},{3,11},{4,12},{5,13},{6,14},{7,15},{8,0},{9,1},... | collective-permute-start | bytes 884744 | tf_op jit(solution)/shard_map/ppermute | solution.py:41
  51.8 13.3 %collective-permute-start.6 = (bf16[2,2,32,1152]{3,2,1,0:T(8,128)(2,1)S(1)}, bf16[2,2,32,1152]{3,2,1,0:T(8,128)(2,1)S(1)}, u32[]{:S(2)}, u32[]{:S(2)}) collective-permute-start(bf16[2,2,32,1152]{3,2,1,0:T(8,128)(2,1)S(1)} %get-tuple-element.56), channel_id=1, source_target_pairs={{0,8},{1,9},{2,10},{3,11},{4,12},{5,13},{6,14},{7,15},{8,0},{9,1},... | collective-permute-start | bytes 884744 | tf_op jit(solution)/shard_map/ppermute | solution.py:41
  54.1 15.7 %collective-permute-start.20 = (bf16[2,2,32,1024]{3,2,1,0:T(8,128)(2,1)}, bf16[2,2,32,1024]{3,2,1,0:T(8,128)(2,1)}, u32[]{:S(2)}, u32[]{:S(2)}) collective-permute-start(bf16[2,2,32,1024]{3,2,1,0:T(8,128)(2,1)} %get-tuple-element.58), channel_id=1, source_target_pairs={{0,8},{1,9},{2,10},{3,11},{4,12},{5,13},{6,14},{7,15},{8,0},{9,1},... | collective-permute-start | bytes 786440 | tf_op jit(solution)/shard_map/ppermute | solution.py:41
  58.9 18.1 %collective-permute-start.13 = (bf16[256,1152]{1,0:T(8,128)(2,1)S(1)}, bf16[256,1152]{1,0:T(8,128)(2,1)S(1)}, u32[]{:S(2)}, u32[]{:S(2)}) collective-permute-start(bf16[256,1152]{1,0:T(8,128)(2,1)S(1)} %bitcast.82), channel_id=1, source_target_pairs={{0,4},{1,5},{2,6},{3,7},{4,0},{5,1},{6,2},{7,3},{8,12},{9,13},{10,... | collective-permute-start | bytes 1769480 | tf_op jit(solution)/shard_map/ppermute | solution.py:41
  65.2 12.6 %collective-permute-start.7 = (bf16[256,1152]{1,0:T(8,128)(2,1)S(1)}, bf16[256,1152]{1,0:T(8,128)(2,1)}, u32[]{:S(2)}, u32[]{:S(2)}) collective-permute-start(bf16[256,1152]{1,0:T(8,128)(2,1)S(1)} %bitcast.85), channel_id=1, source_target_pairs={{0,4},{1,5},{2,6},{3,7},{4,0},{5,1},{6,2},{7,3},{8,12},{9,13},{10,... | collective-permute-start | bytes 1769480 | tf_op jit(solution)/shard_map/ppermute | solution.py:41
  66.0 9.1 %collective-permute-start.16 = (bf16[2,2,32,1024]{3,2,1,0:T(8,128)(2,1)}, bf16[2,2,32,1024]{3,2,1,0:T(8,128)(2,1)S(1)}, u32[]{:S(2)}, u32[]{:S(2)}) collective-permute-start(bf16[2,2,32,1024]{3,2,1,0:T(8,128)(2,1)} %get-tuple-element.60), channel_id=1, source_target_pairs={{0,8},{1,9},{2,10},{3,11},{4,12},{5,13},{6,14},{7,15},{8,0},{9,1},... | collective-permute-start | bytes 786440 | tf_op jit(solution)/shard_map/ppermute | solution.py:41
  70.8 16.3 %collective-permute-start.21 = (bf16[256,1024]{1,0:T(8,128)(2,1)S(1)}, bf16[256,1024]{1,0:T(8,128)(2,1)}, u32[]{:S(2)}, u32[]{:S(2)}) collective-permute-start(bf16[256,1024]{1,0:T(8,128)(2,1)S(1)} %bitcast.88), channel_id=1, source_target_pairs={{0,4},{1,5},{2,6},{3,7},{4,0},{5,1},{6,2},{7,3},{8,12},{9,13},{10,... | collective-permute-start | bytes 1572872 | tf_op jit(solution)/shard_map/ppermute | solution.py:41
  75.1 0.7 copy-start.6
  76.8 17.8 %collective-permute-start.17 = (bf16[256,1024]{1,0:T(8,128)(2,1)S(1)}, bf16[256,1024]{1,0:T(8,128)(2,1)}, u32[]{:S(2)}, u32[]{:S(2)}) collective-permute-start(bf16[256,1024]{1,0:T(8,128)(2,1)S(1)} %bitcast.90), channel_id=1, source_target_pairs={{0,4},{1,5},{2,6},{3,7},{4,0},{5,1},{6,2},{7,3},{8,12},{9,13},{10,... | collective-permute-start | bytes 1572872 | tf_op jit(solution)/shard_map/ppermute | solution.py:41
  77.0 0.8 copy-start
  94.6 7.6 %copy-start.1 = (bf16[256,1152]{1,0:T(8,128)(2,1)S(1)}, bf16[256,1152]{1,0:T(8,128)(2,1)}, u32[]{:S(2)}) copy-start(bf16[256,1152]{1,0:T(8,128)(2,1)} %copy-done) | copy-start | bytes 1769476
  114.8 15.8 %collective-permute-start.26 = (bf16[256,1024]{1,0:T(8,128)(2,1)S(1)}, bf16[256,1024]{1,0:T(8,128)(2,1)S(1)}, u32[]{:S(2)}, u32[]{:S(2)}) collective-permute-start(bf16[256,1024]{1,0:T(8,128)(2,1)S(1)} %get-tuple-element.48), channel_id=1, source_target_pairs={{0,4},{1,5},{2,6},{3,7},{4,0},{5,1},{6,2},{7,3},{8,12},{9,13},{10,... | collective-permute-start | bytes 1572872 | tf_op jit(solution)/shard_map/ppermute | solution.py:41
  120.1 12.1 %collective-permute-start.22 = (bf16[256,1024]{1,0:T(8,128)(2,1)S(1)}, bf16[256,1024]{1,0:T(8,128)(2,1)S(1)}, u32[]{:S(2)}, u32[]{:S(2)}) collective-permute-start(bf16[256,1024]{1,0:T(8,128)(2,1)S(1)} %get-tuple-element.46), channel_id=1, source_target_pairs={{0,4},{1,5},{2,6},{3,7},{4,0},{5,1},{6,2},{7,3},{8,12},{9,13},{10,... | collective-permute-start | bytes 1572872 | tf_op jit(solution)/shard_map/ppermute | solution.py:41
  125.1 8.1 %collective-permute-start.34 = (bf16[256,1024]{1,0:T(8,128)(2,1)S(1)}, bf16[256,1024]{1,0:T(8,128)(2,1)S(1)}, u32[]{:S(2)}, u32[]{:S(2)}) collective-permute-start(bf16[256,1024]{1,0:T(8,128)(2,1)S(1)} %get-tuple-element.52), channel_id=1, source_target_pairs={{0,4},{1,5},{2,6},{3,7},{4,0},{5,1},{6,2},{7,3},{8,12},{9,13},{10,... | collective-permute-start | bytes 1572872 | tf_op jit(solution)/shard_map/ppermute | solution.py:41
  130.5 4.5 %collective-permute-start.30 = (bf16[256,1024]{1,0:T(8,128)(2,1)S(1)}, bf16[256,1024]{1,0:T(8,128)(2,1)S(1)}, u32[]{:S(2)}, u32[]{:S(2)}) collective-permute-start(bf16[256,1024]{1,0:T(8,128)(2,1)S(1)} %get-tuple-element.50), channel_id=1, source_target_pairs={{0,4},{1,5},{2,6},{3,7},{4,0},{5,1},{6,2},{7,3},{8,12},{9,13},{10,... | collective-permute-start | bytes 1572872 | tf_op jit(solution)/shard_map/ppermute | solution.py:41
  130.8 9.2 %collective-permute-start.27 = (bf16[128,1024]{1,0:T(8,128)(2,1)S(1)}, bf16[128,1024]{1,0:T(8,128)(2,1)S(1)}, u32[]{:S(2)}, u32[]{:S(2)}) collective-permute-start(bf16[128,1024]{1,0:T(8,128)(2,1)S(1)} %slice.316), channel_id=1, source_target_pairs={{0,8},{1,9},{2,10},{3,11},{4,12},{5,13},{6,14},{7,15},{8,0},{9,1},... | collective-permute-start | bytes 786440 | tf_op jit(solution)/shard_map/ppermute | solution.py:41
  132.5 13.1 %collective-permute-start.23 = (bf16[128,1024]{1,0:T(8,128)(2,1)S(1)}, bf16[128,1024]{1,0:T(8,128)(2,1)S(1)}, u32[]{:S(2)}, u32[]{:S(2)}) collective-permute-start(bf16[128,1024]{1,0:T(8,128)(2,1)S(1)} %slice.317), channel_id=1, source_target_pairs={{0,8},{1,9},{2,10},{3,11},{4,12},{5,13},{6,14},{7,15},{8,0},{9,1},... | collective-permute-start | bytes 786440 | tf_op jit(solution)/shard_map/ppermute | solution.py:41
  133.4 17.9 %collective-permute-start.35 = (bf16[128,1024]{1,0:T(8,128)(2,1)S(1)}, bf16[128,1024]{1,0:T(8,128)(2,1)S(1)}, u32[]{:S(2)}, u32[]{:S(2)}) collective-permute-start(bf16[128,1024]{1,0:T(8,128)(2,1)S(1)} %slice.314), channel_id=1, source_target_pairs={{0,8},{1,9},{2,10},{3,11},{4,12},{5,13},{6,14},{7,15},{8,0},{9,1},... | collective-permute-start | bytes 786440 | tf_op jit(solution)/shard_map/ppermute | solution.py:41
  135.1 21.3 %collective-permute-start.31 = (bf16[128,1024]{1,0:T(8,128)(2,1)S(1)}, bf16[128,1024]{1,0:T(8,128)(2,1)S(1)}, u32[]{:S(2)}, u32[]{:S(2)}) collective-permute-start(bf16[128,1024]{1,0:T(8,128)(2,1)S(1)} %slice.315), channel_id=1, source_target_pairs={{0,8},{1,9},{2,10},{3,11},{4,12},{5,13},{6,14},{7,15},{8,0},{9,1},... | collective-permute-start | bytes 786440 | tf_op jit(solution)/shard_map/ppermute | solution.py:41
  140.1 11.3 %copy-start.4 = (f32[128,1024]{1,0:T(8,128)}, f32[128,1024]{1,0:T(8,128)S(1)}, u32[]{:S(2)}) copy-start(f32[128,1024]{1,0:T(8,128)S(1)} %slice_add_fusion.2) | copy-start | bytes 1572868
  151.4 8.1 %slice-start = ((f32[128,1024]{1,0:T(8,128)}), f32[64,1024]{1,0:T(8,128)S(1)}, s32[]{:S(2)}) async-start(f32[128,1024]{1,0:T(8,128)} %copy-done.4), calls=%async_computation | async-start | bytes 524288 | tf_op jit(solution)/shard_map/slice | solution.py:64
  151.4 8.1 %collective-permute-start.28 = (bf16[2,32,1024]{2,1,0:T(8,128)(2,1)S(1)}, bf16[2,32,1024]{2,1,0:T(8,128)(2,1)S(1)}, u32[]{:S(2)}, u32[]{:S(2)}) collective-permute-start(bf16[2,32,1024]{2,1,0:T(8,128)(2,1)S(1)} %bitcast.116), channel_id=1, source_target_pairs={{0,1},{1,0},{2,3},{3,2},{4,5},{5,4},{6,7},{7,6},{8,9},{9,8},{10,11... | collective-permute-start | bytes 393224 | tf_op jit(solution)/shard_map/ppermute | solution.py:41
  156.5 7.1 %collective-permute-start.24 = (bf16[2,32,1024]{2,1,0:T(8,128)(2,1)S(1)}, bf16[2,32,1024]{2,1,0:T(8,128)(2,1)S(1)}, u32[]{:S(2)}, u32[]{:S(2)}) collective-permute-start(bf16[2,32,1024]{2,1,0:T(8,128)(2,1)S(1)} %bitcast.114), channel_id=1, source_target_pairs={{0,1},{1,0},{2,3},{3,2},{4,5},{5,4},{6,7},{7,6},{8,9},{9,8},{10,11... | collective-permute-start | bytes 393224 | tf_op jit(solution)/shard_map/ppermute | solution.py:41
  157.5 10.4 %collective-permute-start.36 = (bf16[2,32,1024]{2,1,0:T(8,128)(2,1)S(1)}, bf16[2,32,1024]{2,1,0:T(8,128)(2,1)S(1)}, u32[]{:S(2)}, u32[]{:S(2)}) collective-permute-start(bf16[2,32,1024]{2,1,0:T(8,128)(2,1)S(1)} %bitcast.113), channel_id=1, source_target_pairs={{0,1},{1,0},{2,3},{3,2},{4,5},{5,4},{6,7},{7,6},{8,9},{9,8},{10,11... | collective-permute-start | bytes 393224 | tf_op jit(solution)/shard_map/ppermute | solution.py:41
  158.6 12.1 %collective-permute-start.32 = (bf16[2,32,1024]{2,1,0:T(8,128)(2,1)S(1)}, bf16[2,32,1024]{2,1,0:T(8,128)(2,1)S(1)}, u32[]{:S(2)}, u32[]{:S(2)}) collective-permute-start(bf16[2,32,1024]{2,1,0:T(8,128)(2,1)S(1)} %bitcast.115), channel_id=1, source_target_pairs={{0,1},{1,0},{2,3},{3,2},{4,5},{5,4},{6,7},{7,6},{8,9},{9,8},{10,11... | collective-permute-start | bytes 393224 | tf_op jit(solution)/shard_map/ppermute | solution.py:41
  159.6 11.9 %collective-permute-start.29 = (bf16[1,32,1024]{2,1,0:T(8,128)(2,1)S(1)}, bf16[1,32,1024]{2,1,0:T(8,128)(2,1)S(1)}, u32[]{:S(2)}, u32[]{:S(2)}) collective-permute-start(bf16[1,32,1024]{2,1,0:T(8,128)(2,1)S(1)} %slice.326), channel_id=1, source_target_pairs={{0,2},{1,3},{2,0},{3,1},{4,6},{5,7},{6,4},{7,5},{8,10},{9,11},{10,... | collective-permute-start | bytes 196616 | tf_op jit(solution)/shard_map/ppermute | solution.py:41
  163.7 10.7 %collective-permute-start.25 = (bf16[1,32,1024]{2,1,0:T(8,128)(2,1)S(1)}, bf16[1,32,1024]{2,1,0:T(8,128)(2,1)S(1)}, u32[]{:S(2)}, u32[]{:S(2)}) collective-permute-start(bf16[1,32,1024]{2,1,0:T(8,128)(2,1)S(1)} %slice.327), channel_id=1, source_target_pairs={{0,2},{1,3},{2,0},{3,1},{4,6},{5,7},{6,4},{7,5},{8,10},{9,11},{10,... | collective-permute-start | bytes 196616 | tf_op jit(solution)/shard_map/ppermute | solution.py:41
  167.9 7.8 %collective-permute-start.37 = (bf16[1,32,1024]{2,1,0:T(8,128)(2,1)S(1)}, bf16[1,32,1024]{2,1,0:T(8,128)(2,1)S(1)}, u32[]{:S(2)}, u32[]{:S(2)}) collective-permute-start(bf16[1,32,1024]{2,1,0:T(8,128)(2,1)S(1)} %slice.324), channel_id=1, source_target_pairs={{0,2},{1,3},{2,0},{3,1},{4,6},{5,7},{6,4},{7,5},{8,10},{9,11},{10,... | collective-permute-start | bytes 196616 | tf_op jit(solution)/shard_map/ppermute | solution.py:41
  170.8 5.7 %collective-permute-start.33 = (bf16[1,32,1024]{2,1,0:T(8,128)(2,1)S(1)}, bf16[1,32,1024]{2,1,0:T(8,128)(2,1)S(1)}, u32[]{:S(2)}, u32[]{:S(2)}) collective-permute-start(bf16[1,32,1024]{2,1,0:T(8,128)(2,1)S(1)} %slice.325), channel_id=1, source_target_pairs={{0,2},{1,3},{2,0},{3,1},{4,6},{5,7},{6,4},{7,5},{8,10},{9,11},{10,... | collective-permute-start | bytes 196616 | tf_op jit(solution)/shard_map/ppermute | solution.py:41

commit v3 on v2

--- a/solution.py
+++ b/solution.py
@@ -316,15 +316,57 @@
     )(rows, *in_hbm(out_proj))
 
 
-def up_body(first, last, begin, pieces, width, token_at, *rest):
+def own_columns(lanes, first, held):
+    at = lax.broadcasted_iota(jnp.int32, (lanes, held), 0)
+    to = lax.broadcasted_iota(jnp.int32, (lanes, held), 1)
+    return jnp.where(at == to + first, 1.0, 0.0).astype(BF)
+
+
+def place_body(begin, e0, *rest):
+    xs, (tokens_out, place_out) = rest[:-2], rest[-2:]
+    held, slots = tokens_out.shape
+    named = jnp.concatenate([x[:, begin:] for x in xs], axis=0)
+    count, lanes = named.shape
+    mine = jnp.dot(
+        named, own_columns(lanes, e0[0], held), preferred_element_type=F32
+    )
+    row = lax.broadcasted_iota(jnp.int32, (count, count), 0)
+    column = lax.broadcasted_iota(jnp.int32, (count, count), 1)
+    before = jnp.where(row > column, 1.0, 0.0).astype(BF)
+    rank = jnp.dot(before, mine.astype(BF), preferred_element_type=F32)
+    place = jnp.where(mine > 0, rank, -1.0)
+    place_out[...] = place
+    spot = lax.broadcasted_iota(jnp.int32, (count, slots), 1).astype(F32)
+    token = lax.broadcasted_iota(jnp.int32, (count, slots), 0).astype(F32)
+    for q in range(held):
+        here = jnp.where(spot == place[:, q : q + 1], token, 0.0)
+        tokens_out[q : q + 1] = jnp.sum(here, axis=0, keepdims=True).astype(jnp.int32)
+
+
+def places(e0, xs, begin, held, slots):
+    tokens = sum(x.shape[0] for x in xs)
+    return pl.pallas_call(
+        functools.partial(place_body, begin),
+        in_specs=[pl.BlockSpec(memory_space=pltpu.SMEM)]
+        + [pl.BlockSpec(memory_space=pltpu.VMEM)] * len(xs),
+        out_shape=(
+            jax.ShapeDtypeStruct((held, slots), jnp.int32),
+            jax.ShapeDtypeStruct((tokens, held), F32),
+        ),
+        compiler_params=pltpu.CompilerParams(vmem_limit_bytes=10 << 20),
+        name="places",
+    )(e0, *xs)
+
+
+def up_body(first, last, begin, pieces, width, experts, token_at, *rest):
     rest = list(rest)
     xs = [rest.pop(0) for _ in range(pieces)]
     wg, wu = rest.pop(0), rest.pop(0)
     if not first:
         gin, uin = rest.pop(0), rest.pop(0)
     if last:
-        extra, spot, share = rest.pop(0), rest.pop(0), rest.pop(0)
-        act_out, comb_out, spread, picked, gates_held, ups_held, arrived, scales = rest
+        spot, e0 = rest.pop(0), rest.pop(0)
+        act_out, comb_out, spread, picked, gates_held, ups_held, arrived, scales, extra = rest
     else:
         gout, uout, spread, picked, gates_held, ups_held, arrived = rest
     held = gates_held.shape[0]
@@ -348,11 +390,20 @@
             spread[pl.ds(done * tall + i, tokens, stride=tall), :] = x[
                 :, i * LANES : (i + 1) * LANES
             ].astype(F32)
+        if last:
+            extra[done : done + tokens] = x[:, width:].astype(F32)
         done += tokens
+    if last:
+        lanes = extra.shape[1]
+        share = jnp.dot(
+            extra[...].astype(BF),
+            own_columns(lanes, e0[0] + lanes - experts, held),
+            preferred_element_type=F32,
+        )
 
     def visit(q, carry):
         for c in range(0, slots, BATCH):
-            at = [token_at[q * slots + c + i] for i in range(BATCH)]
+            at = [token_at[q, c + i] for i in range(BATCH)]
             got = [spread[pl.ds(pl.multiple_of(t * tall, tall), tall)] for t in at]
             picked[c * tall : (c + BATCH) * tall] = jnp.concatenate(got, axis=0)
             if last:
@@ -377,21 +428,21 @@
         gated = gated * scale
         lifted = lifted * scale
         act_out[q] = (gated / (1.0 + jnp.exp(-gated)) * lifted).astype(BF)
-        lane = lax.broadcasted_iota(jnp.int32, (done, slots), 1)
+        lane = lax.broadcasted_iota(jnp.int32, (done, slots), 1).astype(F32)
         column = lax.broadcasted_iota(jnp.int32, spot.shape, 1)
-        own_spot = jnp.sum(jnp.where(column == q, spot[...], 0), axis=1, keepdims=True)
-        own_share = jnp.sum(jnp.where(column == q, share[...], 0.0), axis=1, keepdims=True)
+        own_spot = jnp.sum(jnp.where(column == q, spot[...], 0.0), axis=1, keepdims=True)
+        own_share = jnp.sum(jnp.where(column == q, share, 0.0), axis=1, keepdims=True)
         comb_out[q] = jnp.where(lane == own_spot, own_share, 0.0).astype(BF)
         return carry
 
     lax.fori_loop(0, held, visit, 0)
 
 
-def expert_up(k, chunks, token_at, xs, gate_proj, up_proj, sums, extras):
+def expert_up(k, chunks, experts, token_at, xs, gate_proj, up_proj, sums, place, e0):
     held = gate_proj.shape[0]
     width = gate_proj.shape[1] // chunks
     tokens = sum(x.shape[0] for x in xs)
-    slots = token_at.shape[0] // held
+    slots = token_at.shape[1]
     units = gate_proj.shape[2]
     first, last = k == 0, k == chunks - 1
     vmem = pl.BlockSpec(memory_space=pltpu.VMEM)
@@ -412,17 +463,18 @@
         in_specs += [vmem] * 2
         args += list(sums)
     if last:
-        in_specs += [vmem] * 3
-        args += list(extras)
+        in_specs += [vmem, pl.BlockSpec(memory_space=pltpu.SMEM)]
+        args += [place, e0]
         out_shape = (
             jax.ShapeDtypeStruct((held, slots, units), BF),
             jax.ShapeDtypeStruct((held, tokens, slots), BF),
         )
-        scratch.append(pltpu.VMEM((slots, extras[0].shape[1]), F32))
+        lanes = gate_lanes(experts)
+        scratch += [pltpu.VMEM((slots, lanes), F32), pltpu.VMEM((tokens, lanes), F32)]
     else:
         out_shape = (jax.ShapeDtypeStruct((held, slots, units), F32),) * 2
     return pl.pallas_call(
-        functools.partial(up_body, first, last, k * width, len(xs), width),
+        functools.partial(up_body, first, last, k * width, len(xs), width, experts),
         in_specs=in_specs,
         out_specs=(vmem, vmem),
         out_shape=out_shape,
@@ -520,7 +572,7 @@
     head_at = lax.axis_index("head")
     y_at, c_at = head_at // cores, head_at % cores
     device = head_at * reqs + lax.axis_index("req")
-    e0 = (device * held) % experts
+    e0 = ((device * held) % experts).reshape(1).astype(jnp.int32)
 
     states = write_vec.shape[2]
     early = jnp.concatenate(
@@ -564,7 +616,6 @@
         m = k * MIX_CHUNKS // AG_CHUNKS
         local = slice(k * span - m * part_span, (k + 1) * span - m * part_span)
         payload = (mixes[m][:, local].astype(F32) * norm_gain[cut]).astype(BF)
-        extras = None
         if k == AG_CHUNKS - 1:
             extra = gates(after_mixer, norm_gain, router, named)
             payload = jnp.concatenate([payload, extra], axis=1)
@@ -577,23 +628,8 @@
         if cores > 1:
             xs.append(ring.shift(rows, dc=1))
         if k == 0:
-            named_all = jnp.concatenate([x[:, span : span + experts] for x in xs], axis=0)
-            mine = lax.dynamic_slice_in_dim(named_all, e0, held, axis=1)
-            order = jnp.arange(all_tokens, dtype=jnp.int32)
-            before = (order[:, None] > order[None, :]).astype(BF)
-            rank = jnp.dot(before, mine, preferred_element_type=F32)
-            place = jnp.where(mine > 0, rank, -1.0).astype(jnp.int32)
-            spots = jnp.arange(room, dtype=jnp.int32)
-            chosen = place.T[:, None, :] == spots[None, :, None]
-            token_at = jnp.sum(jnp.where(chosen, order, 0), axis=2).reshape(-1)
-        if k == AG_CHUNKS - 1:
-            tail = rows.shape[1] - gate_lanes(experts)
-            extra = jnp.concatenate([x[:, tail:] for x in xs], axis=0).astype(F32)
-            share = lax.dynamic_slice_in_dim(
-                extra, e0 + extra.shape[1] - experts, held, axis=1
-            )
-            extras = (extra, place, share)
-        sums = expert_up(k, AG_CHUNKS, token_at, xs, gate_proj, up_proj, sums, extras)
+            token_at, place = places(e0, xs, span, held, room)
+        sums = expert_up(k, AG_CHUNKS, experts, token_at, xs, gate_proj, up_proj, sums, place, e0)
     act, comb = sums
 
     pieces = []

time: 178 us -> 169 us (0.949)
  starting transfers between devices: 39.6 us -> 36 us
  other arithmetic: 7.03 us -> 3.43 us
  local copies, waits for them, and re-layouts: 2.97 us -> 0.35 us
    ppermute x38, starting transfers between devices: 39.6 us -> 36 us  [shift(): return lax.ppermute(x, AXES, self.pairs(**how))]
    another operation x11, other arithmetic: 4.44 us -> 1.12 us  [gather(): return jnp.stack([x] + moved)]
  transfers between devices with their start and end apart: 38 -> 38, of which waited for: 22 -> 21; matrix products, arithmetic and copies ran while one was open for 4% -> 1% of each run, Pallas kernels for 20% -> 26%
where the time goes in v3:
time: 169 us
  waiting for transfers between devices  66.6 us (39%)
  Pallas kernels  61.8 us (37%)
  starting transfers between devices  36 us (21%)
  other arithmetic  3.43 us (2%)
    ppermute x38, waiting for transfers between devices, shift(): return lax.ppermute(x, AXES, self.pairs(**how))  66.6 us
    ppermute x38, starting transfers between devices, shift(): return lax.ppermute(x, AXES, self.pairs(**how))  36 us
    pallas_call x4, Pallas kernels, expert_up(): pl.pallas_call(functools.partial(up_body, first, last, k * width, len(xs)...  30.1 us
    pallas_call x4, Pallas kernels, expert_down(): pl.pallas_call(functools.partial(down_body, k * width), in_specs=[vmem, v...  19.3 us
    pallas_call x1, Pallas kernels, front(): pl.pallas_call(functools.partial(front_body, heads, part * span), grid_sp...  5.82 us
  transfers between devices with their start and end apart: 38, of which 21 were waited for; matrix products, arithmetic and copies ran while one was open for 1% of the time, Pallas kernels for 26%

profile of v3, /device:TPU:0, one launch (start us, length us, event | category | flops | bytes accessed | tf_op | source)
XLA Modules:
  0.0 168.8 jit_solution(15143403097035067037)
XLA Ops:
  1.2 0.8 collective-permute-done
  2.1 2.8 %collective-permute-start.1 = (bf16[2,32,256]{2,1,0:T(8,128)(2,1)S(1)}, bf16[2,32,256]{2,1,0:T(8,128)(2,1)S(1)}, u32[]{:S(2)}, u32[]{:S(2)}) collective-permute-start(bf16[2,32,256]{2,1,0:T(8,128)(2,1)S(1)} %get-tuple-element.88), channel_id=1, source_target_pairs={{0,8},{1,9},{2,10},{3,11},{4,12},{5,13},{6,14},{7,15},{8,0},{9,1},... | collective-permute-start | bytes 98312 | tf_op jit(solution)/shard_map/ppermute | solution.py:41
  4.9 2.4 %prepare.1 = (f32[16,128,128]{2,1,0:T(8,128)S(1)}, f32[128,16]{1,0:T(8,128)S(1)}, bf16[32,128]{1,0:T(8,128)(2,1)S(1)}) custom-call(s32[8,16]{1,0:T(8,128)} %parents.1, s32[4,8,10]{2,1,0:T(8,128)} %ids.1, f32[16,8,16]{2,1,0:T(8,128)} %step_raw.1, f32[1,16]{1,0:T(1,128)} %bitcast.121, f32[1,16]{1,0:T(1,128)} %bitcast.122), custom_call_target="tpu_custom_call" | custom-call | tf_op jit(solution)/shard_map/prepare/pallas_call | solution.py:123
  7.4 5.8 %front.1 = (f32[64,2048]{1,0:T(8,128)S(1)}, bf16[64,2048]{1,0:T(8,128)(2,1)S(1)}, bf16[128,1024]{1,0:T(8,128)(2,1)S(1)}) custom-call(s32[4]{0:T(128)S(1)} %get-tuple-element.95.slot_of, s32[4]{0:T(128)S(1)} %get-tuple-element.96.goes_to, bf16[4,32,256]{2,1,0:T(8,128)(2,1)S(1)} %bitcast.91, bf16[16,8,1024]{2,1,0:T(8,128)(2,1)} %x.1, ...), custom_call_target="tpu_custom_call" | custom-call | flops 536870912 | bytes 4194304 | tf_op jit(solution)/shard_map/front/pallas_call | solution.py:263
  13.3 2.5 %project.1 = (f32[64,2048]{1,0:T(8,128)S(1)}, bf16[64,2048]{1,0:T(8,128)(2,1)S(1)}) custom-call(bf16[128,1024]{1,0:T(8,128)(2,1)S(1)} %get-tuple-element.37.rows, bf16[1024,4096]{1,0:T(8,128)(2,1)} %weight.3), custom_call_target="tpu_custom_call" | custom-call | flops 536870912 | bytes 4194304 | tf_op jit(solution)/shard_map/project/pallas_call | solution.py:302
  16.5 1.5 collective-permute-start.3
  18.1 1.1 collective-permute-start.9
  19.2 3.8 %collective-permute-done.3 = bf16[32,2048]{1,0:T(8,128)(2,1)S(1)} collective-permute-done((bf16[32,2048]{1,0:T(8,128)(2,1)S(1)}, bf16[32,2048]{1,0:T(8,128)(2,1)S(1)}, u32[]{:S(2)}, u32[]{:S(2)}) %collective-permute-start.3) | collective-permute-done | bytes 131104 | tf_op jit(solution)/shard_map/ppermute | solution.py:41
  22.9 1.9 %collective-permute-done.9 = bf16[32,2048]{1,0:T(8,128)(2,1)S(1)} collective-permute-done((bf16[32,2048]{1,0:T(8,128)(2,1)S(1)}, bf16[32,2048]{1,0:T(8,128)(2,1)S(1)}, u32[]{:S(2)}, u32[]{:S(2)}) %collective-permute-start.9) | collective-permute-done | bytes 131104 | tf_op jit(solution)/shard_map/ppermute | solution.py:41
  25.0 2.7 %collective-permute-start.4 = (bf16[32,1152]{1,0:T(8,128)(2,1)S(1)}, bf16[32,1152]{1,0:T(8,128)(2,1)S(1)}, u32[]{:S(2)}, u32[]{:S(2)}) collective-permute-start(bf16[32,1152]{1,0:T(8,128)(2,1)S(1)} %get-tuple-element.86), channel_id=1, source_target_pairs={{0,2},{1,3},{2,0},{3,1},{4,6},{5,7},{6,4},{7,5},{8,10},{9,11},{10,... | collective-permute-start | bytes 221192 | tf_op jit(solution)/shard_map/ppermute | solution.py:41
  28.0 2.7 %collective-permute-start.14 = (bf16[32,1024]{1,0:T(8,128)(2,1)S(1)}, bf16[32,1024]{1,0:T(8,128)(2,1)S(1)}, u32[]{:S(2)}, u32[]{:S(2)}) collective-permute-start(bf16[32,1024]{1,0:T(8,128)(2,1)S(1)} %get-tuple-element.81), channel_id=1, source_target_pairs={{0,2},{1,3},{2,0},{3,1},{4,6},{5,7},{6,4},{7,5},{8,10},{9,11},{10,... | collective-permute-start | bytes 196616 | tf_op jit(solution)/shard_map/ppermute | solution.py:41
  31.7 4.7 %collective-permute-done.18 = bf16[32,1024]{1,0:T(8,128)(2,1)S(1)} collective-permute-done((bf16[32,1024]{1,0:T(8,128)(2,1)S(1)}, bf16[32,1024]{1,0:T(8,128)(2,1)S(1)}, u32[]{:S(2)}, u32[]{:S(2)}) %collective-permute-start.18) | collective-permute-done | bytes 65568 | tf_op jit(solution)/shard_map/ppermute | solution.py:41
  36.4 1.3 collective-permute-start.19
  37.7 0.9 collective-permute-done.14
  39.2 1.7 collective-permute-start.5
  41.4 1.5 collective-permute-done.19
  42.9 1.5 collective-permute-start.20
  44.4 4.4 %collective-permute-done.5 = bf16[2,32,1152]{2,1,0:T(8,128)(2,1)S(1)} collective-permute-done((bf16[2,32,1152]{2,1,0:T(8,128)(2,1)S(1)}, bf16[2,32,1152]{2,1,0:T(8,128)(2,1)S(1)}, u32[]{:S(2)}, u32[]{:S(2)}) %collective-permute-start.5) | collective-permute-done | bytes 147488 | tf_op jit(solution)/shard_map/ppermute | solution.py:41
  48.9 1.5 collective-permute-start.6
  51.1 0.7 collective-permute-done.11
  51.9 1.5 collective-permute-start.12
  53.4 5.4 %collective-permute-done.6 = bf16[2,2,32,1152]{3,2,1,0:T(8,128)(2,1)S(1)} collective-permute-done((bf16[2,2,32,1152]{3,2,1,0:T(8,128)(2,1)S(1)}, bf16[2,2,32,1152]{3,2,1,0:T(8,128)(2,1)S(1)}, u32[]{:S(2)}, u32[]{:S(2)}) %collective-permute-start.6) | collective-permute-done | bytes 294944 | tf_op jit(solution)/shard_map/ppermute | solution.py:41
  59.6 4.9 %collective-permute-done.16 = bf16[2,2,32,1024]{3,2,1,0:T(8,128)(2,1)S(1)} collective-permute-done((bf16[2,2,32,1024]{3,2,1,0:T(8,128)(2,1)S(1)}, bf16[2,2,32,1024]{3,2,1,0:T(8,128)(2,1)S(1)}, u32[]{:S(2)}, u32[]{:S(2)}) %collective-permute-start.16) | collective-permute-done | bytes 262176 | tf_op jit(solution)/shard_map/ppermute | solution.py:41
  64.6 5.0 %collective-permute-done.12 = bf16[2,2,32,1152]{3,2,1,0:T(8,128)(2,1)S(1)} collective-permute-done((bf16[2,2,32,1152]{3,2,1,0:T(8,128)(2,1)S(1)}, bf16[2,2,32,1152]{3,2,1,0:T(8,128)(2,1)S(1)}, u32[]{:S(2)}, u32[]{:S(2)}) %collective-permute-start.12) | collective-permute-done | bytes 294944 | tf_op jit(solution)/shard_map/ppermute | solution.py:41
  69.7 1.1 places.1
  70.8 7.0 %shard_map.163 = (f32[8,128,384]{2,1,0:T(8,128)S(1)}, f32[8,128,384]{2,1,0:T(8,128)S(1)}) custom-call(s32[8,128]{1,0:T(8,128)S(1)} %get-tuple-element.36.token_at, bf16[256,1152]{1,0:T(8,128)(2,1)S(1)} %bitcast.83, bf16[256,1152]{1,0:T(8,128)(2,1)S(1)} %collective-permute-done.7.rest_1_, bf16[8,4096,384]{2,1,0:T(8,128)(2,1)} %rest_2_.7, ...), custom_call_target="tpu_custom_call" | custom-call | flops 1610612736 | bytes 12582912 | tf_op jit(solution)/shard_map/pallas_call | solution.py:476
  77.8 7.5 %shard_map.164 = (f32[8,128,384]{2,1,0:T(8,128)S(1)}, f32[8,128,384]{2,1,0:T(8,128)S(1)}) custom-call(s32[8,128]{1,0:T(8,128)S(1)} %get-tuple-element.36.token_at, bf16[256,1024]{1,0:T(8,128)(2,1)S(1)} %bitcast.87, bf16[256,1024]{1,0:T(8,128)(2,1)} %collective-permute-done.21.rest_1_, ...), custom_call_target="tpu_custom_call", output_to_operand_aliasing={{0}: (5, {}), {1}: (6, {})} | custom-call | flops 1610612736 | bytes 12582912 | tf_op jit(solution)/shard_map/pallas_call | solution.py:476
  85.4 7.5 %shard_map.165 = (f32[8,128,384]{2,1,0:T(8,128)S(1)}, f32[8,128,384]{2,1,0:T(8,128)S(1)}) custom-call(s32[8,128]{1,0:T(8,128)S(1)} %get-tuple-element.36.token_at, bf16[256,1024]{1,0:T(8,128)(2,1)S(1)} %bitcast.89, bf16[256,1024]{1,0:T(8,128)(2,1)} %collective-permute-done.17.rest_1_, ...), custom_call_target="tpu_custom_call", output_to_operand_aliasing={{0}: (5, {}), {1}: (6, {})} | custom-call | flops 1610612736 | bytes 12582912 | tf_op jit(solution)/shard_map/pallas_call | solution.py:476
  92.9 8.1 %shard_map.166 = (bf16[8,128,384]{2,1,0:T(8,128)(2,1)S(1)}, bf16[8,512,128]{2,1,0:T(8,128)(2,1)S(1)}) custom-call(s32[8,128]{1,0:T(8,128)S(1)} %get-tuple-element.36.token_at, bf16[256,1152]{1,0:T(8,128)(2,1)S(1)} %bitcast.85, bf16[256,1152]{1,0:T(8,128)(2,1)S(1)} %collective-permute-done.13.rest_1_, bf16[8,4096,384]{2,1,0:T(8,128)(2,1)} %rest_2_.7, ...), custom_call_target="tpu_custom_call" | custom-call | flops 1610612736 | bytes 12582912 | tf_op jit(solution)/shard_map/pallas_call | solution.py:476
  101.0 4.8 %shard_map.168 = (f32[256,1024]{1,0:T(8,128)S(1)}, bf16[256,1024]{1,0:T(8,128)(2,1)S(1)}) custom-call(bf16[8,128,384]{2,1,0:T(8,128)(2,1)S(1)} %get-tuple-element.47.act, bf16[8,512,128]{2,1,0:T(8,128)(2,1)S(1)} %get-tuple-element.48.comb, bf16[8,384,4096]{2,1,0:T(8,128)(2,1)} %wd.7), custom_call_target="tpu_custom_call" | custom-call | flops 1879048192 | bytes 6291456 | tf_op jit(solution)/shard_map/pallas_call | solution.py:523
  106.4 4.8 %shard_map.167 = (f32[256,1024]{1,0:T(8,128)S(1)}, bf16[256,1024]{1,0:T(8,128)(2,1)S(1)}) custom-call(bf16[8,128,384]{2,1,0:T(8,128)(2,1)S(1)} %get-tuple-element.47.act, bf16[8,512,128]{2,1,0:T(8,128)(2,1)S(1)} %get-tuple-element.48.comb, bf16[8,384,4096]{2,1,0:T(8,128)(2,1)} %wd.7), custom_call_target="tpu_custom_call" | custom-call | flops 1879048192 | bytes 6291456 | tf_op jit(solution)/shard_map/pallas_call | solution.py:523
  111.3 4.8 %shard_map.170 = (f32[256,1024]{1,0:T(8,128)S(1)}, bf16[256,1024]{1,0:T(8,128)(2,1)S(1)}) custom-call(bf16[8,128,384]{2,1,0:T(8,128)(2,1)S(1)} %get-tuple-element.47.act, bf16[8,512,128]{2,1,0:T(8,128)(2,1)S(1)} %get-tuple-element.48.comb, bf16[8,384,4096]{2,1,0:T(8,128)(2,1)} %wd.7), custom_call_target="tpu_custom_call" | custom-call | flops 1879048192 | bytes 6291456 | tf_op jit(solution)/shard_map/pallas_call | solution.py:523
  116.7 4.8 %shard_map.169 = (f32[256,1024]{1,0:T(8,128)S(1)}, bf16[256,1024]{1,0:T(8,128)(2,1)S(1)}) custom-call(bf16[8,128,384]{2,1,0:T(8,128)(2,1)S(1)} %get-tuple-element.47.act, bf16[8,512,128]{2,1,0:T(8,128)(2,1)S(1)} %get-tuple-element.48.comb, bf16[8,384,4096]{2,1,0:T(8,128)(2,1)} %wd.7), custom_call_target="tpu_custom_call" | custom-call | flops 1879048192 | bytes 6291456 | tf_op jit(solution)/shard_map/pallas_call | solution.py:523
  121.9 1.5 collective-permute-start.27
  124.5 1.5 collective-permute-start.35
  126.9 4.2 %collective-permute-done.27 = bf16[128,1024]{1,0:T(8,128)(2,1)S(1)} collective-permute-done((bf16[128,1024]{1,0:T(8,128)(2,1)S(1)}, bf16[128,1024]{1,0:T(8,128)(2,1)S(1)}, u32[]{:S(2)}, u32[]{:S(2)}) %collective-permute-start.27) | collective-permute-done | bytes 262176 | tf_op jit(solution)/shard_map/ppermute | solution.py:41
  131.2 5.5 %collective-permute-done.23 = bf16[128,1024]{1,0:T(8,128)(2,1)S(1)} collective-permute-done((bf16[128,1024]{1,0:T(8,128)(2,1)S(1)}, bf16[128,1024]{1,0:T(8,128)(2,1)S(1)}, u32[]{:S(2)}, u32[]{:S(2)}) %collective-permute-start.23) | collective-permute-done | bytes 262176 | tf_op jit(solution)/shard_map/ppermute | solution.py:41
  136.9 5.5 %collective-permute-done.35 = bf16[128,1024]{1,0:T(8,128)(2,1)S(1)} collective-permute-done((bf16[128,1024]{1,0:T(8,128)(2,1)S(1)}, bf16[128,1024]{1,0:T(8,128)(2,1)S(1)}, u32[]{:S(2)}, u32[]{:S(2)}) %collective-permute-start.35) | collective-permute-done | bytes 262176 | tf_op jit(solution)/shard_map/ppermute | solution.py:41
  142.6 4.9 %collective-permute-done.31 = bf16[128,1024]{1,0:T(8,128)(2,1)S(1)} collective-permute-done((bf16[128,1024]{1,0:T(8,128)(2,1)S(1)}, bf16[128,1024]{1,0:T(8,128)(2,1)S(1)}, u32[]{:S(2)}, u32[]{:S(2)}) %collective-permute-start.31) | collective-permute-done | bytes 262176 | tf_op jit(solution)/shard_map/ppermute | solution.py:41
  147.7 2.0 %collective-permute-start.36 = (bf16[2,32,1024]{2,1,0:T(8,128)(2,1)S(1)}, bf16[2,32,1024]{2,1,0:T(8,128)(2,1)S(1)}, u32[]{:S(2)}, u32[]{:S(2)}) collective-permute-start(bf16[2,32,1024]{2,1,0:T(8,128)(2,1)S(1)} %bitcast.107), channel_id=1, source_target_pairs={{0,1},{1,0},{2,3},{3,2},{4,5},{5,4},{6,7},{7,6},{8,9},{9,8},{10,11... | collective-permute-start | bytes 393224 | tf_op jit(solution)/shard_map/ppermute | solution.py:41
  149.8 2.9 %collective-permute-start.29 = (bf16[1,32,1024]{2,1,0:T(8,128)(2,1)S(1)}, bf16[1,32,1024]{2,1,0:T(8,128)(2,1)S(1)}, u32[]{:S(2)}, u32[]{:S(2)}) collective-permute-start(bf16[1,32,1024]{2,1,0:T(8,128)(2,1)S(1)} %slice.306), channel_id=1, source_target_pairs={{0,2},{1,3},{2,0},{3,1},{4,6},{5,7},{6,4},{7,5},{8,10},{9,11},{10,... | collective-permute-start | bytes 196616 | tf_op jit(solution)/shard_map/ppermute | solution.py:41
  152.8 3.4 %collective-permute-done.24 = bf16[2,32,1024]{2,1,0:T(8,128)(2,1)S(1)} collective-permute-done((bf16[2,32,1024]{2,1,0:T(8,128)(2,1)S(1)}, bf16[2,32,1024]{2,1,0:T(8,128)(2,1)S(1)}, u32[]{:S(2)}, u32[]{:S(2)}) %collective-permute-start.24) | collective-permute-done | bytes 131104 | tf_op jit(solution)/shard_map/ppermute | solution.py:41
  156.8 2.2 %collective-permute-done.36 = bf16[2,32,1024]{2,1,0:T(8,128)(2,1)S(1)} collective-permute-done((bf16[2,32,1024]{2,1,0:T(8,128)(2,1)S(1)}, bf16[2,32,1024]{2,1,0:T(8,128)(2,1)S(1)}, u32[]{:S(2)}, u32[]{:S(2)}) %collective-permute-start.36) | collective-permute-done | bytes 131104 | tf_op jit(solution)/shard_map/ppermute | solution.py:41
  159.6 1.0 collective-permute-done.32
  160.6 1.5 collective-permute-start.33
  162.1 3.2 %collective-permute-done.25 = bf16[1,32,1024]{2,1,0:T(8,128)(2,1)S(1)} collective-permute-done((bf16[1,32,1024]{2,1,0:T(8,128)(2,1)S(1)}, bf16[1,32,1024]{2,1,0:T(8,128)(2,1)S(1)}, u32[]{:S(2)}, u32[]{:S(2)}) %collective-permute-start.25) | collective-permute-done | bytes 65568 | tf_op jit(solution)/shard_map/ppermute | solution.py:41
  165.4 1.9 %collective-permute-done.37 = bf16[1,32,1024]{2,1,0:T(8,128)(2,1)S(1)} collective-permute-done((bf16[1,32,1024]{2,1,0:T(8,128)(2,1)S(1)}, bf16[1,32,1024]{2,1,0:T(8,128)(2,1)S(1)}, u32[]{:S(2)}, u32[]{:S(2)}) %collective-permute-start.37) | collective-permute-done | bytes 65568 | tf_op jit(solution)/shard_map/ppermute | solution.py:41
  168.1 0.7 maximum_bitcast_fusion
  (116 shorter events, 12.6 us)
Async XLA Ops:
  0.7 1.3 collective-permute-start
  2.1 5.3 %collective-permute-start.1 = (bf16[2,32,256]{2,1,0:T(8,128)(2,1)S(1)}, bf16[2,32,256]{2,1,0:T(8,128)(2,1)S(1)}, u32[]{:S(2)}, u32[]{:S(2)}) collective-permute-start(bf16[2,32,256]{2,1,0:T(8,128)(2,1)S(1)} %get-tuple-element.88), channel_id=1, source_target_pairs={{0,8},{1,9},{2,10},{3,11},{4,12},{5,13},{6,14},{7,15},{8,0},{9,1},... | collective-permute-start | bytes 98312 | tf_op jit(solution)/shard_map/ppermute | solution.py:41
  13.2 3.2 %collective-permute-start.2 = (bf16[64,2048]{1,0:T(8,128)(2,1)S(1)}, bf16[64,2048]{1,0:T(8,128)(2,1)S(1)}, u32[]{:S(2)}, u32[]{:S(2)}) collective-permute-start(bf16[64,2048]{1,0:T(8,128)(2,1)S(1)} %get-tuple-element.34), channel_id=1, source_target_pairs={{0,4},{1,5},{2,6},{3,7},{4,0},{5,1},{6,2},{7,3},{8,12},{9,13},{10,... | collective-permute-start | bytes 786440 | tf_op jit(solution)/shard_map/ppermute | solution.py:41
  15.8 2.2 %collective-permute-start.8 = (bf16[64,2048]{1,0:T(8,128)(2,1)S(1)}, bf16[64,2048]{1,0:T(8,128)(2,1)S(1)}, u32[]{:S(2)}, u32[]{:S(2)}) collective-permute-start(bf16[64,2048]{1,0:T(8,128)(2,1)S(1)} %get-tuple-element.39), channel_id=1, source_target_pairs={{0,4},{1,5},{2,6},{3,7},{4,0},{5,1},{6,2},{7,3},{8,12},{9,13},{10,... | collective-permute-start | bytes 786440 | tf_op jit(solution)/shard_map/ppermute | solution.py:41
  16.4 2.8 %copy-start.1 = (f32[4096]{0:T(1024)S(1)}, f32[4096]{0:T(1024)}, u32[]{:S(2)}) copy-start(f32[4096]{0:T(1024)} %param.28) | copy-start | bytes 49156
  16.4 8.4 %copy-start.6 = (bf16[4,8,4096]{2,1,0:T(8,128)(2,1)S(1)}, bf16[4,8,4096]{2,1,0:T(8,128)(2,1)}, u32[]{:S(2)}) copy-start(bf16[4,8,4096]{2,1,0:T(8,128)(2,1)} %param.27) | copy-start | bytes 786436
  16.5 6.4 %collective-permute-start.3 = (bf16[32,2048]{1,0:T(8,128)(2,1)S(1)}, bf16[32,2048]{1,0:T(8,128)(2,1)S(1)}, u32[]{:S(2)}, u32[]{:S(2)}) collective-permute-start(bf16[32,2048]{1,0:T(8,128)(2,1)S(1)} %slice.303), channel_id=1, source_target_pairs={{0,8},{1,9},{2,10},{3,11},{4,12},{5,13},{6,14},{7,15},{8,0},{9,1},... | collective-permute-start | bytes 393224 | tf_op jit(solution)/shard_map/ppermute | solution.py:41
  18.1 12.6 %copy-start = (bf16[4096,64]{0,1:T(8,128)(2,1)S(1)}, bf16[4096,64]{0,1:T(8,128)(2,1)}, u32[]{:S(2)}) copy-start(bf16[4096,64]{0,1:T(8,128)(2,1)} %param.29) | copy-start | bytes 1572868
  18.1 6.7 %collective-permute-start.9 = (bf16[32,2048]{1,0:T(8,128)(2,1)S(1)}, bf16[32,2048]{1,0:T(8,128)(2,1)S(1)}, u32[]{:S(2)}, u32[]{:S(2)}) collective-permute-start(bf16[32,2048]{1,0:T(8,128)(2,1)S(1)} %slice.302), channel_id=1, source_target_pairs={{0,8},{1,9},{2,10},{3,11},{4,12},{5,13},{6,14},{7,15},{8,0},{9,1},... | collective-permute-start | bytes 393224 | tf_op jit(solution)/shard_map/ppermute | solution.py:41
  24.9 13.7 %copy-start.2 = (bf16[32,2048]{1,0:T(8,128)(2,1)}, bf16[32,2048]{1,0:T(8,128)(2,1)S(1)}, u32[]{:S(2)}) copy-start(bf16[32,2048]{1,0:T(8,128)(2,1)S(1)} %get-tuple-element.66) | copy-start | bytes 393220
  25.0 14.2 %collective-permute-start.4 = (bf16[32,1152]{1,0:T(8,128)(2,1)S(1)}, bf16[32,1152]{1,0:T(8,128)(2,1)S(1)}, u32[]{:S(2)}, u32[]{:S(2)}) collective-permute-start(bf16[32,1152]{1,0:T(8,128)(2,1)S(1)} %get-tuple-element.86), channel_id=1, source_target_pairs={{0,2},{1,3},{2,0},{3,1},{4,6},{5,7},{6,4},{7,5},{8,10},{9,11},{10,... | collective-permute-start | bytes 221192 | tf_op jit(solution)/shard_map/ppermute | solution.py:41
  27.6 8.8 %collective-permute-start.18 = (bf16[32,1024]{1,0:T(8,128)(2,1)S(1)}, bf16[32,1024]{1,0:T(8,128)(2,1)S(1)}, u32[]{:S(2)}, u32[]{:S(2)}) collective-permute-start(bf16[32,1024]{1,0:T(8,128)(2,1)S(1)} %get-tuple-element.77), channel_id=1, source_target_pairs={{0,2},{1,3},{2,0},{3,1},{4,6},{5,7},{6,4},{7,5},{8,10},{9,11},{10,... | collective-permute-start | bytes 196616 | tf_op jit(solution)/shard_map/ppermute | solution.py:41
  28.0 10.6 %collective-permute-start.14 = (bf16[32,1024]{1,0:T(8,128)(2,1)S(1)}, bf16[32,1024]{1,0:T(8,128)(2,1)S(1)}, u32[]{:S(2)}, u32[]{:S(2)}) collective-permute-start(bf16[32,1024]{1,0:T(8,128)(2,1)S(1)} %get-tuple-element.81), channel_id=1, source_target_pairs={{0,2},{1,3},{2,0},{3,1},{4,6},{5,7},{6,4},{7,5},{8,10},{9,11},{10,... | collective-permute-start | bytes 196616 | tf_op jit(solution)/shard_map/ppermute | solution.py:41
  31.3 9.6 %collective-permute-start.10 = (bf16[32,1152]{1,0:T(8,128)(2,1)S(1)}, bf16[32,1152]{1,0:T(8,128)(2,1)S(1)}, u32[]{:S(2)}, u32[]{:S(2)}) collective-permute-start(bf16[32,1152]{1,0:T(8,128)(2,1)S(1)} %get-tuple-element.84), channel_id=1, source_target_pairs={{0,2},{1,3},{2,0},{3,1},{4,6},{5,7},{6,4},{7,5},{8,10},{9,11},{10,... | collective-permute-start | bytes 221192 | tf_op jit(solution)/shard_map/ppermute | solution.py:41
  36.4 6.4 %collective-permute-start.19 = (bf16[2,32,1024]{2,1,0:T(8,128)(2,1)S(1)}, bf16[2,32,1024]{2,1,0:T(8,128)(2,1)S(1)}, u32[]{:S(2)}, u32[]{:S(2)}) collective-permute-start(bf16[2,32,1024]{2,1,0:T(8,128)(2,1)S(1)} %get-tuple-element.76), channel_id=1, source_target_pairs={{0,1},{1,0},{2,3},{3,2},{4,5},{5,4},{6,7},{7,6},{8,9},{9,8},{10,11... | collective-permute-start | bytes 393224 | tf_op jit(solution)/shard_map/ppermute | solution.py:41
  38.6 11.8 %collective-permute-start.15 = (bf16[2,32,1024]{2,1,0:T(8,128)(2,1)S(1)}, bf16[2,32,1024]{2,1,0:T(8,128)(2,1)S(1)}, u32[]{:S(2)}, u32[]{:S(2)}) collective-permute-start(bf16[2,32,1024]{2,1,0:T(8,128)(2,1)S(1)} %get-tuple-element.80), channel_id=1, source_target_pairs={{0,1},{1,0},{2,3},{3,2},{4,5},{5,4},{6,7},{7,6},{8,9},{9,8},{10,11... | collective-permute-start | bytes 393224 | tf_op jit(solution)/shard_map/ppermute | solution.py:41
  39.2 9.7 %collective-permute-start.5 = (bf16[2,32,1152]{2,1,0:T(8,128)(2,1)S(1)}, bf16[2,32,1152]{2,1,0:T(8,128)(2,1)S(1)}, u32[]{:S(2)}, u32[]{:S(2)}) collective-permute-start(bf16[2,32,1152]{2,1,0:T(8,128)(2,1)S(1)} %get-tuple-element.70), channel_id=1, source_target_pairs={{0,1},{1,0},{2,3},{3,2},{4,5},{5,4},{6,7},{7,6},{8,9},{9,8},{10,11... | collective-permute-start | bytes 442376 | tf_op jit(solution)/shard_map/ppermute | solution.py:41
  40.9 11.0 %collective-permute-start.11 = (bf16[2,32,1152]{2,1,0:T(8,128)(2,1)S(1)}, bf16[2,32,1152]{2,1,0:T(8,128)(2,1)S(1)}, u32[]{:S(2)}, u32[]{:S(2)}) collective-permute-start(bf16[2,32,1152]{2,1,0:T(8,128)(2,1)S(1)} %get-tuple-element.68), channel_id=1, source_target_pairs={{0,1},{1,0},{2,3},{3,2},{4,5},{5,4},{6,7},{7,6},{8,9},{9,8},{10,11... | collective-permute-start | bytes 442376 | tf_op jit(solution)/shard_map/ppermute | solution.py:41
  42.9 16.1 %collective-permute-start.20 = (bf16[2,2,32,1024]{3,2,1,0:T(8,128)(2,1)S(1)}, bf16[2,2,32,1024]{3,2,1,0:T(8,128)(2,1)S(1)}, u32[]{:S(2)}, u32[]{:S(2)}) collective-permute-start(bf16[2,2,32,1024]{3,2,1,0:T(8,128)(2,1)S(1)} %get-tuple-element.62), channel_id=1, source_target_pairs={{0,8},{1,9},{2,10},{3,11},{4,12},{5,13},{6,14},{7,15},{8,0},{9,1},... | collective-permute-start | bytes 786440 | tf_op jit(solution)/shard_map/ppermute | solution.py:41
  48.9 9.9 %collective-permute-start.6 = (bf16[2,2,32,1152]{3,2,1,0:T(8,128)(2,1)S(1)}, bf16[2,2,32,1152]{3,2,1,0:T(8,128)(2,1)S(1)}, u32[]{:S(2)}, u32[]{:S(2)}) collective-permute-start(bf16[2,2,32,1152]{3,2,1,0:T(8,128)(2,1)S(1)} %get-tuple-element.60), channel_id=1, source_target_pairs={{0,8},{1,9},{2,10},{3,11},{4,12},{5,13},{6,14},{7,15},{8,0},{9,1},... | collective-permute-start | bytes 884744 | tf_op jit(solution)/shard_map/ppermute | solution.py:41
  50.5 14.0 %collective-permute-start.16 = (bf16[2,2,32,1024]{3,2,1,0:T(8,128)(2,1)S(1)}, bf16[2,2,32,1024]{3,2,1,0:T(8,128)(2,1)S(1)}, u32[]{:S(2)}, u32[]{:S(2)}) collective-permute-start(bf16[2,2,32,1024]{3,2,1,0:T(8,128)(2,1)S(1)} %get-tuple-element.64), channel_id=1, source_target_pairs={{0,8},{1,9},{2,10},{3,11},{4,12},{5,13},{6,14},{7,15},{8,0},{9,1},... | collective-permute-start | bytes 786440 | tf_op jit(solution)/shard_map/ppermute | solution.py:41
  51.9 17.7 %collective-permute-start.12 = (bf16[2,2,32,1152]{3,2,1,0:T(8,128)(2,1)S(1)}, bf16[2,2,32,1152]{3,2,1,0:T(8,128)(2,1)S(1)}, u32[]{:S(2)}, u32[]{:S(2)}) collective-permute-start(bf16[2,2,32,1152]{3,2,1,0:T(8,128)(2,1)S(1)} %get-tuple-element.58), channel_id=1, source_target_pairs={{0,8},{1,9},{2,10},{3,11},{4,12},{5,13},{6,14},{7,15},{8,0},{9,1},... | collective-permute-start | bytes 884744 | tf_op jit(solution)/shard_map/ppermute | solution.py:41
  58.9 10.8 %collective-permute-start.7 = (bf16[256,1152]{1,0:T(8,128)(2,1)S(1)}, bf16[256,1152]{1,0:T(8,128)(2,1)S(1)}, u32[]{:S(2)}, u32[]{:S(2)}) collective-permute-start(bf16[256,1152]{1,0:T(8,128)(2,1)S(1)} %bitcast.81), channel_id=1, source_target_pairs={{0,4},{1,5},{2,6},{3,7},{4,0},{5,1},{6,2},{7,3},{8,12},{9,13},{10,... | collective-permute-start | bytes 1769480 | tf_op jit(solution)/shard_map/ppermute | solution.py:41
  59.0 18.8 %collective-permute-start.21 = (bf16[256,1024]{1,0:T(8,128)(2,1)S(1)}, bf16[256,1024]{1,0:T(8,128)(2,1)}, u32[]{:S(2)}, u32[]{:S(2)}) collective-permute-start(bf16[256,1024]{1,0:T(8,128)(2,1)S(1)} %bitcast.86), channel_id=1, source_target_pairs={{0,4},{1,5},{2,6},{3,7},{4,0},{5,1},{6,2},{7,3},{8,12},{9,13},{10,... | collective-permute-start | bytes 1572872 | tf_op jit(solution)/shard_map/ppermute | solution.py:41
  64.5 20.8 %collective-permute-start.17 = (bf16[256,1024]{1,0:T(8,128)(2,1)S(1)}, bf16[256,1024]{1,0:T(8,128)(2,1)}, u32[]{:S(2)}, u32[]{:S(2)}) collective-permute-start(bf16[256,1024]{1,0:T(8,128)(2,1)S(1)} %bitcast.88), channel_id=1, source_target_pairs={{0,4},{1,5},{2,6},{3,7},{4,0},{5,1},{6,2},{7,3},{8,12},{9,13},{10,... | collective-permute-start | bytes 1572872 | tf_op jit(solution)/shard_map/ppermute | solution.py:41
  69.6 23.2 %collective-permute-start.13 = (bf16[256,1152]{1,0:T(8,128)(2,1)S(1)}, bf16[256,1152]{1,0:T(8,128)(2,1)S(1)}, u32[]{:S(2)}, u32[]{:S(2)}) collective-permute-start(bf16[256,1152]{1,0:T(8,128)(2,1)S(1)} %bitcast.84), channel_id=1, source_target_pairs={{0,4},{1,5},{2,6},{3,7},{4,0},{5,1},{6,2},{7,3},{8,12},{9,13},{10,... | collective-permute-start | bytes 1769480 | tf_op jit(solution)/shard_map/ppermute | solution.py:41
  105.8 15.8 %collective-permute-start.26 = (bf16[256,1024]{1,0:T(8,128)(2,1)S(1)}, bf16[256,1024]{1,0:T(8,128)(2,1)S(1)}, u32[]{:S(2)}, u32[]{:S(2)}) collective-permute-start(bf16[256,1024]{1,0:T(8,128)(2,1)S(1)} %get-tuple-element.52), channel_id=1, source_target_pairs={{0,4},{1,5},{2,6},{3,7},{4,0},{5,1},{6,2},{7,3},{8,12},{9,13},{10,... | collective-permute-start | bytes 1572872 | tf_op jit(solution)/shard_map/ppermute | solution.py:41
  111.2 12.1 %collective-permute-start.22 = (bf16[256,1024]{1,0:T(8,128)(2,1)S(1)}, bf16[256,1024]{1,0:T(8,128)(2,1)S(1)}, u32[]{:S(2)}, u32[]{:S(2)}) collective-permute-start(bf16[256,1024]{1,0:T(8,128)(2,1)S(1)} %get-tuple-element.50), channel_id=1, source_target_pairs={{0,4},{1,5},{2,6},{3,7},{4,0},{5,1},{6,2},{7,3},{8,12},{9,13},{10,... | collective-permute-start | bytes 1572872 | tf_op jit(solution)/shard_map/ppermute | solution.py:41
  116.2 8.1 %collective-permute-start.34 = (bf16[256,1024]{1,0:T(8,128)(2,1)S(1)}, bf16[256,1024]{1,0:T(8,128)(2,1)S(1)}, u32[]{:S(2)}, u32[]{:S(2)}) collective-permute-start(bf16[256,1024]{1,0:T(8,128)(2,1)S(1)} %get-tuple-element.56), channel_id=1, source_target_pairs={{0,4},{1,5},{2,6},{3,7},{4,0},{5,1},{6,2},{7,3},{8,12},{9,13},{10,... | collective-permute-start | bytes 1572872 | tf_op jit(solution)/shard_map/ppermute | solution.py:41
  121.6 4.4 %collective-permute-start.30 = (bf16[256,1024]{1,0:T(8,128)(2,1)S(1)}, bf16[256,1024]{1,0:T(8,128)(2,1)S(1)}, u32[]{:S(2)}, u32[]{:S(2)}) collective-permute-start(bf16[256,1024]{1,0:T(8,128)(2,1)S(1)} %get-tuple-element.54), channel_id=1, source_target_pairs={{0,4},{1,5},{2,6},{3,7},{4,0},{5,1},{6,2},{7,3},{8,12},{9,13},{10,... | collective-permute-start | bytes 1572872 | tf_op jit(solution)/shard_map/ppermute | solution.py:41
  121.9 9.2 %collective-permute-start.27 = (bf16[128,1024]{1,0:T(8,128)(2,1)S(1)}, bf16[128,1024]{1,0:T(8,128)(2,1)S(1)}, u32[]{:S(2)}, u32[]{:S(2)}) collective-permute-start(bf16[128,1024]{1,0:T(8,128)(2,1)S(1)} %slice.296), channel_id=1, source_target_pairs={{0,8},{1,9},{2,10},{3,11},{4,12},{5,13},{6,14},{7,15},{8,0},{9,1},... | collective-permute-start | bytes 786440 | tf_op jit(solution)/shard_map/ppermute | solution.py:41
  123.6 13.1 %collective-permute-start.23 = (bf16[128,1024]{1,0:T(8,128)(2,1)S(1)}, bf16[128,1024]{1,0:T(8,128)(2,1)S(1)}, u32[]{:S(2)}, u32[]{:S(2)}) collective-permute-start(bf16[128,1024]{1,0:T(8,128)(2,1)S(1)} %slice.297), channel_id=1, source_target_pairs={{0,8},{1,9},{2,10},{3,11},{4,12},{5,13},{6,14},{7,15},{8,0},{9,1},... | collective-permute-start | bytes 786440 | tf_op jit(solution)/shard_map/ppermute | solution.py:41
  124.5 17.9 %collective-permute-start.35 = (bf16[128,1024]{1,0:T(8,128)(2,1)S(1)}, bf16[128,1024]{1,0:T(8,128)(2,1)S(1)}, u32[]{:S(2)}, u32[]{:S(2)}) collective-permute-start(bf16[128,1024]{1,0:T(8,128)(2,1)S(1)} %slice.294), channel_id=1, source_target_pairs={{0,8},{1,9},{2,10},{3,11},{4,12},{5,13},{6,14},{7,15},{8,0},{9,1},... | collective-permute-start | bytes 786440 | tf_op jit(solution)/shard_map/ppermute | solution.py:41
  126.2 21.3 %collective-permute-start.31 = (bf16[128,1024]{1,0:T(8,128)(2,1)S(1)}, bf16[128,1024]{1,0:T(8,128)(2,1)S(1)}, u32[]{:S(2)}, u32[]{:S(2)}) collective-permute-start(bf16[128,1024]{1,0:T(8,128)(2,1)S(1)} %slice.295), channel_id=1, source_target_pairs={{0,8},{1,9},{2,10},{3,11},{4,12},{5,13},{6,14},{7,15},{8,0},{9,1},... | collective-permute-start | bytes 786440 | tf_op jit(solution)/shard_map/ppermute | solution.py:41
  131.2 11.2 %copy-start.4 = (f32[128,1024]{1,0:T(8,128)}, f32[128,1024]{1,0:T(8,128)S(1)}, u32[]{:S(2)}) copy-start(f32[128,1024]{1,0:T(8,128)S(1)} %slice_add_fusion.2) | copy-start | bytes 1572868
  136.8 5.7 %copy-start.5 = (f32[128,1024]{1,0:T(8,128)}, f32[128,1024]{1,0:T(8,128)S(1)}, u32[]{:S(2)}) copy-start(f32[128,1024]{1,0:T(8,128)S(1)} %slice_add_fusion.3) | copy-start | bytes 1572868
  142.5 7.3 %slice-start = ((f32[128,1024]{1,0:T(8,128)}), f32[64,1024]{1,0:T(8,128)S(1)}, s32[]{:S(2)}) async-start(f32[128,1024]{1,0:T(8,128)} %copy-done.4), calls=%async_computation | async-start | bytes 524288 | tf_op jit(solution)/shard_map/slice | solution.py:64
  142.5 13.7 %slice-start.1 = ((f32[128,1024]{1,0:T(8,128)}), f32[64,1024]{1,0:T(8,128)S(1)}, s32[]{:S(2)}) async-start(f32[128,1024]{1,0:T(8,128)} %copy-done.5), calls=%async_computation.1 | async-start | bytes 524288 | tf_op jit(solution)/shard_map/slice | solution.py:64
  142.5 7.3 %collective-permute-start.28 = (bf16[2,32,1024]{2,1,0:T(8,128)(2,1)S(1)}, bf16[2,32,1024]{2,1,0:T(8,128)(2,1)S(1)}, u32[]{:S(2)}, u32[]{:S(2)}) collective-permute-start(bf16[2,32,1024]{2,1,0:T(8,128)(2,1)S(1)} %bitcast.110), channel_id=1, source_target_pairs={{0,1},{1,0},{2,3},{3,2},{4,5},{5,4},{6,7},{7,6},{8,9},{9,8},{10,11... | collective-permute-start | bytes 393224 | tf_op jit(solution)/shard_map/ppermute | solution.py:41
  147.6 8.5 %collective-permute-start.24 = (bf16[2,32,1024]{2,1,0:T(8,128)(2,1)S(1)}, bf16[2,32,1024]{2,1,0:T(8,128)(2,1)S(1)}, u32[]{:S(2)}, u32[]{:S(2)}) collective-permute-start(bf16[2,32,1024]{2,1,0:T(8,128)(2,1)S(1)} %bitcast.108), channel_id=1, source_target_pairs={{0,1},{1,0},{2,3},{3,2},{4,5},{5,4},{6,7},{7,6},{8,9},{9,8},{10,11... | collective-permute-start | bytes 393224 | tf_op jit(solution)/shard_map/ppermute | solution.py:41
  147.7 11.3 %collective-permute-start.36 = (bf16[2,32,1024]{2,1,0:T(8,128)(2,1)S(1)}, bf16[2,32,1024]{2,1,0:T(8,128)(2,1)S(1)}, u32[]{:S(2)}, u32[]{:S(2)}) collective-permute-start(bf16[2,32,1024]{2,1,0:T(8,128)(2,1)S(1)} %bitcast.107), channel_id=1, source_target_pairs={{0,1},{1,0},{2,3},{3,2},{4,5},{5,4},{6,7},{7,6},{8,9},{9,8},{10,11... | collective-permute-start | bytes 393224 | tf_op jit(solution)/shard_map/ppermute | solution.py:41
  149.7 10.8 %collective-permute-start.32 = (bf16[2,32,1024]{2,1,0:T(8,128)(2,1)S(1)}, bf16[2,32,1024]{2,1,0:T(8,128)(2,1)S(1)}, u32[]{:S(2)}, u32[]{:S(2)}) collective-permute-start(bf16[2,32,1024]{2,1,0:T(8,128)(2,1)S(1)} %bitcast.109), channel_id=1, source_target_pairs={{0,1},{1,0},{2,3},{3,2},{4,5},{5,4},{6,7},{7,6},{8,9},{9,8},{10,11... | collective-permute-start | bytes 393224 | tf_op jit(solution)/shard_map/ppermute | solution.py:41
  149.8 15.5 %copy-start.3 = (bf16[32,2048]{1,0:T(8,128)(2,1)S(1)}, bf16[32,2048]{1,0:T(8,128)(2,1)}, u32[]{:S(2)}) copy-start(bf16[32,2048]{1,0:T(8,128)(2,1)} %copy-done.2) | copy-start | bytes 393220
  149.8 12.3 %collective-permute-start.29 = (bf16[1,32,1024]{2,1,0:T(8,128)(2,1)S(1)}, bf16[1,32,1024]{2,1,0:T(8,128)(2,1)S(1)}, u32[]{:S(2)}, u32[]{:S(2)}) collective-permute-start(bf16[1,32,1024]{2,1,0:T(8,128)(2,1)S(1)} %slice.306), channel_id=1, source_target_pairs={{0,2},{1,3},{2,0},{3,1},{4,6},{5,7},{6,4},{7,5},{8,10},{9,11},{10,... | collective-permute-start | bytes 196616 | tf_op jit(solution)/shard_map/ppermute | solution.py:41
  156.2 9.1 %collective-permute-start.25 = (bf16[1,32,1024]{2,1,0:T(8,128)(2,1)S(1)}, bf16[1,32,1024]{2,1,0:T(8,128)(2,1)S(1)}, u32[]{:S(2)}, u32[]{:S(2)}) collective-permute-start(bf16[1,32,1024]{2,1,0:T(8,128)(2,1)S(1)} %slice.307), channel_id=1, source_target_pairs={{0,2},{1,3},{2,0},{3,1},{4,6},{5,7},{6,4},{7,5},{8,10},{9,11},{10,... | collective-permute-start | bytes 196616 | tf_op jit(solution)/shard_map/ppermute | solution.py:41
  159.0 8.3 %collective-permute-start.37 = (bf16[1,32,1024]{2,1,0:T(8,128)(2,1)S(1)}, bf16[1,32,1024]{2,1,0:T(8,128)(2,1)S(1)}, u32[]{:S(2)}, u32[]{:S(2)}) collective-permute-start(bf16[1,32,1024]{2,1,0:T(8,128)(2,1)S(1)} %slice.304), channel_id=1, source_target_pairs={{0,2},{1,3},{2,0},{3,1},{4,6},{5,7},{6,4},{7,5},{8,10},{9,11},{10,... | collective-permute-start | bytes 196616 | tf_op jit(solution)/shard_map/ppermute | solution.py:41
  160.6 7.4 %collective-permute-start.33 = (bf16[1,32,1024]{2,1,0:T(8,128)(2,1)S(1)}, bf16[1,32,1024]{2,1,0:T(8,128)(2,1)S(1)}, u32[]{:S(2)}, u32[]{:S(2)}) collective-permute-start(bf16[1,32,1024]{2,1,0:T(8,128)(2,1)S(1)} %slice.305), channel_id=1, source_target_pairs={{0,2},{1,3},{2,0},{3,1},{4,6},{5,7},{6,4},{7,5},{8,10},{9,11},{10,... | collective-permute-start | bytes 196616 | tf_op jit(solution)/shard_map/ppermute | solution.py:41

commit v4 on v3

--- a/solution.py
+++ b/solution.py
@@ -11,10 +11,11 @@
 F32 = jnp.float32
 AXES = ("head", "req")
 LANES = 128
-MIX_CHUNKS = 2
+MIX_PARTS = ((0, 1), (1, 4))
 AG_CHUNKS = 4
 RS_CHUNKS = 4
 BATCH = 16
+Z_GROUPS = ((0,), (1,), (2, 3))
 
 
 def in_hbm(*arrays):
@@ -249,19 +250,18 @@
     ]
 
 
-def front(early, x, state, factor, grown, skip_gain, out_proj, slot_of, goes_to, near_rows, part, parts):
+def front(early, x, state, factor, grown, skip_gain, out_proj, slot_of, goes_to, near_rows, begin, span):
     nodes, reqs, columns = x.shape
     heads = skip_gain.shape[0]
     rows = nodes * reqs
     states = state.shape[3]
-    span = out_proj.shape[1] // parts
     state = state.reshape(state.shape[0], columns, states)
     skip = skip_gain.reshape(1, heads)
     x, state, skip, out_proj = in_hbm(x, state, skip, out_proj)
     vmem = pl.BlockSpec(memory_space=pltpu.VMEM)
     hbm = pl.BlockSpec(memory_space=pltpu.HBM)
     return pl.pallas_call(
-        functools.partial(front_body, heads, part * span),
+        functools.partial(front_body, heads, begin),
         grid_spec=pltpu.PrefetchScalarGridSpec(
             num_scalar_prefetch=2,
             in_specs=[vmem, vmem, hbm, vmem, vmem, vmem, hbm],
@@ -295,12 +295,11 @@
     project_blocks(rows[...], weight, held, arrived, first, near, far)
 
 
-def project(rows, out_proj, near_rows, part, parts):
+def project(rows, out_proj, near_rows, begin, span):
     count, columns = rows.shape
-    span = out_proj.shape[1] // parts
     vmem = pl.BlockSpec(memory_space=pltpu.VMEM)
     return pl.pallas_call(
-        functools.partial(project_body, part * span),
+        functools.partial(project_body, begin),
         in_specs=[vmem, pl.BlockSpec(memory_space=pltpu.HBM)],
         out_specs=(vmem, vmem),
         out_shape=(
@@ -371,7 +370,7 @@
         gout, uout, spread, picked, gates_held, ups_held, arrived = rest
     held = gates_held.shape[0]
     tall = width // LANES
-    slots = picked.shape[0] // tall
+    slots = picked.shape[1] // tall
 
     def copies(e):
         cut = pl.ds(begin, width)
@@ -401,20 +400,21 @@
             preferred_element_type=F32,
         )
 
-    def visit(q, carry):
+    def pick(q, b):
         for c in range(0, slots, BATCH):
             at = [token_at[q, c + i] for i in range(BATCH)]
             got = [spread[pl.ds(pl.multiple_of(t * tall, tall), tall)] for t in at]
-            picked[c * tall : (c + BATCH) * tall] = jnp.concatenate(got, axis=0)
+            picked[b, c * tall : (c + BATCH) * tall] = jnp.concatenate(got, axis=0)
             if last:
                 got = [extra[pl.ds(t, 1)] for t in at]
                 for i in range(BATCH):
-                    scales[c + i : c + i + 1] = got[i]
+                    scales[b, c + i : c + i + 1] = got[i]
+
+    def multiply(q, b):
+        half = picked.at[b]
         rows = jnp.concatenate(
-            [picked[pl.ds(i, slots, stride=tall), :].astype(BF) for i in range(tall)], axis=1
+            [half[pl.ds(i, slots, stride=tall), :].astype(BF) for i in range(tall)], axis=1
         )
-        for copy in copies(q):
-            copy.wait()
         gated = jnp.dot(rows, gates_held[q], preferred_element_type=F32)
         lifted = jnp.dot(rows, ups_held[q], preferred_element_type=F32)
         if not first:
@@ -423,8 +423,8 @@
         if not last:
             gout[q] = gated
             uout[q] = lifted
-            return carry
-        scale = scales[:, 0:1] + scales[:, 1:2] + scales[:, 2:3]
+            return
+        scale = scales[b, :, 0:1] + scales[b, :, 1:2] + scales[b, :, 2:3]
         gated = gated * scale
         lifted = lifted * scale
         act_out[q] = (gated / (1.0 + jnp.exp(-gated)) * lifted).astype(BF)
@@ -432,10 +432,22 @@
         column = lax.broadcasted_iota(jnp.int32, spot.shape, 1)
         own_spot = jnp.sum(jnp.where(column == q, spot[...], 0.0), axis=1, keepdims=True)
         own_share = jnp.sum(jnp.where(column == q, share, 0.0), axis=1, keepdims=True)
-        comb_out[q] = jnp.where(lane == own_spot, own_share, 0.0).astype(BF)
+        at = pl.ds(pl.multiple_of(q * slots, LANES), slots)
+        comb_out[:, at] = jnp.where(lane == own_spot, own_share, 0.0).astype(BF)
+
+    count = picked.shape[0]
+
+    def visit(p, carry):
+        for b in range(count):
+            for copy in copies(p * count + b):
+                copy.wait()
+        for b in range(count):
+            pick(p * count + b, b)
+        for b in range(count):
+            multiply(p * count + b, b)
         return carry
 
-    lax.fori_loop(0, held, visit, 0)
+    lax.fori_loop(0, held // count, visit, 0)
 
 
 def expert_up(k, chunks, experts, token_at, xs, gate_proj, up_proj, sums, place, e0):
@@ -449,9 +461,10 @@
     hbm = pl.BlockSpec(memory_space=pltpu.HBM)
     in_specs = [pl.BlockSpec(memory_space=pltpu.SMEM)] + [vmem] * len(xs) + [hbm, hbm]
     args = [token_at, *xs, *in_hbm(gate_proj, up_proj)]
+    pair = 2 if held % 2 == 0 else 1
     scratch = [
         pltpu.VMEM((tokens * width // LANES, LANES), F32),
-        pltpu.VMEM((slots * width // LANES, LANES), F32),
+        pltpu.VMEM((pair, slots * width // LANES, LANES), F32),
         pltpu.VMEM((held, width, units), BF),
         pltpu.VMEM((held, width, units), BF),
         pltpu.SemaphoreType.DMA((2, held)),
@@ -467,10 +480,10 @@
         args += [place, e0]
         out_shape = (
             jax.ShapeDtypeStruct((held, slots, units), BF),
-            jax.ShapeDtypeStruct((held, tokens, slots), BF),
+            jax.ShapeDtypeStruct((tokens, held * slots), BF),
         )
         lanes = gate_lanes(experts)
-        scratch += [pltpu.VMEM((slots, lanes), F32), pltpu.VMEM((tokens, lanes), F32)]
+        scratch += [pltpu.VMEM((pair, slots, lanes), F32), pltpu.VMEM((tokens, lanes), F32)]
     else:
         out_shape = (jax.ShapeDtypeStruct((held, slots, units), F32),) * 2
     return pl.pallas_call(
@@ -506,18 +519,17 @@
             act[q], held_rows[q], preferred_element_type=F32
         ).astype(BF)
     kept = keep.shape[0]
-    comb_rows = jnp.concatenate([comb[q] for q in range(held)], axis=1)
     block = min(width, 256)
     for j in range(0, width, block):
         cut = slice(j, j + block)
-        total = jnp.dot(comb_rows, halves[:, cut], preferred_element_type=F32)
+        total = jnp.dot(comb[...], halves[:, cut], preferred_element_type=F32)
         keep[:, cut] = total[:kept]
         send[:, cut] = total[kept:].astype(BF)
 
 
 def expert_down(k, chunks, act, comb, down_proj, kept):
     held, slots, units = act.shape
-    tokens = comb.shape[1]
+    tokens = comb.shape[0]
     width = down_proj.shape[2] // chunks
     vmem = pl.BlockSpec(memory_space=pltpu.VMEM)
     return pl.pallas_call(
@@ -593,35 +605,49 @@
 
     rows_left = residual.reshape(tokens, width)
     mixes = []
-    part_span = width // MIX_CHUNKS
-    for m in range(MIX_CHUNKS):
-        cut = slice(m * part_span, (m + 1) * part_span)
+    span = width // AG_CHUNKS
+    for m, (low, high) in enumerate(MIX_PARTS):
+        begin, part_span = low * span, (high - low) * span
+        cut = slice(begin, begin + part_span)
         if m == 0:
             mixed, away, mixed_rows = front(
                 early, ssm_input, cache_state, factor, grown, skip_gain, out_proj,
-                slot_of, goes_to, near_rows, m, MIX_CHUNKS,
+                slot_of, goes_to, near_rows, begin, part_span,
             )
         else:
-            mixed, away = project(mixed_rows, out_proj, near_rows, m, MIX_CHUNKS)
+            mixed, away = project(mixed_rows, out_proj, near_rows, begin, part_span)
         if cores > 1:
             mixed = ring.scatter([away], mixed, "dc")
         mixed = mixed.reshape(ys, tokens, part_span)
         mixed = ring.scatter([mixed[s].astype(BF) for s in range(1, ys)], mixed[0], "dy")
         mixes.append((rows_left[:, cut].astype(F32) + mixed).astype(BF))
-    span = width // AG_CHUNKS
     after_mixer = jnp.concatenate(mixes, axis=1)
+    moved = {}
+    for members in Z_GROUPS:
+        parts = []
+        for k in members:
+            cut = slice(k * span, (k + 1) * span)
+            m = [low <= k < high for low, high in MIX_PARTS].index(True)
+            local = slice((k - MIX_PARTS[m][0]) * span, (k + 1 - MIX_PARTS[m][0]) * span)
+            parts.append((mixes[m][:, local].astype(F32) * norm_gain[cut]).astype(BF))
+            if k == AG_CHUNKS - 1:
+                parts.append(gates(after_mixer, norm_gain, router, named))
+            if k == 0:
+                parts.append(named)
+        payload = jnp.concatenate(parts, axis=1) if len(parts) > 1 else parts[0]
+        rows = ring.gather_z(payload)
+        done = 0
+        for k in members:
+            wide = span
+            if k == 0:
+                wide += named.shape[1]
+            if k == AG_CHUNKS - 1:
+                wide += gate_lanes(experts)
+            moved[k] = rows[..., done : done + wide]
+            done += wide
     sums = None
     for k in range(AG_CHUNKS):
-        cut = slice(k * span, (k + 1) * span)
-        m = k * MIX_CHUNKS // AG_CHUNKS
-        local = slice(k * span - m * part_span, (k + 1) * span - m * part_span)
-        payload = (mixes[m][:, local].astype(F32) * norm_gain[cut]).astype(BF)
-        if k == AG_CHUNKS - 1:
-            extra = gates(after_mixer, norm_gain, router, named)
-            payload = jnp.concatenate([payload, extra], axis=1)
-        if k == 0:
-            payload = jnp.concatenate([payload, named], axis=1)
-        rows = ring.gather_z(payload)
+        rows = moved[k]
         rows = ring.gather(rows, "dy")
         rows = rows.reshape(all_tokens // cores, -1)
         xs = [rows]

time: 169 us -> 161 us (0.953)
  starting transfers between devices: 36 us -> 31.5 us
  waiting for transfers between devices: 66.6 us -> 64.3 us
  Pallas kernels: 61.8 us -> 60.1 us
    ppermute x38 -> x36, starting transfers between devices: 36 us -> 31.5 us  [shift(): return lax.ppermute(x, AXES, self.pairs(**how))]
    ppermute x38 -> x36, waiting for transfers between devices: 66.6 us -> 64.3 us  [shift(): return lax.ppermute(x, AXES, self.pairs(**how))]
  transfers between devices with their start and end apart: 38 -> 36, of which waited for: 21 -> 20; matrix products, arithmetic and copies ran while one was open for 1% -> 1% of each run, Pallas kernels for 26% -> 26%
where the time goes in v4:
time: 161 us; the launch traced here: 160 us
  waiting for transfers between devices  64.3 us (40%)
  Pallas kernels  60.1 us (37%)
  starting transfers between devices  31.5 us (20%)
  other arithmetic  3.42 us (2%)
    ppermute x36, waiting for transfers between devices, shift(): return lax.ppermute(x, AXES, self.pairs(**how))  64.3 us
    ppermute x36, starting transfers between devices, shift(): return lax.ppermute(x, AXES, self.pairs(**how))  31.5 us
    pallas_call x4, Pallas kernels, expert_up(): pl.pallas_call(functools.partial(up_body, first, last, k * width, len(xs)...  28.6 us
    pallas_call x4, Pallas kernels, expert_down(): pl.pallas_call(functools.partial(down_body, k * width), in_specs=[vmem, v...  19.3 us
    pallas_call x1, Pallas kernels, front(): pl.pallas_call(functools.partial(front_body, heads, begin), grid_spec=plt...  4.98 us
    pallas_call x1, Pallas kernels, project(): pl.pallas_call(functools.partial(project_body, begin), in_specs=[vmem, pl...  3.24 us
  transfers between devices with their start and end apart: 36, of which 20 were waited for; matrix products, arithmetic and copies ran while one was open for 1% of the time, Pallas kernels for 26%

profile of v4, /device:TPU:0, one launch (start us, length us, event | category | flops | bytes accessed | tf_op | source)
XLA Modules:
  0.0 160.4 jit_solution(5608860574383898153)
XLA Ops:
  2.1 2.8 %collective-permute-start.1 = (bf16[2,32,256]{2,1,0:T(8,128)(2,1)S(1)}, bf16[2,32,256]{2,1,0:T(8,128)(2,1)S(1)}, u32[]{:S(2)}, u32[]{:S(2)}) collective-permute-start(bf16[2,32,256]{2,1,0:T(8,128)(2,1)S(1)} %get-tuple-element.80), channel_id=1, source_target_pairs={{0,8},{1,9},{2,10},{3,11},{4,12},{5,13},{6,14},{7,15},{8,0},{9,1},... | collective-permute-start | bytes 98312 | tf_op jit(solution)/shard_map/ppermute | solution.py:42
  4.9 2.4 %prepare.1 = (f32[16,128,128]{2,1,0:T(8,128)S(1)}, f32[128,16]{1,0:T(8,128)S(1)}, bf16[32,128]{1,0:T(8,128)(2,1)S(1)}) custom-call(s32[8,16]{1,0:T(8,128)} %parents.1, s32[4,8,10]{2,1,0:T(8,128)} %ids.1, f32[16,8,16]{2,1,0:T(8,128)} %step_raw.1, f32[1,16]{1,0:T(1,128)} %bitcast.117, f32[1,16]{1,0:T(1,128)} %bitcast.118), custom_call_target="tpu_custom_call" | custom-call | tf_op jit(solution)/shard_map/prepare/pallas_call | solution.py:124
  7.4 5.0 %front.1 = (f32[64,1024]{1,0:T(8,128)S(1)}, bf16[64,1024]{1,0:T(8,128)(2,1)S(1)}, bf16[128,1024]{1,0:T(8,128)(2,1)S(1)}) custom-call(s32[4]{0:T(128)S(1)} %get-tuple-element.87.slot_of, s32[4]{0:T(128)S(1)} %get-tuple-element.88.goes_to, bf16[4,32,256]{2,1,0:T(8,128)(2,1)S(1)} %bitcast.86, bf16[16,8,1024]{2,1,0:T(8,128)(2,1)} %x.1, ...), custom_call_target="tpu_custom_call" | custom-call | flops 268435456 | bytes 2097152 | tf_op jit(solution)/shard_map/front/pallas_call | solution.py:263
  12.5 1.3 collective-permute-done.2
  13.9 1.5 collective-permute-start.3
  15.4 3.2 %project.1 = (f32[64,3072]{1,0:T(8,128)S(1)}, bf16[64,3072]{1,0:T(8,128)(2,1)S(1)}) custom-call(bf16[128,1024]{1,0:T(8,128)(2,1)S(1)} %get-tuple-element.37.rows, bf16[1024,4096]{1,0:T(8,128)(2,1)} %weight.3), custom_call_target="tpu_custom_call" | custom-call | flops 805306368 | bytes 6291456 | tf_op jit(solution)/shard_map/project/pallas_call | solution.py:301
  18.8 2.7 %collective-permute-start.4 = (bf16[32,1152]{1,0:T(8,128)(2,1)S(1)}, bf16[32,1152]{1,0:T(8,128)(2,1)S(1)}, u32[]{:S(2)}, u32[]{:S(2)}) collective-permute-start(bf16[32,1152]{1,0:T(8,128)(2,1)S(1)} %get-tuple-element.78), channel_id=1, source_target_pairs={{0,2},{1,3},{2,0},{3,1},{4,6},{5,7},{6,4},{7,5},{8,10},{9,11},{10,... | collective-permute-start | bytes 221192 | tf_op jit(solution)/shard_map/ppermute | solution.py:42
  21.5 1.0 collective-permute-start.9
  22.5 3.4 %collective-permute-done.4 = bf16[32,1152]{1,0:T(8,128)(2,1)S(1)} collective-permute-done((bf16[32,1152]{1,0:T(8,128)(2,1)S(1)}, bf16[32,1152]{1,0:T(8,128)(2,1)S(1)}, u32[]{:S(2)}, u32[]{:S(2)}) %collective-permute-start.4) | collective-permute-done | bytes 73760 | tf_op jit(solution)/shard_map/ppermute | solution.py:42
  26.8 1.9 %collective-permute-done.9 = bf16[32,3072]{1,0:T(8,128)(2,1)S(1)} collective-permute-done((bf16[32,3072]{1,0:T(8,128)(2,1)S(1)}, bf16[32,3072]{1,0:T(8,128)(2,1)S(1)}, u32[]{:S(2)}, u32[]{:S(2)}) %collective-permute-start.9) | collective-permute-done | bytes 196640 | tf_op jit(solution)/shard_map/ppermute | solution.py:42
  28.7 1.6 collective-permute-start.16
  30.9 1.5 collective-permute-start.10
  33.1 4.5 %collective-permute-done.16 = bf16[32,1024]{1,0:T(8,128)(2,1)S(1)} collective-permute-done((bf16[32,1024]{1,0:T(8,128)(2,1)S(1)}, bf16[32,1024]{1,0:T(8,128)(2,1)S(1)}, u32[]{:S(2)}, u32[]{:S(2)}) %collective-permute-start.16) | collective-permute-done | bytes 65568 | tf_op jit(solution)/shard_map/ppermute | solution.py:42
  38.1 3.1 %collective-permute-done.10 = bf16[32,2176]{1,0:T(8,128)(2,1)S(1)} collective-permute-done((bf16[32,2176]{1,0:T(8,128)(2,1)S(1)}, bf16[32,2176]{1,0:T(8,128)(2,1)S(1)}, u32[]{:S(2)}, u32[]{:S(2)}) %collective-permute-start.10) | collective-permute-done | bytes 139296 | tf_op jit(solution)/shard_map/ppermute | solution.py:42
  41.5 1.2 collective-permute-done.17
  42.8 1.3 collective-permute-start.18
  44.1 5.6 %collective-permute-done.11 = bf16[2,32,2176]{2,1,0:T(8,128)(2,1)S(1)} collective-permute-done((bf16[2,32,2176]{2,1,0:T(8,128)(2,1)S(1)}, bf16[2,32,2176]{2,1,0:T(8,128)(2,1)S(1)}, u32[]{:S(2)}, u32[]{:S(2)}) %collective-permute-start.11) | collective-permute-done | bytes 278560 | tf_op jit(solution)/shard_map/ppermute | solution.py:42
  50.4 1.5 collective-permute-start.12
  52.1 6.9 %collective-permute-done.14 = bf16[2,2,32,1024]{3,2,1,0:T(8,128)(2,1)S(1)} collective-permute-done((bf16[2,2,32,1024]{3,2,1,0:T(8,128)(2,1)S(1)}, bf16[2,2,32,1024]{3,2,1,0:T(8,128)(2,1)S(1)}, u32[]{:S(2)}, u32[]{:S(2)}) %collective-permute-start.14) | collective-permute-done | bytes 262176 | tf_op jit(solution)/shard_map/ppermute | solution.py:42
  59.1 4.1 %collective-permute-done.12 = bf16[2,2,32,1152]{3,2,1,0:T(8,128)(2,1)S(1)} collective-permute-done((bf16[2,2,32,1152]{3,2,1,0:T(8,128)(2,1)S(1)}, bf16[2,2,32,1152]{3,2,1,0:T(8,128)(2,1)S(1)}, u32[]{:S(2)}, u32[]{:S(2)}) %collective-permute-start.12) | collective-permute-done | bytes 294944 | tf_op jit(solution)/shard_map/ppermute | solution.py:42
  63.4 1.1 places.1
  64.5 6.4 %shard_map.163 = (f32[8,128,384]{2,1,0:T(8,128)S(1)}, f32[8,128,384]{2,1,0:T(8,128)S(1)}) custom-call(s32[8,128]{1,0:T(8,128)S(1)} %get-tuple-element.36.token_at, bf16[256,1152]{1,0:T(8,128)(2,1)S(1)} %bitcast.78, bf16[256,1152]{1,0:T(8,128)(2,1)S(1)} %collective-permute-done.7.rest_1_, bf16[8,4096,384]{2,1,0:T(8,128)(2,1)} %rest_2_.7, ...), custom_call_target="tpu_custom_call" | custom-call | flops 1610612736 | bytes 12582912 | tf_op jit(solution)/shard_map/pallas_call | solution.py:489
  70.9 7.0 %shard_map.164 = (f32[8,128,384]{2,1,0:T(8,128)S(1)}, f32[8,128,384]{2,1,0:T(8,128)S(1)}) custom-call(s32[8,128]{1,0:T(8,128)S(1)} %get-tuple-element.36.token_at, bf16[256,1024]{1,0:T(8,128)(2,1)S(1)} %bitcast.82, bf16[256,1024]{1,0:T(8,128)(2,1)} %collective-permute-done.19.rest_1_, ...), custom_call_target="tpu_custom_call", output_to_operand_aliasing={{0}: (5, {}), {1}: (6, {})} | custom-call | flops 1610612736 | bytes 12582912 | tf_op jit(solution)/shard_map/pallas_call | solution.py:489
  77.9 6.8 %shard_map.165 = (f32[8,128,384]{2,1,0:T(8,128)S(1)}, f32[8,128,384]{2,1,0:T(8,128)S(1)}) custom-call(s32[8,128]{1,0:T(8,128)S(1)} %get-tuple-element.36.token_at, bf16[256,1024]{1,0:T(8,128)(2,1)S(1)} %bitcast.84, bf16[256,1024]{1,0:T(8,128)(2,1)} %collective-permute-done.15.rest_1_, ...), custom_call_target="tpu_custom_call", output_to_operand_aliasing={{0}: (5, {}), {1}: (6, {})} | custom-call | flops 1610612736 | bytes 12582912 | tf_op jit(solution)/shard_map/pallas_call | solution.py:489
  84.8 8.3 %shard_map.166 = (bf16[8,128,384]{2,1,0:T(8,128)(2,1)S(1)}, bf16[512,1024]{1,0:T(8,128)(2,1)S(1)}) custom-call(s32[8,128]{1,0:T(8,128)S(1)} %get-tuple-element.36.token_at, bf16[256,1152]{1,0:T(8,128)(2,1)S(1)} %bitcast.80, bf16[256,1152]{1,0:T(8,128)(2,1)S(1)} %collective-permute-done.13.rest_1_, bf16[8,4096,384]{2,1,0:T(8,128)(2,1)} %rest_2_.7, ...), custom_call_target="tpu_custom_call" | custom-call | flops 1610612736 | bytes 12582912 | tf_op jit(solution)/shard_map/pallas_call | solution.py:489
  93.1 4.8 %shard_map.167 = (f32[256,1024]{1,0:T(8,128)S(1)}, bf16[256,1024]{1,0:T(8,128)(2,1)S(1)}) custom-call(bf16[8,128,384]{2,1,0:T(8,128)(2,1)S(1)} %get-tuple-element.47.act, bf16[512,1024]{1,0:T(8,128)(2,1)S(1)} %get-tuple-element.48.comb, bf16[8,384,4096]{2,1,0:T(8,128)(2,1)} %wd.7), custom_call_target="tpu_custom_call" | custom-call | flops 1879048192 | bytes 6291456 | tf_op jit(solution)/shard_map/pallas_call | solution.py:535
  98.5 4.8 %shard_map.170 = (f32[256,1024]{1,0:T(8,128)S(1)}, bf16[256,1024]{1,0:T(8,128)(2,1)S(1)}) custom-call(bf16[8,128,384]{2,1,0:T(8,128)(2,1)S(1)} %get-tuple-element.47.act, bf16[512,1024]{1,0:T(8,128)(2,1)S(1)} %get-tuple-element.48.comb, bf16[8,384,4096]{2,1,0:T(8,128)(2,1)} %wd.7), custom_call_target="tpu_custom_call" | custom-call | flops 1879048192 | bytes 6291456 | tf_op jit(solution)/shard_map/pallas_call | solution.py:535
  103.4 4.8 %shard_map.169 = (f32[256,1024]{1,0:T(8,128)S(1)}, bf16[256,1024]{1,0:T(8,128)(2,1)S(1)}) custom-call(bf16[8,128,384]{2,1,0:T(8,128)(2,1)S(1)} %get-tuple-element.47.act, bf16[512,1024]{1,0:T(8,128)(2,1)S(1)} %get-tuple-element.48.comb, bf16[8,384,4096]{2,1,0:T(8,128)(2,1)} %wd.7), custom_call_target="tpu_custom_call" | custom-call | flops 1879048192 | bytes 6291456 | tf_op jit(solution)/shard_map/pallas_call | solution.py:535
  108.8 4.8 %shard_map.168 = (f32[256,1024]{1,0:T(8,128)S(1)}, bf16[256,1024]{1,0:T(8,128)(2,1)S(1)}) custom-call(bf16[8,128,384]{2,1,0:T(8,128)(2,1)S(1)} %get-tuple-element.47.act, bf16[512,1024]{1,0:T(8,128)(2,1)S(1)} %get-tuple-element.48.comb, bf16[8,384,4096]{2,1,0:T(8,128)(2,1)} %wd.7), custom_call_target="tpu_custom_call" | custom-call | flops 1879048192 | bytes 6291456 | tf_op jit(solution)/shard_map/pallas_call | solution.py:535
  114.8 1.5 collective-permute-start.33
  117.4 1.5 collective-permute-start.25
  119.0 4.2 %collective-permute-done.21 = bf16[128,1024]{1,0:T(8,128)(2,1)S(1)} collective-permute-done((bf16[128,1024]{1,0:T(8,128)(2,1)S(1)}, bf16[128,1024]{1,0:T(8,128)(2,1)S(1)}, u32[]{:S(2)}, u32[]{:S(2)}) %collective-permute-start.21) | collective-permute-done | bytes 262176 | tf_op jit(solution)/shard_map/ppermute | solution.py:42
  123.3 5.5 %collective-permute-done.33 = bf16[128,1024]{1,0:T(8,128)(2,1)S(1)} collective-permute-done((bf16[128,1024]{1,0:T(8,128)(2,1)S(1)}, bf16[128,1024]{1,0:T(8,128)(2,1)S(1)}, u32[]{:S(2)}, u32[]{:S(2)}) %collective-permute-start.33) | collective-permute-done | bytes 262176 | tf_op jit(solution)/shard_map/ppermute | solution.py:42
  128.9 5.5 %collective-permute-done.29 = bf16[128,1024]{1,0:T(8,128)(2,1)S(1)} collective-permute-done((bf16[128,1024]{1,0:T(8,128)(2,1)S(1)}, bf16[128,1024]{1,0:T(8,128)(2,1)S(1)}, u32[]{:S(2)}, u32[]{:S(2)}) %collective-permute-start.29) | collective-permute-done | bytes 262176 | tf_op jit(solution)/shard_map/ppermute | solution.py:42
  134.6 1.1 collective-permute-start.22
  135.7 3.8 %collective-permute-done.25 = bf16[128,1024]{1,0:T(8,128)(2,1)S(1)} collective-permute-done((bf16[128,1024]{1,0:T(8,128)(2,1)S(1)}, bf16[128,1024]{1,0:T(8,128)(2,1)S(1)}, u32[]{:S(2)}, u32[]{:S(2)}) %collective-permute-start.25) | collective-permute-done | bytes 262176 | tf_op jit(solution)/shard_map/ppermute | solution.py:42
  139.6 1.1 collective-permute-start.34
  140.8 1.0 collective-permute-start.30
  141.7 1.1 collective-permute-start.26
  142.9 2.2 %collective-permute-start.23 = (bf16[1,32,1024]{2,1,0:T(8,128)(2,1)S(1)}, bf16[1,32,1024]{2,1,0:T(8,128)(2,1)S(1)}, u32[]{:S(2)}, u32[]{:S(2)}) collective-permute-start(bf16[1,32,1024]{2,1,0:T(8,128)(2,1)S(1)} %slice.314), channel_id=1, source_target_pairs={{0,2},{1,3},{2,0},{3,1},{4,6},{5,7},{6,4},{7,5},{8,10},{9,11},{10,... | collective-permute-start | bytes 196616 | tf_op jit(solution)/shard_map/ppermute | solution.py:42
  145.0 1.7 %collective-permute-done.34 = bf16[2,32,1024]{2,1,0:T(8,128)(2,1)S(1)} collective-permute-done((bf16[2,32,1024]{2,1,0:T(8,128)(2,1)S(1)}, bf16[2,32,1024]{2,1,0:T(8,128)(2,1)S(1)}, u32[]{:S(2)}, u32[]{:S(2)}) %collective-permute-start.34) | collective-permute-done | bytes 131104 | tf_op jit(solution)/shard_map/ppermute | solution.py:42
  146.8 0.9 collective-permute-start.35
  147.7 3.7 %collective-permute-done.30 = bf16[2,32,1024]{2,1,0:T(8,128)(2,1)S(1)} collective-permute-done((bf16[2,32,1024]{2,1,0:T(8,128)(2,1)S(1)}, bf16[2,32,1024]{2,1,0:T(8,128)(2,1)S(1)}, u32[]{:S(2)}, u32[]{:S(2)}) %collective-permute-start.30) | collective-permute-done | bytes 131104 | tf_op jit(solution)/shard_map/ppermute | solution.py:42
  151.8 1.8 %collective-permute-done.26 = bf16[2,32,1024]{2,1,0:T(8,128)(2,1)S(1)} collective-permute-done((bf16[2,32,1024]{2,1,0:T(8,128)(2,1)S(1)}, bf16[2,32,1024]{2,1,0:T(8,128)(2,1)S(1)}, u32[]{:S(2)}, u32[]{:S(2)}) %collective-permute-start.26) | collective-permute-done | bytes 131104 | tf_op jit(solution)/shard_map/ppermute | solution.py:42
  153.6 0.9 collective-permute-start.27
  154.6 2.3 %collective-permute-done.35 = bf16[1,32,1024]{2,1,0:T(8,128)(2,1)S(1)} collective-permute-done((bf16[1,32,1024]{2,1,0:T(8,128)(2,1)S(1)}, bf16[1,32,1024]{2,1,0:T(8,128)(2,1)S(1)}, u32[]{:S(2)}, u32[]{:S(2)}) %collective-permute-start.35) | collective-permute-done | bytes 65568 | tf_op jit(solution)/shard_map/ppermute | solution.py:42
  156.9 1.1 collective-permute-done.31
  158.0 1.5 collective-permute-done.27
  (113 shorter events, 11.5 us)
Async XLA Ops:
  0.7 1.3 collective-permute-start
  2.1 5.3 %collective-permute-start.1 = (bf16[2,32,256]{2,1,0:T(8,128)(2,1)S(1)}, bf16[2,32,256]{2,1,0:T(8,128)(2,1)S(1)}, u32[]{:S(2)}, u32[]{:S(2)}) collective-permute-start(bf16[2,32,256]{2,1,0:T(8,128)(2,1)S(1)} %get-tuple-element.80), channel_id=1, source_target_pairs={{0,8},{1,9},{2,10},{3,11},{4,12},{5,13},{6,14},{7,15},{8,0},{9,1},... | collective-permute-start | bytes 98312 | tf_op jit(solution)/shard_map/ppermute | solution.py:42
  7.4 5.1 %copy-start.1 = (f32[4096]{0:T(1024)S(1)}, f32[4096]{0:T(1024)}, u32[]{:S(2)}) copy-start(f32[4096]{0:T(1024)} %param.28) | copy-start | bytes 49156
  12.4 1.4 collective-permute-start.2
  13.9 4.8 %collective-permute-start.3 = (bf16[32,1024]{1,0:T(8,128)(2,1)S(1)}, bf16[32,1024]{1,0:T(8,128)(2,1)S(1)}, u32[]{:S(2)}, u32[]{:S(2)}) collective-permute-start(bf16[32,1024]{1,0:T(8,128)(2,1)S(1)} %slice.315), channel_id=1, source_target_pairs={{0,8},{1,9},{2,10},{3,11},{4,12},{5,13},{6,14},{7,15},{8,0},{9,1},... | collective-permute-start | bytes 196616 | tf_op jit(solution)/shard_map/ppermute | solution.py:42
  15.4 3.3 %copy-start.6 = (bf16[4,8,4096]{2,1,0:T(8,128)(2,1)S(1)}, bf16[4,8,4096]{2,1,0:T(8,128)(2,1)}, u32[]{:S(2)}) copy-start(bf16[4,8,4096]{2,1,0:T(8,128)(2,1)} %param.27) | copy-start | bytes 786436
  18.6 2.8 %collective-permute-start.8 = (bf16[64,3072]{1,0:T(8,128)(2,1)S(1)}, bf16[64,3072]{1,0:T(8,128)(2,1)S(1)}, u32[]{:S(2)}, u32[]{:S(2)}) collective-permute-start(bf16[64,3072]{1,0:T(8,128)(2,1)S(1)} %get-tuple-element.39), channel_id=1, source_target_pairs={{0,4},{1,5},{2,6},{3,7},{4,0},{5,1},{6,2},{7,3},{8,12},{9,13},{10,... | collective-permute-start | bytes 1179656 | tf_op jit(solution)/shard_map/ppermute | solution.py:42
  18.8 7.2 %collective-permute-start.4 = (bf16[32,1152]{1,0:T(8,128)(2,1)S(1)}, bf16[32,1152]{1,0:T(8,128)(2,1)S(1)}, u32[]{:S(2)}, u32[]{:S(2)}) collective-permute-start(bf16[32,1152]{1,0:T(8,128)(2,1)S(1)} %get-tuple-element.78), channel_id=1, source_target_pairs={{0,2},{1,3},{2,0},{3,1},{4,6},{5,7},{6,4},{7,5},{8,10},{9,11},{10,... | collective-permute-start | bytes 221192 | tf_op jit(solution)/shard_map/ppermute | solution.py:42
  21.5 8.8 %copy-start = (bf16[4096,64]{0,1:T(8,128)(2,1)S(1)}, bf16[4096,64]{0,1:T(8,128)(2,1)}, u32[]{:S(2)}) copy-start(bf16[4096,64]{0,1:T(8,128)(2,1)} %param.29) | copy-start | bytes 1572868
  21.5 7.1 %collective-permute-start.9 = (bf16[32,3072]{1,0:T(8,128)(2,1)S(1)}, bf16[32,3072]{1,0:T(8,128)(2,1)S(1)}, u32[]{:S(2)}, u32[]{:S(2)}) collective-permute-start(bf16[32,3072]{1,0:T(8,128)(2,1)S(1)} %slice.306), channel_id=1, source_target_pairs={{0,8},{1,9},{2,10},{3,11},{4,12},{5,13},{6,14},{7,15},{8,0},{9,1},... | collective-permute-start | bytes 589832 | tf_op jit(solution)/shard_map/ppermute | solution.py:42
  26.0 6.4 %collective-permute-start.5 = (bf16[2,32,1152]{2,1,0:T(8,128)(2,1)S(1)}, bf16[2,32,1152]{2,1,0:T(8,128)(2,1)S(1)}, u32[]{:S(2)}, u32[]{:S(2)}) collective-permute-start(bf16[2,32,1152]{2,1,0:T(8,128)(2,1)S(1)} %get-tuple-element.72), channel_id=1, source_target_pairs={{0,1},{1,0},{2,3},{3,2},{4,5},{5,4},{6,7},{7,6},{8,9},{9,8},{10,11... | collective-permute-start | bytes 442376 | tf_op jit(solution)/shard_map/ppermute | solution.py:42
  28.7 9.0 %copy-start.2 = (bf16[32,3072]{1,0:T(8,128)(2,1)}, bf16[32,3072]{1,0:T(8,128)(2,1)S(1)}, u32[]{:S(2)}) copy-start(bf16[32,3072]{1,0:T(8,128)(2,1)S(1)} %fusion.1) | copy-start | bytes 589828
  28.7 8.9 %collective-permute-start.16 = (bf16[32,1024]{1,0:T(8,128)(2,1)S(1)}, bf16[32,1024]{1,0:T(8,128)(2,1)S(1)}, u32[]{:S(2)}, u32[]{:S(2)}) collective-permute-start(bf16[32,1024]{1,0:T(8,128)(2,1)S(1)} %get-tuple-element.68), channel_id=1, source_target_pairs={{0,2},{1,3},{2,0},{3,1},{4,6},{5,7},{6,4},{7,5},{8,10},{9,11},{10,... | collective-permute-start | bytes 196616 | tf_op jit(solution)/shard_map/ppermute | solution.py:42
  30.9 10.3 %collective-permute-start.10 = (bf16[32,2176]{1,0:T(8,128)(2,1)S(1)}, bf16[32,2176]{1,0:T(8,128)(2,1)S(1)}, u32[]{:S(2)}, u32[]{:S(2)}) collective-permute-start(bf16[32,2176]{1,0:T(8,128)(2,1)S(1)} %get-tuple-element.74), channel_id=1, source_target_pairs={{0,2},{1,3},{2,0},{3,1},{4,6},{5,7},{6,4},{7,5},{8,10},{9,11},{10,... | collective-permute-start | bytes 417800 | tf_op jit(solution)/shard_map/ppermute | solution.py:42
  32.5 8.9 %collective-permute-start.6 = (bf16[2,2,32,1152]{3,2,1,0:T(8,128)(2,1)S(1)}, bf16[2,2,32,1152]{3,2,1,0:T(8,128)(2,1)S(1)}, u32[]{:S(2)}, u32[]{:S(2)}) collective-permute-start(bf16[2,2,32,1152]{3,2,1,0:T(8,128)(2,1)S(1)} %get-tuple-element.60), channel_id=1, source_target_pairs={{0,8},{1,9},{2,10},{3,11},{4,12},{5,13},{6,14},{7,15},{8,0},{9,1},... | collective-permute-start | bytes 884744 | tf_op jit(solution)/shard_map/ppermute | solution.py:42
  37.7 5.0 %collective-permute-start.17 = (bf16[2,32,1024]{2,1,0:T(8,128)(2,1)S(1)}, bf16[2,32,1024]{2,1,0:T(8,128)(2,1)S(1)}, u32[]{:S(2)}, u32[]{:S(2)}) collective-permute-start(bf16[2,32,1024]{2,1,0:T(8,128)(2,1)S(1)} %get-tuple-element.76), channel_id=1, source_target_pairs={{0,1},{1,0},{2,3},{3,2},{4,5},{5,4},{6,7},{7,6},{8,9},{9,8},{10,11... | collective-permute-start | bytes 393224 | tf_op jit(solution)/shard_map/ppermute | solution.py:42
  41.3 8.4 %collective-permute-start.11 = (bf16[2,32,2176]{2,1,0:T(8,128)(2,1)S(1)}, bf16[2,32,2176]{2,1,0:T(8,128)(2,1)S(1)}, u32[]{:S(2)}, u32[]{:S(2)}) collective-permute-start(bf16[2,32,2176]{2,1,0:T(8,128)(2,1)S(1)} %get-tuple-element.61), channel_id=1, source_target_pairs={{0,1},{1,0},{2,3},{3,2},{4,5},{5,4},{6,7},{7,6},{8,9},{9,8},{10,11... | collective-permute-start | bytes 835592 | tf_op jit(solution)/shard_map/ppermute | solution.py:42
  41.4 22.0 %collective-permute-start.7 = (bf16[256,1152]{1,0:T(8,128)(2,1)S(1)}, bf16[256,1152]{1,0:T(8,128)(2,1)S(1)}, u32[]{:S(2)}, u32[]{:S(2)}) collective-permute-start(bf16[256,1152]{1,0:T(8,128)(2,1)S(1)} %bitcast.76), channel_id=1, source_target_pairs={{0,4},{1,5},{2,6},{3,7},{4,0},{5,1},{6,2},{7,3},{8,12},{9,13},{10,... | collective-permute-start | bytes 1769480 | tf_op jit(solution)/shard_map/ppermute | solution.py:42
  42.8 9.2 %collective-permute-start.18 = (bf16[2,2,32,1024]{3,2,1,0:T(8,128)(2,1)S(1)}, bf16[2,2,32,1024]{3,2,1,0:T(8,128)(2,1)S(1)}, u32[]{:S(2)}, u32[]{:S(2)}) collective-permute-start(bf16[2,2,32,1024]{3,2,1,0:T(8,128)(2,1)S(1)} %get-tuple-element.64), channel_id=1, source_target_pairs={{0,8},{1,9},{2,10},{3,11},{4,12},{5,13},{6,14},{7,15},{8,0},{9,1},... | collective-permute-start | bytes 786440 | tf_op jit(solution)/shard_map/ppermute | solution.py:42
  49.7 9.2 %collective-permute-start.14 = (bf16[2,2,32,1024]{3,2,1,0:T(8,128)(2,1)S(1)}, bf16[2,2,32,1024]{3,2,1,0:T(8,128)(2,1)S(1)}, u32[]{:S(2)}, u32[]{:S(2)}) collective-permute-start(bf16[2,2,32,1024]{3,2,1,0:T(8,128)(2,1)S(1)} %pad_maximum_fusion.6), channel_id=1, source_target_pairs={{0,8},{1,9},{2,10},{3,11},{4,12},{5,13},{6,14},{7,15},{8,0},{9,1},... | collective-permute-start | bytes 786440 | tf_op jit(solution)/shard_map/ppermute | solution.py:42
  50.4 12.9 %collective-permute-start.12 = (bf16[2,2,32,1152]{3,2,1,0:T(8,128)(2,1)S(1)}, bf16[2,2,32,1152]{3,2,1,0:T(8,128)(2,1)S(1)}, u32[]{:S(2)}, u32[]{:S(2)}) collective-permute-start(bf16[2,2,32,1152]{3,2,1,0:T(8,128)(2,1)S(1)} %fusion.2), channel_id=1, source_target_pairs={{0,8},{1,9},{2,10},{3,11},{4,12},{5,13},{6,14},{7,15},{8,0},{9,1},... | collective-permute-start | bytes 884744 | tf_op jit(solution)/shard_map/ppermute | solution.py:42
  52.0 18.9 %collective-permute-start.19 = (bf16[256,1024]{1,0:T(8,128)(2,1)S(1)}, bf16[256,1024]{1,0:T(8,128)(2,1)}, u32[]{:S(2)}, u32[]{:S(2)}) collective-permute-start(bf16[256,1024]{1,0:T(8,128)(2,1)S(1)} %bitcast.81), channel_id=1, source_target_pairs={{0,4},{1,5},{2,6},{3,7},{4,0},{5,1},{6,2},{7,3},{8,12},{9,13},{10,... | collective-permute-start | bytes 1572872 | tf_op jit(solution)/shard_map/ppermute | solution.py:42
  59.0 18.9 %collective-permute-start.15 = (bf16[256,1024]{1,0:T(8,128)(2,1)S(1)}, bf16[256,1024]{1,0:T(8,128)(2,1)}, u32[]{:S(2)}, u32[]{:S(2)}) collective-permute-start(bf16[256,1024]{1,0:T(8,128)(2,1)S(1)} %bitcast.83), channel_id=1, source_target_pairs={{0,4},{1,5},{2,6},{3,7},{4,0},{5,1},{6,2},{7,3},{8,12},{9,13},{10,... | collective-permute-start | bytes 1572872 | tf_op jit(solution)/shard_map/ppermute | solution.py:42
  63.3 21.5 %collective-permute-start.13 = (bf16[256,1152]{1,0:T(8,128)(2,1)S(1)}, bf16[256,1152]{1,0:T(8,128)(2,1)S(1)}, u32[]{:S(2)}, u32[]{:S(2)}) collective-permute-start(bf16[256,1152]{1,0:T(8,128)(2,1)S(1)} %bitcast.79), channel_id=1, source_target_pairs={{0,4},{1,5},{2,6},{3,7},{4,0},{5,1},{6,2},{7,3},{8,12},{9,13},{10,... | collective-permute-start | bytes 1769480 | tf_op jit(solution)/shard_map/ppermute | solution.py:42
  97.9 15.8 %collective-permute-start.20 = (bf16[256,1024]{1,0:T(8,128)(2,1)S(1)}, bf16[256,1024]{1,0:T(8,128)(2,1)S(1)}, u32[]{:S(2)}, u32[]{:S(2)}) collective-permute-start(bf16[256,1024]{1,0:T(8,128)(2,1)S(1)} %get-tuple-element.50), channel_id=1, source_target_pairs={{0,4},{1,5},{2,6},{3,7},{4,0},{5,1},{6,2},{7,3},{8,12},{9,13},{10,... | collective-permute-start | bytes 1572872 | tf_op jit(solution)/shard_map/ppermute | solution.py:42
  103.3 11.3 %collective-permute-start.32 = (bf16[256,1024]{1,0:T(8,128)(2,1)S(1)}, bf16[256,1024]{1,0:T(8,128)(2,1)S(1)}, u32[]{:S(2)}, u32[]{:S(2)}) collective-permute-start(bf16[256,1024]{1,0:T(8,128)(2,1)S(1)} %get-tuple-element.56), channel_id=1, source_target_pairs={{0,4},{1,5},{2,6},{3,7},{4,0},{5,1},{6,2},{7,3},{8,12},{9,13},{10,... | collective-permute-start | bytes 1572872 | tf_op jit(solution)/shard_map/ppermute | solution.py:42
  108.2 8.1 %collective-permute-start.28 = (bf16[256,1024]{1,0:T(8,128)(2,1)S(1)}, bf16[256,1024]{1,0:T(8,128)(2,1)S(1)}, u32[]{:S(2)}, u32[]{:S(2)}) collective-permute-start(bf16[256,1024]{1,0:T(8,128)(2,1)S(1)} %get-tuple-element.54), channel_id=1, source_target_pairs={{0,4},{1,5},{2,6},{3,7},{4,0},{5,1},{6,2},{7,3},{8,12},{9,13},{10,... | collective-permute-start | bytes 1572872 | tf_op jit(solution)/shard_map/ppermute | solution.py:42
  113.6 3.6 %collective-permute-start.24 = (bf16[256,1024]{1,0:T(8,128)(2,1)S(1)}, bf16[256,1024]{1,0:T(8,128)(2,1)S(1)}, u32[]{:S(2)}, u32[]{:S(2)}) collective-permute-start(bf16[256,1024]{1,0:T(8,128)(2,1)S(1)} %get-tuple-element.52), channel_id=1, source_target_pairs={{0,4},{1,5},{2,6},{3,7},{4,0},{5,1},{6,2},{7,3},{8,12},{9,13},{10,... | collective-permute-start | bytes 1572872 | tf_op jit(solution)/shard_map/ppermute | solution.py:42
  113.9 9.2 %collective-permute-start.21 = (bf16[128,1024]{1,0:T(8,128)(2,1)S(1)}, bf16[128,1024]{1,0:T(8,128)(2,1)S(1)}, u32[]{:S(2)}, u32[]{:S(2)}) collective-permute-start(bf16[128,1024]{1,0:T(8,128)(2,1)S(1)} %slice.305), channel_id=1, source_target_pairs={{0,8},{1,9},{2,10},{3,11},{4,12},{5,13},{6,14},{7,15},{8,0},{9,1},... | collective-permute-start | bytes 786440 | tf_op jit(solution)/shard_map/ppermute | solution.py:42
  114.8 14.0 %collective-permute-start.33 = (bf16[128,1024]{1,0:T(8,128)(2,1)S(1)}, bf16[128,1024]{1,0:T(8,128)(2,1)S(1)}, u32[]{:S(2)}, u32[]{:S(2)}) collective-permute-start(bf16[128,1024]{1,0:T(8,128)(2,1)S(1)} %slice.302), channel_id=1, source_target_pairs={{0,8},{1,9},{2,10},{3,11},{4,12},{5,13},{6,14},{7,15},{8,0},{9,1},... | collective-permute-start | bytes 786440 | tf_op jit(solution)/shard_map/ppermute | solution.py:42
  116.6 17.9 %collective-permute-start.29 = (bf16[128,1024]{1,0:T(8,128)(2,1)S(1)}, bf16[128,1024]{1,0:T(8,128)(2,1)S(1)}, u32[]{:S(2)}, u32[]{:S(2)}) collective-permute-start(bf16[128,1024]{1,0:T(8,128)(2,1)S(1)} %slice.303), channel_id=1, source_target_pairs={{0,8},{1,9},{2,10},{3,11},{4,12},{5,13},{6,14},{7,15},{8,0},{9,1},... | collective-permute-start | bytes 786440 | tf_op jit(solution)/shard_map/ppermute | solution.py:42
  117.4 22.1 %collective-permute-start.25 = (bf16[128,1024]{1,0:T(8,128)(2,1)S(1)}, bf16[128,1024]{1,0:T(8,128)(2,1)S(1)}, u32[]{:S(2)}, u32[]{:S(2)}) collective-permute-start(bf16[128,1024]{1,0:T(8,128)(2,1)S(1)} %slice.304), channel_id=1, source_target_pairs={{0,8},{1,9},{2,10},{3,11},{4,12},{5,13},{6,14},{7,15},{8,0},{9,1},... | collective-permute-start | bytes 786440 | tf_op jit(solution)/shard_map/ppermute | solution.py:42
  123.2 11.2 %copy-start.4 = (f32[128,1024]{1,0:T(8,128)}, f32[128,1024]{1,0:T(8,128)S(1)}, u32[]{:S(2)}) copy-start(f32[128,1024]{1,0:T(8,128)S(1)} %slice_add_fusion.3) | copy-start | bytes 1572868
  128.9 5.7 %copy-start.5 = (f32[128,1024]{1,0:T(8,128)}, f32[128,1024]{1,0:T(8,128)S(1)}, u32[]{:S(2)}) copy-start(f32[128,1024]{1,0:T(8,128)S(1)} %slice_add_fusion) | copy-start | bytes 1572868
  134.5 8.3 %slice-start = ((f32[128,1024]{1,0:T(8,128)}), f32[64,1024]{1,0:T(8,128)S(1)}, s32[]{:S(2)}) async-start(f32[128,1024]{1,0:T(8,128)} %copy-done.4), calls=%async_computation | async-start | bytes 524288 | tf_op jit(solution)/shard_map/slice | solution.py:65
  134.6 12.2 %slice-start.1 = ((f32[128,1024]{1,0:T(8,128)}), f32[64,1024]{1,0:T(8,128)S(1)}, s32[]{:S(2)}) async-start(f32[128,1024]{1,0:T(8,128)} %copy-done.5), calls=%async_computation.1 | async-start | bytes 524288 | tf_op jit(solution)/shard_map/slice | solution.py:65
  134.6 8.2 %collective-permute-start.22 = (bf16[2,32,1024]{2,1,0:T(8,128)(2,1)S(1)}, bf16[2,32,1024]{2,1,0:T(8,128)(2,1)S(1)}, u32[]{:S(2)}, u32[]{:S(2)}) collective-permute-start(bf16[2,32,1024]{2,1,0:T(8,128)(2,1)S(1)} %bitcast.109), channel_id=1, source_target_pairs={{0,1},{1,0},{2,3},{3,2},{4,5},{5,4},{6,7},{7,6},{8,9},{9,8},{10,11... | collective-permute-start | bytes 393224 | tf_op jit(solution)/shard_map/ppermute | solution.py:42
  139.6 7.1 %collective-permute-start.34 = (bf16[2,32,1024]{2,1,0:T(8,128)(2,1)S(1)}, bf16[2,32,1024]{2,1,0:T(8,128)(2,1)S(1)}, u32[]{:S(2)}, u32[]{:S(2)}) collective-permute-start(bf16[2,32,1024]{2,1,0:T(8,128)(2,1)S(1)} %bitcast.107), channel_id=1, source_target_pairs={{0,1},{1,0},{2,3},{3,2},{4,5},{5,4},{6,7},{7,6},{8,9},{9,8},{10,11... | collective-permute-start | bytes 393224 | tf_op jit(solution)/shard_map/ppermute | solution.py:42
  140.8 10.6 %collective-permute-start.30 = (bf16[2,32,1024]{2,1,0:T(8,128)(2,1)S(1)}, bf16[2,32,1024]{2,1,0:T(8,128)(2,1)S(1)}, u32[]{:S(2)}, u32[]{:S(2)}) collective-permute-start(bf16[2,32,1024]{2,1,0:T(8,128)(2,1)S(1)} %bitcast.106), channel_id=1, source_target_pairs={{0,1},{1,0},{2,3},{3,2},{4,5},{5,4},{6,7},{7,6},{8,9},{9,8},{10,11... | collective-permute-start | bytes 393224 | tf_op jit(solution)/shard_map/ppermute | solution.py:42
  141.7 11.9 %collective-permute-start.26 = (bf16[2,32,1024]{2,1,0:T(8,128)(2,1)S(1)}, bf16[2,32,1024]{2,1,0:T(8,128)(2,1)S(1)}, u32[]{:S(2)}, u32[]{:S(2)}) collective-permute-start(bf16[2,32,1024]{2,1,0:T(8,128)(2,1)S(1)} %bitcast.108), channel_id=1, source_target_pairs={{0,1},{1,0},{2,3},{3,2},{4,5},{5,4},{6,7},{7,6},{8,9},{9,8},{10,11... | collective-permute-start | bytes 393224 | tf_op jit(solution)/shard_map/ppermute | solution.py:42
  142.9 16.7 %copy-start.3 = (bf16[32,3072]{1,0:T(8,128)(2,1)S(1)}, bf16[32,3072]{1,0:T(8,128)(2,1)}, u32[]{:S(2)}) copy-start(bf16[32,3072]{1,0:T(8,128)(2,1)} %copy-done.2) | copy-start | bytes 589828
  142.9 11.7 %collective-permute-start.23 = (bf16[1,32,1024]{2,1,0:T(8,128)(2,1)S(1)}, bf16[1,32,1024]{2,1,0:T(8,128)(2,1)S(1)}, u32[]{:S(2)}, u32[]{:S(2)}) collective-permute-start(bf16[1,32,1024]{2,1,0:T(8,128)(2,1)S(1)} %slice.314), channel_id=1, source_target_pairs={{0,2},{1,3},{2,0},{3,1},{4,6},{5,7},{6,4},{7,5},{8,10},{9,11},{10,... | collective-permute-start | bytes 196616 | tf_op jit(solution)/shard_map/ppermute | solution.py:42
  146.8 10.0 %collective-permute-start.35 = (bf16[1,32,1024]{2,1,0:T(8,128)(2,1)S(1)}, bf16[1,32,1024]{2,1,0:T(8,128)(2,1)S(1)}, u32[]{:S(2)}, u32[]{:S(2)}) collective-permute-start(bf16[1,32,1024]{2,1,0:T(8,128)(2,1)S(1)} %slice.311), channel_id=1, source_target_pairs={{0,2},{1,3},{2,0},{3,1},{4,6},{5,7},{6,4},{7,5},{8,10},{9,11},{10,... | collective-permute-start | bytes 196616 | tf_op jit(solution)/shard_map/ppermute | solution.py:42
  151.4 6.6 %collective-permute-start.31 = (bf16[1,32,1024]{2,1,0:T(8,128)(2,1)S(1)}, bf16[1,32,1024]{2,1,0:T(8,128)(2,1)S(1)}, u32[]{:S(2)}, u32[]{:S(2)}) collective-permute-start(bf16[1,32,1024]{2,1,0:T(8,128)(2,1)S(1)} %slice.312), channel_id=1, source_target_pairs={{0,2},{1,3},{2,0},{3,1},{4,6},{5,7},{6,4},{7,5},{8,10},{9,11},{10,... | collective-permute-start | bytes 196616 | tf_op jit(solution)/shard_map/ppermute | solution.py:42
  153.6 5.9 %collective-permute-start.27 = (bf16[1,32,1024]{2,1,0:T(8,128)(2,1)S(1)}, bf16[1,32,1024]{2,1,0:T(8,128)(2,1)S(1)}, u32[]{:S(2)}, u32[]{:S(2)}) collective-permute-start(bf16[1,32,1024]{2,1,0:T(8,128)(2,1)S(1)} %slice.313), channel_id=1, source_target_pairs={{0,2},{1,3},{2,0},{3,1},{4,6},{5,7},{6,4},{7,5},{8,10},{9,11},{10,... | collective-permute-start | bytes 196616 | tf_op jit(solution)/shard_map/ppermute | solution.py:42

commit v5 on v4

--- a/solution.py
+++ b/solution.py
@@ -13,7 +13,7 @@
 LANES = 128
 MIX_PARTS = ((0, 1), (1, 4))
 AG_CHUNKS = 4
-RS_CHUNKS = 4
+RS_PARTS = (1, 1, 1, 1)
 BATCH = 16
 Z_GROUPS = ((0,), (1,), (2, 3))
 
@@ -429,11 +429,10 @@
         lifted = lifted * scale
         act_out[q] = (gated / (1.0 + jnp.exp(-gated)) * lifted).astype(BF)
         lane = lax.broadcasted_iota(jnp.int32, (done, slots), 1).astype(F32)
-        column = lax.broadcasted_iota(jnp.int32, spot.shape, 1)
-        own_spot = jnp.sum(jnp.where(column == q, spot[...], 0.0), axis=1, keepdims=True)
-        own_share = jnp.sum(jnp.where(column == q, share, 0.0), axis=1, keepdims=True)
-        at = pl.ds(pl.multiple_of(q * slots, LANES), slots)
-        comb_out[:, at] = jnp.where(lane == own_spot, own_share, 0.0).astype(BF)
+        here = lane == spot[:, q : q + 1]
+        comb_out[:, q * slots : (q + 1) * slots] = jnp.where(
+            here, share[:, q : q + 1], 0.0
+        ).astype(BF)
 
     count = picked.shape[0]
 
@@ -447,7 +446,11 @@
             multiply(p * count + b, b)
         return carry
 
-    lax.fori_loop(0, held // count, visit, 0)
+    if last:
+        for p in range(held // count):
+            visit(p, 0)
+    else:
+        lax.fori_loop(0, held // count, visit, 0)
 
 
 def expert_up(k, chunks, experts, token_at, xs, gate_proj, up_proj, sums, place, e0):
@@ -527,13 +530,12 @@
         send[:, cut] = total[kept:].astype(BF)
 
 
-def expert_down(k, chunks, act, comb, down_proj, kept):
+def expert_down(begin, width, act, comb, down_proj, kept):
     held, slots, units = act.shape
     tokens = comb.shape[0]
-    width = down_proj.shape[2] // chunks
     vmem = pl.BlockSpec(memory_space=pltpu.VMEM)
     return pl.pallas_call(
-        functools.partial(down_body, k * width),
+        functools.partial(down_body, begin),
         in_specs=[vmem, vmem, pl.BlockSpec(memory_space=pltpu.HBM)],
         out_specs=(vmem, vmem),
         out_shape=(
@@ -590,8 +592,13 @@
     early = jnp.concatenate(
         [write_vec.reshape(tokens, states), read_vec.reshape(tokens, states)], axis=1
     )
-    early = ring.gather(ring.gather(early, "dc"), "dy")
-    early = early.reshape(ys * cores, tokens, -1)
+    early = jnp.stack(
+        [
+            ring.shift(early, dy=sy, dc=sc) if sy + sc else early
+            for sy in range(ys)
+            for sc in range(cores)
+        ]
+    )
     absolute = jnp.arange(ys * cores, dtype=jnp.int32)
     slot_of = ((y_at - absolute // cores) % ys) * cores + (c_at - absolute % cores) % cores
     slots = jnp.arange(cores * ys, dtype=jnp.int32)
@@ -659,14 +666,16 @@
     act, comb = sums
 
     pieces = []
-    span = width // RS_CHUNKS
-    for k in range(RS_CHUNKS):
-        keep, send = expert_down(k, RS_CHUNKS, act, comb, down_proj, ys * reqs * tokens)
+    begin = 0
+    for part in RS_PARTS:
+        span = width * part // sum(RS_PARTS)
+        keep, send = expert_down(begin, span, act, comb, down_proj, ys * reqs * tokens)
         total = ring.scatter([send], keep, "dc") if cores > 1 else keep
         total = total.reshape(ys, reqs * tokens, span)
         total = ring.scatter([total[s].astype(BF) for s in range(1, ys)], total[0], "dy")
         total = ring.scatter_z(total.reshape(reqs, tokens, span))
-        cut = slice(k * span, (k + 1) * span)
+        cut = slice(begin, begin + span)
+        begin += span
         pieces.append((after_mixer[:, cut].astype(F32) + total).astype(BF))
     return jnp.concatenate(pieces, axis=1).reshape(local_nodes, requests, width)
 

time: 161 us -> 160 us (level)
    ppermute x36 -> x37, waiting for transfers between devices: 64.3 us -> 63.9 us  [shift(): return lax.ppermute(x, AXES, self.pairs(**how))]
    ppermute x36 -> x37, starting transfers between devices: 31.5 us -> 31.2 us  [shift(): return lax.ppermute(x, AXES, self.pairs(**how))]
  transfers between devices with their start and end apart: 36 -> 37, of which waited for: 20 -> 20; matrix products, arithmetic and copies ran while one was open for 1% -> 1% of each run, Pallas kernels for 26% -> 27%
where the time goes in v5:
time: 160 us
  waiting for transfers between devices  63.9 us (40%)
  Pallas kernels  60 us (38%)
  starting transfers between devices  31.2 us (20%)
  other arithmetic  3.42 us (2%)
    ppermute x37, waiting for transfers between devices, shift(): return lax.ppermute(x, AXES, self.pairs(**how))  63.9 us
    ppermute x37, starting transfers between devices, shift(): return lax.ppermute(x, AXES, self.pairs(**how))  31.2 us
    pallas_call x4, Pallas kernels, expert_up(): pl.pallas_call(functools.partial(up_body, first, last, k * width, len(xs)...  28.2 us
    pallas_call x4, Pallas kernels, expert_down(): pl.pallas_call(functools.partial(down_body, begin), in_specs=[vmem, vmem,...  19.5 us
    pallas_call x1, Pallas kernels, front(): pl.pallas_call(functools.partial(front_body, heads, begin), grid_spec=plt...  4.99 us
    pallas_call x1, Pallas kernels, project(): pl.pallas_call(functools.partial(project_body, begin), in_specs=[vmem, pl...  3.25 us
  transfers between devices with their start and end apart: 37, of which 20 were waited for; matrix products, arithmetic and copies ran while one was open for 1% of the time, Pallas kernels for 27%

profile of v5, /device:TPU:0, one launch (start us, length us, event | category | flops | bytes accessed | tf_op | source)
XLA Modules:
  0.0 159.5 jit_solution(1366558922174535602)
XLA Ops:
  1.2 2.6 %collective-permute-start.1 = (bf16[32,256]{1,0:T(8,128)(2,1)S(1)}, bf16[32,256]{1,0:T(8,128)(2,1)S(1)}, u32[]{:S(2)}, u32[]{:S(2)}) collective-permute-start(bf16[32,256]{1,0:T(8,128)(2,1)S(1)} %get-tuple-element.84), channel_id=1, source_target_pairs={{0,8},{1,9},{2,10},{3,11},{4,12},{5,13},{6,14},{7,15},{8,0},{9,1},... | collective-permute-start | bytes 49160 | tf_op jit(solution)/shard_map/ppermute | solution.py:42
  3.8 2.4 %prepare.1 = (f32[16,128,128]{2,1,0:T(8,128)S(1)}, f32[128,16]{1,0:T(8,128)S(1)}, bf16[32,128]{1,0:T(8,128)(2,1)S(1)}) custom-call(s32[8,16]{1,0:T(8,128)} %parents.1, s32[4,8,10]{2,1,0:T(8,128)} %ids.1, f32[16,8,16]{2,1,0:T(8,128)} %step_raw.1, f32[1,16]{1,0:T(1,128)} %bitcast.115, f32[1,16]{1,0:T(1,128)} %bitcast.116), custom_call_target="tpu_custom_call" | custom-call | tf_op jit(solution)/shard_map/prepare/pallas_call | solution.py:124
  7.0 5.0 %front.1 = (f32[64,1024]{1,0:T(8,128)S(1)}, bf16[64,1024]{1,0:T(8,128)(2,1)S(1)}, bf16[128,1024]{1,0:T(8,128)(2,1)S(1)}) custom-call(s32[4]{0:T(128)S(1)} %get-tuple-element.85.slot_of, s32[4]{0:T(128)S(1)} %get-tuple-element.86.goes_to, bf16[4,32,256]{2,1,0:T(8,128)(2,1)S(1)} %pad_maximum_fusion.13.early, bf16[16,8,1024]{2,1,0:T(8,128)(2,1)} %x.1, ...), custom_call_target="tpu_custom_call" | custom-call | flops 268435456 | bytes 2097152 | tf_op jit(solution)/shard_map/front/pallas_call | solution.py:263
  12.2 1.2 collective-permute-done.3
  13.4 1.2 collective-permute-start.4
  14.6 3.2 %project.1 = (f32[64,3072]{1,0:T(8,128)S(1)}, bf16[64,3072]{1,0:T(8,128)(2,1)S(1)}) custom-call(bf16[128,1024]{1,0:T(8,128)(2,1)S(1)} %get-tuple-element.37.rows, bf16[1024,4096]{1,0:T(8,128)(2,1)} %weight.3), custom_call_target="tpu_custom_call" | custom-call | flops 805306368 | bytes 6291456 | tf_op jit(solution)/shard_map/project/pallas_call | solution.py:301
  18.1 2.6 %collective-permute-start.5 = (bf16[32,1152]{1,0:T(8,128)(2,1)S(1)}, bf16[32,1152]{1,0:T(8,128)(2,1)S(1)}, u32[]{:S(2)}, u32[]{:S(2)}) collective-permute-start(bf16[32,1152]{1,0:T(8,128)(2,1)S(1)} %get-tuple-element.78), channel_id=1, source_target_pairs={{0,2},{1,3},{2,0},{3,1},{4,6},{5,7},{6,4},{7,5},{8,10},{9,11},{10,... | collective-permute-start | bytes 221192 | tf_op jit(solution)/shard_map/ppermute | solution.py:42
  20.8 1.0 collective-permute-start.10
  21.9 3.4 %collective-permute-done.5 = bf16[32,1152]{1,0:T(8,128)(2,1)S(1)} collective-permute-done((bf16[32,1152]{1,0:T(8,128)(2,1)S(1)}, bf16[32,1152]{1,0:T(8,128)(2,1)S(1)}, u32[]{:S(2)}, u32[]{:S(2)}) %collective-permute-start.5) | collective-permute-done | bytes 73760 | tf_op jit(solution)/shard_map/ppermute | solution.py:42
  26.0 1.9 %collective-permute-done.10 = bf16[32,3072]{1,0:T(8,128)(2,1)S(1)} collective-permute-done((bf16[32,3072]{1,0:T(8,128)(2,1)S(1)}, bf16[32,3072]{1,0:T(8,128)(2,1)S(1)}, u32[]{:S(2)}, u32[]{:S(2)}) %collective-permute-start.10) | collective-permute-done | bytes 196640 | tf_op jit(solution)/shard_map/ppermute | solution.py:42
  28.0 1.6 collective-permute-start.17
  30.2 1.5 collective-permute-start.11
  31.7 1.0 collective-permute-start.7
  32.7 4.3 %collective-permute-done.17 = bf16[32,1024]{1,0:T(8,128)(2,1)S(1)} collective-permute-done((bf16[32,1024]{1,0:T(8,128)(2,1)S(1)}, bf16[32,1024]{1,0:T(8,128)(2,1)S(1)}, u32[]{:S(2)}, u32[]{:S(2)}) %collective-permute-start.17) | collective-permute-done | bytes 65568 | tf_op jit(solution)/shard_map/ppermute | solution.py:42
  37.3 3.1 %collective-permute-done.11 = bf16[32,2176]{1,0:T(8,128)(2,1)S(1)} collective-permute-done((bf16[32,2176]{1,0:T(8,128)(2,1)S(1)}, bf16[32,2176]{1,0:T(8,128)(2,1)S(1)}, u32[]{:S(2)}, u32[]{:S(2)}) %collective-permute-start.11) | collective-permute-done | bytes 139296 | tf_op jit(solution)/shard_map/ppermute | solution.py:42
  40.8 1.3 collective-permute-done.18
  42.1 1.2 collective-permute-start.19
  43.3 5.6 %collective-permute-done.12 = bf16[2,32,2176]{2,1,0:T(8,128)(2,1)S(1)} collective-permute-done((bf16[2,32,2176]{2,1,0:T(8,128)(2,1)S(1)}, bf16[2,32,2176]{2,1,0:T(8,128)(2,1)S(1)}, u32[]{:S(2)}, u32[]{:S(2)}) %collective-permute-start.12) | collective-permute-done | bytes 278560 | tf_op jit(solution)/shard_map/ppermute | solution.py:42
  49.0 1.0 collective-permute-start.15
  50.0 1.2 collective-permute-start.13
  51.4 6.9 %collective-permute-done.15 = bf16[2,2,32,1024]{3,2,1,0:T(8,128)(2,1)S(1)} collective-permute-done((bf16[2,2,32,1024]{3,2,1,0:T(8,128)(2,1)S(1)}, bf16[2,2,32,1024]{3,2,1,0:T(8,128)(2,1)S(1)}, u32[]{:S(2)}, u32[]{:S(2)}) %collective-permute-start.15) | collective-permute-done | bytes 262176 | tf_op jit(solution)/shard_map/ppermute | solution.py:42
  58.4 4.1 %collective-permute-done.13 = bf16[2,2,32,1152]{3,2,1,0:T(8,128)(2,1)S(1)} collective-permute-done((bf16[2,2,32,1152]{3,2,1,0:T(8,128)(2,1)S(1)}, bf16[2,2,32,1152]{3,2,1,0:T(8,128)(2,1)S(1)}, u32[]{:S(2)}, u32[]{:S(2)}) %collective-permute-start.13) | collective-permute-done | bytes 294944 | tf_op jit(solution)/shard_map/ppermute | solution.py:42
  62.7 1.1 places.1
  63.7 6.4 %shard_map.163 = (f32[8,128,384]{2,1,0:T(8,128)S(1)}, f32[8,128,384]{2,1,0:T(8,128)S(1)}) custom-call(s32[8,128]{1,0:T(8,128)S(1)} %get-tuple-element.36.token_at, bf16[256,1152]{1,0:T(8,128)(2,1)S(1)} %bitcast.76, bf16[256,1152]{1,0:T(8,128)(2,1)S(1)} %collective-permute-done.8.rest_1_, bf16[8,4096,384]{2,1,0:T(8,128)(2,1)} %rest_2_.7, ...), custom_call_target="tpu_custom_call" | custom-call | flops 1610612736 | bytes 12582912 | tf_op jit(solution)/shard_map/pallas_call | solution.py:492
  70.2 7.0 %shard_map.164 = (f32[8,128,384]{2,1,0:T(8,128)S(1)}, f32[8,128,384]{2,1,0:T(8,128)S(1)}) custom-call(s32[8,128]{1,0:T(8,128)S(1)} %get-tuple-element.36.token_at, bf16[256,1024]{1,0:T(8,128)(2,1)S(1)} %bitcast.80, bf16[256,1024]{1,0:T(8,128)(2,1)} %collective-permute-done.20.rest_1_, ...), custom_call_target="tpu_custom_call", output_to_operand_aliasing={{0}: (5, {}), {1}: (6, {})} | custom-call | flops 1610612736 | bytes 12582912 | tf_op jit(solution)/shard_map/pallas_call | solution.py:492
  77.2 7.0 %shard_map.165 = (f32[8,128,384]{2,1,0:T(8,128)S(1)}, f32[8,128,384]{2,1,0:T(8,128)S(1)}) custom-call(s32[8,128]{1,0:T(8,128)S(1)} %get-tuple-element.36.token_at, bf16[256,1024]{1,0:T(8,128)(2,1)S(1)} %bitcast.82, bf16[256,1024]{1,0:T(8,128)(2,1)} %collective-permute-done.16.rest_1_, ...), custom_call_target="tpu_custom_call", output_to_operand_aliasing={{0}: (5, {}), {1}: (6, {})} | custom-call | flops 1610612736 | bytes 12582912 | tf_op jit(solution)/shard_map/pallas_call | solution.py:492
  84.2 7.8 %shard_map.166 = (bf16[8,128,384]{2,1,0:T(8,128)(2,1)S(1)}, bf16[512,1024]{1,0:T(8,128)(2,1)S(1)}) custom-call(s32[8,128]{1,0:T(8,128)S(1)} %get-tuple-element.36.token_at, bf16[256,1152]{1,0:T(8,128)(2,1)S(1)} %bitcast.78, bf16[256,1152]{1,0:T(8,128)(2,1)S(1)} %collective-permute-done.14.rest_1_, bf16[8,4096,384]{2,1,0:T(8,128)(2,1)} %rest_2_.7, ...), custom_call_target="tpu_custom_call" | custom-call | flops 1610612736 | bytes 12582912 | tf_op jit(solution)/shard_map/pallas_call | solution.py:492
  92.0 4.8 %shard_map.167 = (f32[256,1024]{1,0:T(8,128)S(1)}, bf16[256,1024]{1,0:T(8,128)(2,1)S(1)}) custom-call(bf16[8,128,384]{2,1,0:T(8,128)(2,1)S(1)} %get-tuple-element.47.act, bf16[512,1024]{1,0:T(8,128)(2,1)S(1)} %get-tuple-element.48.comb, bf16[8,384,4096]{2,1,0:T(8,128)(2,1)} %wd.7), custom_call_target="tpu_custom_call" | custom-call | flops 1879048192 | bytes 6291456 | tf_op jit(solution)/shard_map/pallas_call | solution.py:537
  97.4 4.8 %shard_map.170 = (f32[256,1024]{1,0:T(8,128)S(1)}, bf16[256,1024]{1,0:T(8,128)(2,1)S(1)}) custom-call(bf16[8,128,384]{2,1,0:T(8,128)(2,1)S(1)} %get-tuple-element.47.act, bf16[512,1024]{1,0:T(8,128)(2,1)S(1)} %get-tuple-element.48.comb, bf16[8,384,4096]{2,1,0:T(8,128)(2,1)} %wd.7), custom_call_target="tpu_custom_call" | custom-call | flops 1879048192 | bytes 6291456 | tf_op jit(solution)/shard_map/pallas_call | solution.py:537
  102.3 4.8 %shard_map.169 = (f32[256,1024]{1,0:T(8,128)S(1)}, bf16[256,1024]{1,0:T(8,128)(2,1)S(1)}) custom-call(bf16[8,128,384]{2,1,0:T(8,128)(2,1)S(1)} %get-tuple-element.47.act, bf16[512,1024]{1,0:T(8,128)(2,1)S(1)} %get-tuple-element.48.comb, bf16[8,384,4096]{2,1,0:T(8,128)(2,1)} %wd.7), custom_call_target="tpu_custom_call" | custom-call | flops 1879048192 | bytes 6291456 | tf_op jit(solution)/shard_map/pallas_call | solution.py:537
  107.7 5.0 %shard_map.168 = (f32[256,1024]{1,0:T(8,128)S(1)}, bf16[256,1024]{1,0:T(8,128)(2,1)S(1)}) custom-call(bf16[8,128,384]{2,1,0:T(8,128)(2,1)S(1)} %get-tuple-element.47.act, bf16[512,1024]{1,0:T(8,128)(2,1)S(1)} %get-tuple-element.48.comb, bf16[8,384,4096]{2,1,0:T(8,128)(2,1)} %wd.7), custom_call_target="tpu_custom_call" | custom-call | flops 1879048192 | bytes 6291456 | tf_op jit(solution)/shard_map/pallas_call | solution.py:537
  114.3 1.2 collective-permute-start.34
  116.9 1.2 collective-permute-start.26
  118.1 4.2 %collective-permute-done.22 = bf16[128,1024]{1,0:T(8,128)(2,1)S(1)} collective-permute-done((bf16[128,1024]{1,0:T(8,128)(2,1)S(1)}, bf16[128,1024]{1,0:T(8,128)(2,1)S(1)}, u32[]{:S(2)}, u32[]{:S(2)}) %collective-permute-start.22) | collective-permute-done | bytes 262176 | tf_op jit(solution)/shard_map/ppermute | solution.py:42
  122.4 5.5 %collective-permute-done.34 = bf16[128,1024]{1,0:T(8,128)(2,1)S(1)} collective-permute-done((bf16[128,1024]{1,0:T(8,128)(2,1)S(1)}, bf16[128,1024]{1,0:T(8,128)(2,1)S(1)}, u32[]{:S(2)}, u32[]{:S(2)}) %collective-permute-start.34) | collective-permute-done | bytes 262176 | tf_op jit(solution)/shard_map/ppermute | solution.py:42
  128.1 5.5 %collective-permute-done.30 = bf16[128,1024]{1,0:T(8,128)(2,1)S(1)} collective-permute-done((bf16[128,1024]{1,0:T(8,128)(2,1)S(1)}, bf16[128,1024]{1,0:T(8,128)(2,1)S(1)}, u32[]{:S(2)}, u32[]{:S(2)}) %collective-permute-start.30) | collective-permute-done | bytes 262176 | tf_op jit(solution)/shard_map/ppermute | solution.py:42
  133.7 1.1 collective-permute-start.23
  134.8 3.9 %collective-permute-done.26 = bf16[128,1024]{1,0:T(8,128)(2,1)S(1)} collective-permute-done((bf16[128,1024]{1,0:T(8,128)(2,1)S(1)}, bf16[128,1024]{1,0:T(8,128)(2,1)S(1)}, u32[]{:S(2)}, u32[]{:S(2)}) %collective-permute-start.26) | collective-permute-done | bytes 262176 | tf_op jit(solution)/shard_map/ppermute | solution.py:42
  138.8 1.1 collective-permute-start.35
  139.9 1.0 collective-permute-start.31
  140.9 1.0 collective-permute-start.27
  142.0 2.2 %collective-permute-start.24 = (bf16[1,32,1024]{2,1,0:T(8,128)(2,1)S(1)}, bf16[1,32,1024]{2,1,0:T(8,128)(2,1)S(1)}, u32[]{:S(2)}, u32[]{:S(2)}) collective-permute-start(bf16[1,32,1024]{2,1,0:T(8,128)(2,1)S(1)} %slice.314), channel_id=1, source_target_pairs={{0,2},{1,3},{2,0},{3,1},{4,6},{5,7},{6,4},{7,5},{8,10},{9,11},{10,... | collective-permute-start | bytes 196616 | tf_op jit(solution)/shard_map/ppermute | solution.py:42
  144.2 1.8 %collective-permute-done.35 = bf16[2,32,1024]{2,1,0:T(8,128)(2,1)S(1)} collective-permute-done((bf16[2,32,1024]{2,1,0:T(8,128)(2,1)S(1)}, bf16[2,32,1024]{2,1,0:T(8,128)(2,1)S(1)}, u32[]{:S(2)}, u32[]{:S(2)}) %collective-permute-start.35) | collective-permute-done | bytes 131104 | tf_op jit(solution)/shard_map/ppermute | solution.py:42
  146.9 3.7 %collective-permute-done.31 = bf16[2,32,1024]{2,1,0:T(8,128)(2,1)S(1)} collective-permute-done((bf16[2,32,1024]{2,1,0:T(8,128)(2,1)S(1)}, bf16[2,32,1024]{2,1,0:T(8,128)(2,1)S(1)}, u32[]{:S(2)}, u32[]{:S(2)}) %collective-permute-start.31) | collective-permute-done | bytes 131104 | tf_op jit(solution)/shard_map/ppermute | solution.py:42
  150.9 1.8 %collective-permute-done.27 = bf16[2,32,1024]{2,1,0:T(8,128)(2,1)S(1)} collective-permute-done((bf16[2,32,1024]{2,1,0:T(8,128)(2,1)S(1)}, bf16[2,32,1024]{2,1,0:T(8,128)(2,1)S(1)}, u32[]{:S(2)}, u32[]{:S(2)}) %collective-permute-start.27) | collective-permute-done | bytes 131104 | tf_op jit(solution)/shard_map/ppermute | solution.py:42
  153.7 2.3 %collective-permute-done.36 = bf16[1,32,1024]{2,1,0:T(8,128)(2,1)S(1)} collective-permute-done((bf16[1,32,1024]{2,1,0:T(8,128)(2,1)S(1)}, bf16[1,32,1024]{2,1,0:T(8,128)(2,1)S(1)}, u32[]{:S(2)}, u32[]{:S(2)}) %collective-permute-start.36) | collective-permute-done | bytes 65568 | tf_op jit(solution)/shard_map/ppermute | solution.py:42
  156.1 1.1 collective-permute-done.32
  157.2 1.5 collective-permute-done.28
  (114 shorter events, 12.6 us)
Async XLA Ops:
  0.7 5.6 %collective-permute-start = (bf16[32,256]{1,0:T(8,128)(2,1)S(1)}, bf16[32,256]{1,0:T(8,128)(2,1)S(1)}, u32[]{:S(2)}, u32[]{:S(2)}) collective-permute-start(bf16[32,256]{1,0:T(8,128)(2,1)S(1)} %get-tuple-element.84), channel_id=1, source_target_pairs={{0,4},{1,5},{2,6},{3,7},{4,0},{5,1},{6,2},{7,3},{8,12},{9,13},{10,... | collective-permute-start | bytes 49160 | tf_op jit(solution)/shard_map/ppermute | solution.py:42
  1.2 5.1 %collective-permute-start.1 = (bf16[32,256]{1,0:T(8,128)(2,1)S(1)}, bf16[32,256]{1,0:T(8,128)(2,1)S(1)}, u32[]{:S(2)}, u32[]{:S(2)}) collective-permute-start(bf16[32,256]{1,0:T(8,128)(2,1)S(1)} %get-tuple-element.84), channel_id=1, source_target_pairs={{0,8},{1,9},{2,10},{3,11},{4,12},{5,13},{6,14},{7,15},{8,0},{9,1},... | collective-permute-start | bytes 49160 | tf_op jit(solution)/shard_map/ppermute | solution.py:42
  3.8 3.2 %collective-permute-start.2 = (bf16[32,256]{1,0:T(8,128)(2,1)S(1)}, bf16[32,256]{1,0:T(8,128)(2,1)S(1)}, u32[]{:S(2)}, u32[]{:S(2)}) collective-permute-start(bf16[32,256]{1,0:T(8,128)(2,1)S(1)} %get-tuple-element.84), channel_id=1, source_target_pairs={{0,12},{1,13},{2,14},{3,15},{4,8},{5,9},{6,10},{7,11},{8,4},{9,5},... | collective-permute-start | bytes 49160 | tf_op jit(solution)/shard_map/ppermute | solution.py:42
  6.9 5.2 %copy-start.1 = (f32[4096]{0:T(1024)S(1)}, f32[4096]{0:T(1024)}, u32[]{:S(2)}) copy-start(f32[4096]{0:T(1024)} %param.28) | copy-start | bytes 49156
  12.0 1.4 collective-permute-start.3
  13.4 4.6 %collective-permute-start.4 = (bf16[32,1024]{1,0:T(8,128)(2,1)S(1)}, bf16[32,1024]{1,0:T(8,128)(2,1)S(1)}, u32[]{:S(2)}, u32[]{:S(2)}) collective-permute-start(bf16[32,1024]{1,0:T(8,128)(2,1)S(1)} %slice.315), channel_id=1, source_target_pairs={{0,8},{1,9},{2,10},{3,11},{4,12},{5,13},{6,14},{7,15},{8,0},{9,1},... | collective-permute-start | bytes 196616 | tf_op jit(solution)/shard_map/ppermute | solution.py:42
  14.6 3.4 %copy-start.6 = (bf16[4,8,4096]{2,1,0:T(8,128)(2,1)S(1)}, bf16[4,8,4096]{2,1,0:T(8,128)(2,1)}, u32[]{:S(2)}) copy-start(bf16[4,8,4096]{2,1,0:T(8,128)(2,1)} %param.27) | copy-start | bytes 786436
  17.9 2.8 %collective-permute-start.9 = (bf16[64,3072]{1,0:T(8,128)(2,1)S(1)}, bf16[64,3072]{1,0:T(8,128)(2,1)S(1)}, u32[]{:S(2)}, u32[]{:S(2)}) collective-permute-start(bf16[64,3072]{1,0:T(8,128)(2,1)S(1)} %get-tuple-element.39), channel_id=1, source_target_pairs={{0,4},{1,5},{2,6},{3,7},{4,0},{5,1},{6,2},{7,3},{8,12},{9,13},{10,... | collective-permute-start | bytes 1179656 | tf_op jit(solution)/shard_map/ppermute | solution.py:42
  18.1 7.2 %collective-permute-start.5 = (bf16[32,1152]{1,0:T(8,128)(2,1)S(1)}, bf16[32,1152]{1,0:T(8,128)(2,1)S(1)}, u32[]{:S(2)}, u32[]{:S(2)}) collective-permute-start(bf16[32,1152]{1,0:T(8,128)(2,1)S(1)} %get-tuple-element.78), channel_id=1, source_target_pairs={{0,2},{1,3},{2,0},{3,1},{4,6},{5,7},{6,4},{7,5},{8,10},{9,11},{10,... | collective-permute-start | bytes 221192 | tf_op jit(solution)/shard_map/ppermute | solution.py:42
  20.8 8.8 %copy-start = (bf16[4096,64]{0,1:T(8,128)(2,1)S(1)}, bf16[4096,64]{0,1:T(8,128)(2,1)}, u32[]{:S(2)}) copy-start(bf16[4096,64]{0,1:T(8,128)(2,1)} %param.29) | copy-start | bytes 1572868
  20.8 7.0 %collective-permute-start.10 = (bf16[32,3072]{1,0:T(8,128)(2,1)S(1)}, bf16[32,3072]{1,0:T(8,128)(2,1)S(1)}, u32[]{:S(2)}, u32[]{:S(2)}) collective-permute-start(bf16[32,3072]{1,0:T(8,128)(2,1)S(1)} %slice.306), channel_id=1, source_target_pairs={{0,8},{1,9},{2,10},{3,11},{4,12},{5,13},{6,14},{7,15},{8,0},{9,1},... | collective-permute-start | bytes 589832 | tf_op jit(solution)/shard_map/ppermute | solution.py:42
  25.3 6.4 %collective-permute-start.6 = (bf16[2,32,1152]{2,1,0:T(8,128)(2,1)S(1)}, bf16[2,32,1152]{2,1,0:T(8,128)(2,1)S(1)}, u32[]{:S(2)}, u32[]{:S(2)}) collective-permute-start(bf16[2,32,1152]{2,1,0:T(8,128)(2,1)S(1)} %get-tuple-element.72), channel_id=1, source_target_pairs={{0,1},{1,0},{2,3},{3,2},{4,5},{5,4},{6,7},{7,6},{8,9},{9,8},{10,11... | collective-permute-start | bytes 442376 | tf_op jit(solution)/shard_map/ppermute | solution.py:42
  27.9 9.1 %copy-start.2 = (bf16[32,3072]{1,0:T(8,128)(2,1)}, bf16[32,3072]{1,0:T(8,128)(2,1)S(1)}, u32[]{:S(2)}) copy-start(bf16[32,3072]{1,0:T(8,128)(2,1)S(1)} %fusion.1) | copy-start | bytes 589828
  28.0 9.0 %collective-permute-start.17 = (bf16[32,1024]{1,0:T(8,128)(2,1)S(1)}, bf16[32,1024]{1,0:T(8,128)(2,1)S(1)}, u32[]{:S(2)}, u32[]{:S(2)}) collective-permute-start(bf16[32,1024]{1,0:T(8,128)(2,1)S(1)} %get-tuple-element.68), channel_id=1, source_target_pairs={{0,2},{1,3},{2,0},{3,1},{4,6},{5,7},{6,4},{7,5},{8,10},{9,11},{10,... | collective-permute-start | bytes 196616 | tf_op jit(solution)/shard_map/ppermute | solution.py:42
  30.2 10.3 %collective-permute-start.11 = (bf16[32,2176]{1,0:T(8,128)(2,1)S(1)}, bf16[32,2176]{1,0:T(8,128)(2,1)S(1)}, u32[]{:S(2)}, u32[]{:S(2)}) collective-permute-start(bf16[32,2176]{1,0:T(8,128)(2,1)S(1)} %get-tuple-element.74), channel_id=1, source_target_pairs={{0,2},{1,3},{2,0},{3,1},{4,6},{5,7},{6,4},{7,5},{8,10},{9,11},{10,... | collective-permute-start | bytes 417800 | tf_op jit(solution)/shard_map/ppermute | solution.py:42
  31.7 8.9 %collective-permute-start.7 = (bf16[2,2,32,1152]{3,2,1,0:T(8,128)(2,1)S(1)}, bf16[2,2,32,1152]{3,2,1,0:T(8,128)(2,1)S(1)}, u32[]{:S(2)}, u32[]{:S(2)}) collective-permute-start(bf16[2,2,32,1152]{3,2,1,0:T(8,128)(2,1)S(1)} %get-tuple-element.60), channel_id=1, source_target_pairs={{0,8},{1,9},{2,10},{3,11},{4,12},{5,13},{6,14},{7,15},{8,0},{9,1},... | collective-permute-start | bytes 884744 | tf_op jit(solution)/shard_map/ppermute | solution.py:42
  37.1 5.0 %collective-permute-start.18 = (bf16[2,32,1024]{2,1,0:T(8,128)(2,1)S(1)}, bf16[2,32,1024]{2,1,0:T(8,128)(2,1)S(1)}, u32[]{:S(2)}, u32[]{:S(2)}) collective-permute-start(bf16[2,32,1024]{2,1,0:T(8,128)(2,1)S(1)} %get-tuple-element.76), channel_id=1, source_target_pairs={{0,1},{1,0},{2,3},{3,2},{4,5},{5,4},{6,7},{7,6},{8,9},{9,8},{10,11... | collective-permute-start | bytes 393224 | tf_op jit(solution)/shard_map/ppermute | solution.py:42
  40.5 8.4 %collective-permute-start.12 = (bf16[2,32,2176]{2,1,0:T(8,128)(2,1)S(1)}, bf16[2,32,2176]{2,1,0:T(8,128)(2,1)S(1)}, u32[]{:S(2)}, u32[]{:S(2)}) collective-permute-start(bf16[2,32,2176]{2,1,0:T(8,128)(2,1)S(1)} %get-tuple-element.61), channel_id=1, source_target_pairs={{0,1},{1,0},{2,3},{3,2},{4,5},{5,4},{6,7},{7,6},{8,9},{9,8},{10,11... | collective-permute-start | bytes 835592 | tf_op jit(solution)/shard_map/ppermute | solution.py:42
  40.7 22.0 %collective-permute-start.8 = (bf16[256,1152]{1,0:T(8,128)(2,1)S(1)}, bf16[256,1152]{1,0:T(8,128)(2,1)S(1)}, u32[]{:S(2)}, u32[]{:S(2)}) collective-permute-start(bf16[256,1152]{1,0:T(8,128)(2,1)S(1)} %bitcast.74), channel_id=1, source_target_pairs={{0,4},{1,5},{2,6},{3,7},{4,0},{5,1},{6,2},{7,3},{8,12},{9,13},{10,... | collective-permute-start | bytes 1769480 | tf_op jit(solution)/shard_map/ppermute | solution.py:42
  42.1 9.1 %collective-permute-start.19 = (bf16[2,2,32,1024]{3,2,1,0:T(8,128)(2,1)S(1)}, bf16[2,2,32,1024]{3,2,1,0:T(8,128)(2,1)S(1)}, u32[]{:S(2)}, u32[]{:S(2)}) collective-permute-start(bf16[2,2,32,1024]{3,2,1,0:T(8,128)(2,1)S(1)} %get-tuple-element.64), channel_id=1, source_target_pairs={{0,8},{1,9},{2,10},{3,11},{4,12},{5,13},{6,14},{7,15},{8,0},{9,1},... | collective-permute-start | bytes 786440 | tf_op jit(solution)/shard_map/ppermute | solution.py:42
  49.0 9.2 %collective-permute-start.15 = (bf16[2,2,32,1024]{3,2,1,0:T(8,128)(2,1)S(1)}, bf16[2,2,32,1024]{3,2,1,0:T(8,128)(2,1)S(1)}, u32[]{:S(2)}, u32[]{:S(2)}) collective-permute-start(bf16[2,2,32,1024]{3,2,1,0:T(8,128)(2,1)S(1)} %pad_maximum_fusion.6), channel_id=1, source_target_pairs={{0,8},{1,9},{2,10},{3,11},{4,12},{5,13},{6,14},{7,15},{8,0},{9,1},... | collective-permute-start | bytes 786440 | tf_op jit(solution)/shard_map/ppermute | solution.py:42
  50.0 12.5 %collective-permute-start.13 = (bf16[2,2,32,1152]{3,2,1,0:T(8,128)(2,1)S(1)}, bf16[2,2,32,1152]{3,2,1,0:T(8,128)(2,1)S(1)}, u32[]{:S(2)}, u32[]{:S(2)}) collective-permute-start(bf16[2,2,32,1152]{3,2,1,0:T(8,128)(2,1)S(1)} %fusion.2), channel_id=1, source_target_pairs={{0,8},{1,9},{2,10},{3,11},{4,12},{5,13},{6,14},{7,15},{8,0},{9,1},... | collective-permute-start | bytes 884744 | tf_op jit(solution)/shard_map/ppermute | solution.py:42
  51.3 18.9 %collective-permute-start.20 = (bf16[256,1024]{1,0:T(8,128)(2,1)S(1)}, bf16[256,1024]{1,0:T(8,128)(2,1)}, u32[]{:S(2)}, u32[]{:S(2)}) collective-permute-start(bf16[256,1024]{1,0:T(8,128)(2,1)S(1)} %bitcast.79), channel_id=1, source_target_pairs={{0,4},{1,5},{2,6},{3,7},{4,0},{5,1},{6,2},{7,3},{8,12},{9,13},{10,... | collective-permute-start | bytes 1572872 | tf_op jit(solution)/shard_map/ppermute | solution.py:42
  58.3 18.9 %collective-permute-start.16 = (bf16[256,1024]{1,0:T(8,128)(2,1)S(1)}, bf16[256,1024]{1,0:T(8,128)(2,1)}, u32[]{:S(2)}, u32[]{:S(2)}) collective-permute-start(bf16[256,1024]{1,0:T(8,128)(2,1)S(1)} %bitcast.81), channel_id=1, source_target_pairs={{0,4},{1,5},{2,6},{3,7},{4,0},{5,1},{6,2},{7,3},{8,12},{9,13},{10,... | collective-permute-start | bytes 1572872 | tf_op jit(solution)/shard_map/ppermute | solution.py:42
  62.6 21.6 %collective-permute-start.14 = (bf16[256,1152]{1,0:T(8,128)(2,1)S(1)}, bf16[256,1152]{1,0:T(8,128)(2,1)S(1)}, u32[]{:S(2)}, u32[]{:S(2)}) collective-permute-start(bf16[256,1152]{1,0:T(8,128)(2,1)S(1)} %bitcast.77), channel_id=1, source_target_pairs={{0,4},{1,5},{2,6},{3,7},{4,0},{5,1},{6,2},{7,3},{8,12},{9,13},{10,... | collective-permute-start | bytes 1769480 | tf_op jit(solution)/shard_map/ppermute | solution.py:42
  96.9 16.0 %collective-permute-start.21 = (bf16[256,1024]{1,0:T(8,128)(2,1)S(1)}, bf16[256,1024]{1,0:T(8,128)(2,1)S(1)}, u32[]{:S(2)}, u32[]{:S(2)}) collective-permute-start(bf16[256,1024]{1,0:T(8,128)(2,1)S(1)} %get-tuple-element.50), channel_id=1, source_target_pairs={{0,4},{1,5},{2,6},{3,7},{4,0},{5,1},{6,2},{7,3},{8,12},{9,13},{10,... | collective-permute-start | bytes 1572872 | tf_op jit(solution)/shard_map/ppermute | solution.py:42
  102.3 11.8 %collective-permute-start.33 = (bf16[256,1024]{1,0:T(8,128)(2,1)S(1)}, bf16[256,1024]{1,0:T(8,128)(2,1)S(1)}, u32[]{:S(2)}, u32[]{:S(2)}) collective-permute-start(bf16[256,1024]{1,0:T(8,128)(2,1)S(1)} %get-tuple-element.56), channel_id=1, source_target_pairs={{0,4},{1,5},{2,6},{3,7},{4,0},{5,1},{6,2},{7,3},{8,12},{9,13},{10,... | collective-permute-start | bytes 1572872 | tf_op jit(solution)/shard_map/ppermute | solution.py:42
  107.2 8.3 %collective-permute-start.29 = (bf16[256,1024]{1,0:T(8,128)(2,1)S(1)}, bf16[256,1024]{1,0:T(8,128)(2,1)S(1)}, u32[]{:S(2)}, u32[]{:S(2)}) collective-permute-start(bf16[256,1024]{1,0:T(8,128)(2,1)S(1)} %get-tuple-element.54), channel_id=1, source_target_pairs={{0,4},{1,5},{2,6},{3,7},{4,0},{5,1},{6,2},{7,3},{8,12},{9,13},{10,... | collective-permute-start | bytes 1572872 | tf_op jit(solution)/shard_map/ppermute | solution.py:42
  112.8 3.9 %collective-permute-start.25 = (bf16[256,1024]{1,0:T(8,128)(2,1)S(1)}, bf16[256,1024]{1,0:T(8,128)(2,1)S(1)}, u32[]{:S(2)}, u32[]{:S(2)}) collective-permute-start(bf16[256,1024]{1,0:T(8,128)(2,1)S(1)} %get-tuple-element.52), channel_id=1, source_target_pairs={{0,4},{1,5},{2,6},{3,7},{4,0},{5,1},{6,2},{7,3},{8,12},{9,13},{10,... | collective-permute-start | bytes 1572872 | tf_op jit(solution)/shard_map/ppermute | solution.py:42
  113.1 9.2 %collective-permute-start.22 = (bf16[128,1024]{1,0:T(8,128)(2,1)S(1)}, bf16[128,1024]{1,0:T(8,128)(2,1)S(1)}, u32[]{:S(2)}, u32[]{:S(2)}) collective-permute-start(bf16[128,1024]{1,0:T(8,128)(2,1)S(1)} %slice.305), channel_id=1, source_target_pairs={{0,8},{1,9},{2,10},{3,11},{4,12},{5,13},{6,14},{7,15},{8,0},{9,1},... | collective-permute-start | bytes 786440 | tf_op jit(solution)/shard_map/ppermute | solution.py:42
  114.3 13.7 %collective-permute-start.34 = (bf16[128,1024]{1,0:T(8,128)(2,1)S(1)}, bf16[128,1024]{1,0:T(8,128)(2,1)S(1)}, u32[]{:S(2)}, u32[]{:S(2)}) collective-permute-start(bf16[128,1024]{1,0:T(8,128)(2,1)S(1)} %slice.302), channel_id=1, source_target_pairs={{0,8},{1,9},{2,10},{3,11},{4,12},{5,13},{6,14},{7,15},{8,0},{9,1},... | collective-permute-start | bytes 786440 | tf_op jit(solution)/shard_map/ppermute | solution.py:42
  115.7 17.9 %collective-permute-start.30 = (bf16[128,1024]{1,0:T(8,128)(2,1)S(1)}, bf16[128,1024]{1,0:T(8,128)(2,1)S(1)}, u32[]{:S(2)}, u32[]{:S(2)}) collective-permute-start(bf16[128,1024]{1,0:T(8,128)(2,1)S(1)} %slice.303), channel_id=1, source_target_pairs={{0,8},{1,9},{2,10},{3,11},{4,12},{5,13},{6,14},{7,15},{8,0},{9,1},... | collective-permute-start | bytes 786440 | tf_op jit(solution)/shard_map/ppermute | solution.py:42
  116.9 21.8 %collective-permute-start.26 = (bf16[128,1024]{1,0:T(8,128)(2,1)S(1)}, bf16[128,1024]{1,0:T(8,128)(2,1)S(1)}, u32[]{:S(2)}, u32[]{:S(2)}) collective-permute-start(bf16[128,1024]{1,0:T(8,128)(2,1)S(1)} %slice.304), channel_id=1, source_target_pairs={{0,8},{1,9},{2,10},{3,11},{4,12},{5,13},{6,14},{7,15},{8,0},{9,1},... | collective-permute-start | bytes 786440 | tf_op jit(solution)/shard_map/ppermute | solution.py:42
  122.4 11.2 %copy-start.4 = (f32[128,1024]{1,0:T(8,128)}, f32[128,1024]{1,0:T(8,128)S(1)}, u32[]{:S(2)}) copy-start(f32[128,1024]{1,0:T(8,128)S(1)} %slice_add_fusion.3) | copy-start | bytes 1572868
  128.0 5.7 %copy-start.5 = (f32[128,1024]{1,0:T(8,128)}, f32[128,1024]{1,0:T(8,128)S(1)}, u32[]{:S(2)}) copy-start(f32[128,1024]{1,0:T(8,128)S(1)} %slice_add_fusion) | copy-start | bytes 1572868
  133.7 8.2 %slice-start = ((f32[128,1024]{1,0:T(8,128)}), f32[64,1024]{1,0:T(8,128)S(1)}, s32[]{:S(2)}) async-start(f32[128,1024]{1,0:T(8,128)} %copy-done.4), calls=%async_computation | async-start | bytes 524288 | tf_op jit(solution)/shard_map/slice | solution.py:65
  133.7 12.2 %slice-start.1 = ((f32[128,1024]{1,0:T(8,128)}), f32[64,1024]{1,0:T(8,128)S(1)}, s32[]{:S(2)}) async-start(f32[128,1024]{1,0:T(8,128)} %copy-done.5), calls=%async_computation.1 | async-start | bytes 524288 | tf_op jit(solution)/shard_map/slice | solution.py:65
  133.7 8.2 %collective-permute-start.23 = (bf16[2,32,1024]{2,1,0:T(8,128)(2,1)S(1)}, bf16[2,32,1024]{2,1,0:T(8,128)(2,1)S(1)}, u32[]{:S(2)}, u32[]{:S(2)}) collective-permute-start(bf16[2,32,1024]{2,1,0:T(8,128)(2,1)S(1)} %bitcast.106), channel_id=1, source_target_pairs={{0,1},{1,0},{2,3},{3,2},{4,5},{5,4},{6,7},{7,6},{8,9},{9,8},{10,11... | collective-permute-start | bytes 393224 | tf_op jit(solution)/shard_map/ppermute | solution.py:42
  138.8 7.1 %collective-permute-start.35 = (bf16[2,32,1024]{2,1,0:T(8,128)(2,1)S(1)}, bf16[2,32,1024]{2,1,0:T(8,128)(2,1)S(1)}, u32[]{:S(2)}, u32[]{:S(2)}) collective-permute-start(bf16[2,32,1024]{2,1,0:T(8,128)(2,1)S(1)} %bitcast.104), channel_id=1, source_target_pairs={{0,1},{1,0},{2,3},{3,2},{4,5},{5,4},{6,7},{7,6},{8,9},{9,8},{10,11... | collective-permute-start | bytes 393224 | tf_op jit(solution)/shard_map/ppermute | solution.py:42
  139.9 10.6 %collective-permute-start.31 = (bf16[2,32,1024]{2,1,0:T(8,128)(2,1)S(1)}, bf16[2,32,1024]{2,1,0:T(8,128)(2,1)S(1)}, u32[]{:S(2)}, u32[]{:S(2)}) collective-permute-start(bf16[2,32,1024]{2,1,0:T(8,128)(2,1)S(1)} %bitcast.103), channel_id=1, source_target_pairs={{0,1},{1,0},{2,3},{3,2},{4,5},{5,4},{6,7},{7,6},{8,9},{9,8},{10,11... | collective-permute-start | bytes 393224 | tf_op jit(solution)/shard_map/ppermute | solution.py:42
  140.9 11.8 %collective-permute-start.27 = (bf16[2,32,1024]{2,1,0:T(8,128)(2,1)S(1)}, bf16[2,32,1024]{2,1,0:T(8,128)(2,1)S(1)}, u32[]{:S(2)}, u32[]{:S(2)}) collective-permute-start(bf16[2,32,1024]{2,1,0:T(8,128)(2,1)S(1)} %bitcast.105), channel_id=1, source_target_pairs={{0,1},{1,0},{2,3},{3,2},{4,5},{5,4},{6,7},{7,6},{8,9},{9,8},{10,11... | collective-permute-start | bytes 393224 | tf_op jit(solution)/shard_map/ppermute | solution.py:42
  142.0 16.8 %copy-start.3 = (bf16[32,3072]{1,0:T(8,128)(2,1)S(1)}, bf16[32,3072]{1,0:T(8,128)(2,1)}, u32[]{:S(2)}) copy-start(bf16[32,3072]{1,0:T(8,128)(2,1)} %copy-done.2) | copy-start | bytes 589828
  142.0 11.7 %collective-permute-start.24 = (bf16[1,32,1024]{2,1,0:T(8,128)(2,1)S(1)}, bf16[1,32,1024]{2,1,0:T(8,128)(2,1)S(1)}, u32[]{:S(2)}, u32[]{:S(2)}) collective-permute-start(bf16[1,32,1024]{2,1,0:T(8,128)(2,1)S(1)} %slice.314), channel_id=1, source_target_pairs={{0,2},{1,3},{2,0},{3,1},{4,6},{5,7},{6,4},{7,5},{8,10},{9,11},{10,... | collective-permute-start | bytes 196616 | tf_op jit(solution)/shard_map/ppermute | solution.py:42
  146.0 10.1 %collective-permute-start.36 = (bf16[1,32,1024]{2,1,0:T(8,128)(2,1)S(1)}, bf16[1,32,1024]{2,1,0:T(8,128)(2,1)S(1)}, u32[]{:S(2)}, u32[]{:S(2)}) collective-permute-start(bf16[1,32,1024]{2,1,0:T(8,128)(2,1)S(1)} %slice.311), channel_id=1, source_target_pairs={{0,2},{1,3},{2,0},{3,1},{4,6},{5,7},{6,4},{7,5},{8,10},{9,11},{10,... | collective-permute-start | bytes 196616 | tf_op jit(solution)/shard_map/ppermute | solution.py:42
  150.6 6.6 %collective-permute-start.32 = (bf16[1,32,1024]{2,1,0:T(8,128)(2,1)S(1)}, bf16[1,32,1024]{2,1,0:T(8,128)(2,1)S(1)}, u32[]{:S(2)}, u32[]{:S(2)}) collective-permute-start(bf16[1,32,1024]{2,1,0:T(8,128)(2,1)S(1)} %slice.312), channel_id=1, source_target_pairs={{0,2},{1,3},{2,0},{3,1},{4,6},{5,7},{6,4},{7,5},{8,10},{9,11},{10,... | collective-permute-start | bytes 196616 | tf_op jit(solution)/shard_map/ppermute | solution.py:42
  152.8 5.9 %collective-permute-start.28 = (bf16[1,32,1024]{2,1,0:T(8,128)(2,1)S(1)}, bf16[1,32,1024]{2,1,0:T(8,128)(2,1)S(1)}, u32[]{:S(2)}, u32[]{:S(2)}) collective-permute-start(bf16[1,32,1024]{2,1,0:T(8,128)(2,1)S(1)} %slice.313), channel_id=1, source_target_pairs={{0,2},{1,3},{2,0},{3,1},{4,6},{5,7},{6,4},{7,5},{8,10},{9,11},{10,... | collective-permute-start | bytes 196616 | tf_op jit(solution)/shard_map/ppermute | solution.py:42
